TPU v7x, 32 devices: a whole 2x2x4 slice. The times are simulated.
32 devices in a mesh: grp: 2 (over y), seq: 16 (over z, x, core).
Axes of the slice: x: 2, y: 2, z: 4, core: 2. Of those that a mesh axis runs over, the one named last changes fastest.
Arguments:
- queries: bfloat16 [4096, 128], P(('grp', 'seq')), parts along dimension 0, may hold values from -6 to 6
- keys: bfloat16 [4096, 128], P(('grp', 'seq')), parts along dimension 0, may hold values from -6 to 6
- values: bfloat16 [4096, 128], P(('grp', 'seq')), parts along dimension 0, may hold values from -6 to 6
- log_gate: float32 [4096], P(('grp', 'seq')), parts along dimension 0, may hold values from -1 to 0, as said below
- out_grad: bfloat16 [4096, 128], P(('grp', 'seq')), parts along dimension 0, may hold values from -6 to 6
- segment_order: int32 [64], P(('grp', 'seq')), parts along dimension 0, may hold values from 0 to 31, each once
Outputs:
- attn_out: bfloat16 [4096, 128], P(('grp', 'seq')), parts along dimension 0
- query_grad: float32 [4096, 128], P(('grp', 'seq')), parts along dimension 0
- key_grad: float32 [4096, 128], P(('grp', 'seq')), parts along dimension 0
- value_grad: float32 [4096, 128], P(('grp', 'seq')), parts along dimension 0
- gate_grad: float32 [4096], P(('grp', 'seq')), parts along dimension 0
There are 2 independent parts, one for each index of `grp`. A program takes and returns all parts, laid end to end along the dimension named above; each array names one. Nothing has to cross between parts.
Inputs may be any that keep to these rules, and one draw needn't show every extreme that they name: `log_gate`: every gate is below one. `segment_order`: each segment index appears once.
All inputs are finite; a program needn't handle non-finite values.
Results may differ from a plain program's by a relative error of at most 0.0095.
Values may be sent and summed in bfloat16 or wider, within the bound.
No kernel may reach another device: no remote copies, remote signals or barrier semaphores. Data moves between devices by JAX's collectives and lax.ppermute only.
A program may use at most 64 MiB of HBM per device.

v0:
```python
import jax
import jax.numpy as jnp
from jax import lax
from jax.sharding import PartitionSpec as P

masked_value = -1e30


def contract_last(left, right):
    return lax.dot_general(
        left, right, (((1,), (1,)), ((), ())), preferred_element_type=jnp.float32
    )


def contract_first(left, right):
    return lax.dot_general(
        left, right, (((0,), (0,)), ((), ())), preferred_element_type=jnp.float32
    )


def tile_scores(query_rows, query_gate, query_pos, key_rows, key_gate, key_pos, score_scale):
    scores = (
        contract_last(query_rows, key_rows) * score_scale + query_gate[:, None] - key_gate[None, :]
    )
    visible = key_pos[None, :] <= query_pos[:, None]
    return (scores, visible)


def tile_probs(scores, visible, row_total):
    return jnp.where(visible, jnp.exp(scores - row_total[:, None]), 0.0)


def local(queries, keys, values, log_gate, out_grad, segment_order):
    tokens_here, width = queries.shape
    devices = lax.axis_size("seq")
    segment_rows = tokens_here // 2
    total_len = tokens_here * devices
    score_scale = width ** (-0.5)
    offsets_in = lax.broadcasted_iota(jnp.int32, (1, segment_rows), 1)
    local_cum = jnp.cumsum(log_gate.reshape(2, segment_rows), axis=1)
    segment_total = local_cum[:, -1]
    segment_place = segment_order.astype(jnp.float32)
    own_pos = (segment_order[:, None] * segment_rows + offsets_in).reshape(-1)
    all_totals, all_place = (
        lax.all_gather(segment_total, "seq", axis=0, tiled=True),
        lax.all_gather(segment_place, "seq", axis=0, tiled=True),
    )
    earlier = (all_place[None, :] < segment_place[:, None]).astype(jnp.float32)
    own_offset = jnp.sum(earlier * all_totals[None, :], axis=1)
    own_gate = (local_cum + own_offset[:, None]).reshape(-1)
    all_gate = lax.all_gather(own_gate, "seq", axis=0, tiled=True)
    all_pos = (all_place.astype(jnp.int32)[:, None] * segment_rows + offsets_in).reshape(-1)
    key_all, value_all = (
        lax.all_gather(keys, "seq", axis=0, tiled=True),
        lax.all_gather(values, "seq", axis=0, tiled=True),
    )
    block = 2048
    count = total_len // block

    def key_tile(block_index):
        start = block_index * block
        return (
            lax.dynamic_slice_in_dim(key_all, start, block),
            lax.dynamic_slice_in_dim(value_all, start, block),
            lax.dynamic_slice_in_dim(all_gate, start, block),
            lax.dynamic_slice_in_dim(all_pos, start, block),
        )

    def stats_step(block_index, carry):
        run_max, run_sum = carry
        key_rows, value_rows, key_gate, key_pos = key_tile(block_index)
        scores, visible = tile_scores(
            queries, own_gate, own_pos, key_rows, key_gate, key_pos, score_scale
        )
        kept = jnp.where(visible, scores, masked_value)
        new_max = jnp.maximum(run_max, jnp.max(kept, axis=1))
        fresh = jnp.sum(jnp.where(visible, jnp.exp(kept - new_max[:, None]), 0.0), axis=1)
        return (new_max, run_sum * jnp.exp(run_max - new_max) + fresh)

    start_max = jnp.full((tokens_here,), masked_value, jnp.float32)
    run_max, run_sum = lax.fori_loop(
        0, count, stats_step, (start_max, jnp.zeros((tokens_here,), jnp.float32))
    )
    log_total = run_max + jnp.log(run_sum)

    def output_step(block_index, total):
        key_rows, value_rows, key_gate, key_pos = key_tile(block_index)
        scores, visible = tile_scores(
            queries, own_gate, own_pos, key_rows, key_gate, key_pos, score_scale
        )
        probs = tile_probs(scores, visible, log_total).astype(jnp.bfloat16)
        return total + jnp.dot(probs, value_rows, preferred_element_type=jnp.float32)

    out_full = lax.fori_loop(0, count, output_step, jnp.zeros((tokens_here, width), jnp.float32))
    attn_out = out_full.astype(jnp.bfloat16)
    row_delta = jnp.sum(out_grad.astype(jnp.float32) * out_full, axis=1)

    def row_terms(block_index):
        key_rows, value_rows, key_gate, key_pos = key_tile(block_index)
        scores, visible = tile_scores(
            queries, own_gate, own_pos, key_rows, key_gate, key_pos, score_scale
        )
        probs = tile_probs(scores, visible, log_total)
        dprob = contract_last(out_grad, value_rows)
        return (key_rows, probs, probs * (dprob - row_delta[:, None]))

    def query_step(block_index, total):
        key_rows, probs, dscore = row_terms(block_index)
        return total + jnp.dot(
            dscore.astype(jnp.bfloat16), key_rows, preferred_element_type=jnp.float32
        )

    query_acc = lax.fori_loop(0, count, query_step, jnp.zeros((tokens_here, width), jnp.float32))
    query_all, grad_all = (
        lax.all_gather(queries, "seq", axis=0, tiled=True),
        lax.all_gather(out_grad, "seq", axis=0, tiled=True),
    )
    total_all, delta_all = (
        lax.all_gather(log_total, "seq", axis=0, tiled=True),
        lax.all_gather(row_delta, "seq", axis=0, tiled=True),
    )

    def column_step(block_index, carry):
        key_acc, value_acc, column_acc = carry
        start = block_index * block
        query_rows = lax.dynamic_slice_in_dim(query_all, start, block)
        grad_rows = lax.dynamic_slice_in_dim(grad_all, start, block)
        scores, visible = tile_scores(
            query_rows,
            lax.dynamic_slice_in_dim(all_gate, start, block),
            lax.dynamic_slice_in_dim(all_pos, start, block),
            keys,
            own_gate,
            own_pos,
            score_scale,
        )
        probs = tile_probs(scores, visible, lax.dynamic_slice_in_dim(total_all, start, block))
        dprob = contract_last(grad_rows, values)
        dscore = probs * (dprob - lax.dynamic_slice_in_dim(delta_all, start, block)[:, None])
        dscore_low = dscore.astype(jnp.bfloat16)
        key_acc = key_acc + contract_first(dscore_low, query_rows) * score_scale
        value_acc = value_acc + contract_first(probs.astype(jnp.bfloat16), grad_rows)
        column_acc = column_acc - jnp.sum(dscore, axis=0)
        return (key_acc, value_acc, column_acc)

    zeros_own = jnp.zeros((tokens_here, width), jnp.float32)
    key_grad, value_grad, gate_point = lax.fori_loop(
        0, count, column_step, (zeros_own, zeros_own, jnp.zeros((tokens_here,), jnp.float32))
    )
    query_grad = query_acc * score_scale
    point_rows = gate_point.reshape(2, segment_rows)
    within = jnp.flip(jnp.cumsum(jnp.flip(point_rows, 1), axis=1), 1)
    all_point = lax.all_gather(within[:, 0], "seq", axis=0, tiled=True)
    later = (all_place[None, :] > segment_place[:, None]).astype(jnp.float32)
    gate_grad = (within + jnp.sum(later * all_point[None, :], axis=1)[:, None]).reshape(-1)
    return (attn_out, query_grad, key_grad, value_grad, gate_grad)


def solution(mesh):
    placed = (
        P(("grp", "seq"), None),
        P(("grp", "seq"), None),
        P(("grp", "seq"), None),
        P(("grp", "seq")),
        P(("grp", "seq"), None),
        P(("grp", "seq")),
    )
    return jax.shard_map(
        local,
        mesh=mesh,
        in_specs=placed,
        out_specs=(
            P(("grp", "seq"), None),
            P(("grp", "seq"), None),
            P(("grp", "seq"), None),
            P(("grp", "seq"), None),
            P(("grp", "seq")),
        ),
        check_vma=False,
    )
```

profile of v0, /device:TPU:0, one launch (start us, length us, event | category | flops | bytes accessed | tf_op | source)
XLA Modules:
  0.0 211.5 jit_solution(15644140626693972713)
XLA Ops:
  0.6 0.0 copy-start
  0.6 0.9 copy.17
  1.5 0.0 copy-start.4
  1.5 24.6 %all_gather.34 = bf16[2048,128]{1,0:T(8,128)(2,1)S(1)} all-gather(bf16[128,128]{1,0:T(8,128)(2,1)S(1)} %copy-done), channel_id=1, replica_groups=mesh['grp'=2,'seq'=16] {'seq'}, dimensions={0}, use_global_device_ids=true | all-gather | bytes 557056 | tf_op jit(solution)/shard_map/all_gather | solution.py:55
  26.1 0.0 copy-done.4
  26.2 0.1 reshape.129
  26.2 0.2 reduce_window_sum.17
  26.5 0.2 slice_reduce_fusion.1
  26.7 0.6 copy-done.6
  27.3 0.6 dynamic-slice
  28.6 0.2 dynamic-update-slice.1
  28.8 0.7 copy-done.5
  29.5 0.1 convert_dynamic-update-slice_fusion
  29.5 29.8 %all-reduce.3 = (f32[32]{0:T(128)S(1)}, f32[32]{0:T(128)S(1)}) all-reduce(f32[32]{0:T(128)S(1)} %dynamic-update-slice.1, f32[32]{0:T(128)S(1)} %convert_dynamic-update-slice_fusion), channel_id=2, replica_groups=mesh['grp'=2,'seq'=16] {'seq'}, use_global_device_ids=true, to_apply=%add.1 | all-reduce | flops 64 | bytes 512
  59.4 0.1 iota_add_fusion
  59.4 0.1 add.179
  59.5 0.1 iota_add_fusion.1
  59.6 0.1 add.183
  59.7 0.2 fusion.29
  59.9 0.1 broadcast_add_fusion.1
  59.9 0.1 reshape.142
  60.0 17.1 %all-gather.2 = f32[16,1,128]{2,1,0:T(1,128)S(1)} all-gather(f32[1,1,128]{2,1,0:T(1,128)S(1)} %reshape.142), channel_id=1, replica_groups=mesh['grp'=2,'seq'=16] {'seq'}, dimensions={0}, use_global_device_ids=true | all-gather | bytes 8704 | tf_op jit(solution)/shard_map/all_gather | solution.py:51
  77.2 0.1 add.186
  77.2 20.7 %all_gather.31 = bf16[2048,128]{1,0:T(8,128)(2,1)S(1)} all-gather(bf16[128,128]{1,0:T(8,128)(2,1)S(1)} %copy-done.3), channel_id=1, replica_groups=mesh['grp'=2,'seq'=16] {'seq'}, dimensions={0}, use_global_device_ids=true | all-gather | bytes 557056 | tf_op jit(solution)/shard_map/all_gather | solution.py:54
  98.0 0.5 fusion.13
  98.4 0.4 fusion.12
  98.8 0.5 multiply_reduce_fusion
  99.3 0.7 copy.18
  100.0 0.0 copy-done.1
  100.1 1.2 fusion.11
  101.3 18.9 %all_gather.35 = bf16[2048,128]{1,0:T(8,128)(2,1)S(1)} all-gather(bf16[128,128]{1,0:T(8,128)(2,1)S(1)} %copy-done.2), channel_id=1, replica_groups=mesh['grp'=2,'seq'=16] {'seq'}, dimensions={0}, use_global_device_ids=true | all-gather | bytes 557056 | tf_op jit(solution)/shard_map/all_gather | solution.py:115
  120.1 18.8 %all-gather.3 = f32[16,1,128]{2,1,0:T(1,128)S(1)} all-gather(f32[1,1,128]{2,1,0:T(1,128)S(1)} %bitcast.24), channel_id=1, replica_groups=mesh['grp'=2,'seq'=16] {'seq'}, dimensions={0}, use_global_device_ids=true | all-gather | bytes 8704 | tf_op jit(solution)/shard_map/all_gather | solution.py:119
  138.9 0.9 fusion.5
  139.8 17.4 %all-gather.4 = f32[16,1,128]{2,1,0:T(1,128)S(1)} all-gather(f32[1,1,128]{2,1,0:T(1,128)S(1)} %bitcast.23), channel_id=1, replica_groups=mesh['grp'=2,'seq'=16] {'seq'}, dimensions={0}, use_global_device_ids=true | all-gather | bytes 8704 | tf_op jit(solution)/shard_map/all_gather | solution.py:120
  157.2 20.3 %all_gather.37 = bf16[2048,128]{1,0:T(8,128)(2,1)S(1)} all-gather(bf16[128,128]{1,0:T(8,128)(2,1)S(1)} %copy-done.1), channel_id=1, replica_groups=mesh['grp'=2,'seq'=16] {'seq'}, dimensions={0}, use_global_device_ids=true | all-gather | bytes 557056 | tf_op jit(solution)/shard_map/all_gather | solution.py:116
  177.5 0.4 fusion.33
  178.0 1.0 convolution_multiply_fusion.2
  178.9 1.0 fusion.17
  179.9 0.1 reduce_sum.53
  180.0 0.1 reverse.4
  180.1 0.2 reduce_window_sum.18
  180.3 0.1 rev.8
  180.4 0.2 slice_reduce_fusion
  180.6 0.2 dynamic-update-slice.2
  180.9 29.8 %all-reduce.2 = f32[32]{0:T(128)S(1)} all-reduce(f32[32]{0:T(128)S(1)} %dynamic-update-slice.2), channel_id=3, replica_groups=mesh['grp'=2,'seq'=16] {'seq'}, use_global_device_ids=true, to_apply=%add.2 | all-reduce | flops 32 | bytes 256
  210.7 0.2 fusion.30
  210.9 0.1 broadcast_add_fusion
  210.9 0.6 reshape.130
  (16 shorter events, 0.1 us)
Async XLA Ops:
  0.6 0.9 copy-start
  1.5 24.6 %copy-start.4 = (f32[128]{0:T(128)S(1)}, f32[128]{0:T(128)}, u32[]{:S(2)}) copy-start(f32[128]{0:T(128)} %param.9) | copy-start | bytes 1540
  26.7 0.7 copy-start.6
  28.8 0.7 copy-start.5
  59.4 17.9 %copy-start.3 = (bf16[128,128]{1,0:T(8,128)(2,1)S(1)}, bf16[128,128]{1,0:T(8,128)(2,1)}, u32[]{:S(2)}) copy-start(bf16[128,128]{1,0:T(8,128)(2,1)} %param.7) | copy-start | bytes 98308
  77.2 20.7 %copy-start.2 = (bf16[128,128]{1,0:T(8,128)(2,1)S(1)}, bf16[128,128]{1,0:T(8,128)(2,1)}, u32[]{:S(2)}) copy-start(bf16[128,128]{1,0:T(8,128)(2,1)} %param.6) | copy-start | bytes 98308
  99.3 0.8 copy-start.1
where the time goes:
time: 212 us
  blocking collectives  197 us (93%)
  local copies, waits for them, and re-layouts  5.65 us (3%)
  matrix products  5.38 us (3%)
    unnamed x2, blocking collectives  59.6 us
    all_gather x1, blocking collectives, local(): lax.all_gather(values, 'seq', axis=0, tiled=True)  24.6 us
    all_gather x1, blocking collectives, local(): lax.all_gather(keys, 'seq', axis=0, tiled=True)  20.7 us
    all_gather x1, blocking collectives, local(): lax.all_gather(out_grad, 'seq', axis=0, tiled=True)  20.3 us
    all_gather x1, blocking collectives, local(): lax.all_gather(queries, 'seq', axis=0, tiled=True)  18.9 us
    all_gather x1, blocking collectives, local(): lax.all_gather(log_total, 'seq', axis=0, tiled=True)  18.8 us
    all_gather x1, blocking collectives, local(): lax.all_gather(row_delta, 'seq', axis=0, tiled=True)  17.4 us
    all_gather x1, blocking collectives, local(): all_gate = lax.all_gather(own_gate, 'seq', axis=0, tiled=True)  17.1 us

commit v1 on v0

--- a/solution.py
+++ b/solution.py
@@ -1,6 +1,8 @@
 import jax
 import jax.numpy as jnp
 from jax import lax
+from jax.experimental import pallas as pl
+from jax.experimental.pallas import tpu as pltpu
 from jax.sharding import PartitionSpec as P
 
 masked_value = -1e30
@@ -30,7 +32,7 @@
     return jnp.where(visible, jnp.exp(scores - row_total[:, None]), 0.0)
 
 
-def local(queries, keys, values, log_gate, out_grad, segment_order):
+def local_general(queries, keys, values, log_gate, out_grad, segment_order):
     tokens_here, width = queries.shape
     devices = lax.axis_size("seq")
     segment_rows = tokens_here // 2
@@ -156,6 +158,283 @@
     return (attn_out, query_grad, key_grad, value_grad, gate_grad)
 
 
+LOG2E = 1.4426950408889634
+META = 16
+ROWS = 256
+
+
+def pack_kernel(q_ref, k_ref, v_ref, g_ref, gate_ref, order_ref, out_ref):
+    tokens = q_ref.shape[0]
+    out_ref[0:tokens] = q_ref[...]
+    out_ref[tokens : 2 * tokens] = k_ref[...]
+    out_ref[2 * tokens : 3 * tokens] = v_ref[...]
+    out_ref[3 * tokens : 4 * tokens] = g_ref[...]
+    gate = gate_ref[...]
+    high = gate.astype(jnp.bfloat16).astype(jnp.float32)
+    rest = gate - high
+    mid = rest.astype(jnp.bfloat16).astype(jnp.float32)
+    low = rest - mid
+    lane = lax.broadcasted_iota(jnp.int32, (META, tokens), 1)
+    row = lax.broadcasted_iota(jnp.int32, (META, tokens), 0)
+    order = order_ref[...].astype(jnp.float32)
+    place = jnp.where(lane < tokens // 2, order[:, 0:1], order[:, 1:2])
+    meta = jnp.where(
+        row == 0, high, jnp.where(row == 1, mid, jnp.where(row == 2, low, place))
+    )
+    out_ref[4 * tokens : 4 * tokens + META] = meta.astype(jnp.bfloat16)
+
+
+def roll_sum_lanes(x, span, reverse):
+    lanes = x.shape[1]
+    lane = lax.broadcasted_iota(jnp.int32, x.shape, 1)
+    step = 1
+    while step < span:
+        if reverse:
+            x = x + jnp.where(lane < lanes - step, pltpu.roll(x, lanes - step, 1), 0.0)
+        else:
+            x = x + jnp.where(lane >= step, pltpu.roll(x, step, 1), 0.0)
+        step *= 2
+    return x
+
+
+def roll_sum_rows(x, reverse):
+    rows = x.shape[0]
+    row = lax.broadcasted_iota(jnp.int32, x.shape, 0)
+    step = 1
+    while step < rows:
+        if reverse:
+            x = x + jnp.where(row < rows - step, pltpu.roll(x, rows - step, 0), 0.0)
+        else:
+            x = x + jnp.where(row >= step, pltpu.roll(x, step, 0), 0.0)
+        step *= 2
+    return x
+
+
+def core_kernel(counts, tokens, width, *refs):
+    blocks = refs[: len(counts)]
+    out_ref, dq_ref, dk_ref, dv_ref, gate_ref = refs[len(counts) : len(counts) + 5]
+    (qs, ks, vs, gs, cums, key_row, scores, top_col, inv_col, delta_col, outs, points,
+     point_rows) = refs[len(counts) + 5 :]
+    seg = tokens // 2
+    total = qs.shape[0]
+    segments = total // seg
+    size = 4 * tokens + META
+    scale = width ** (-0.5)
+    lane1 = lax.broadcasted_iota(jnp.int32, (1, tokens), 1)
+    left = lane1 < seg
+
+    own_place = None
+    for ref, count in zip(blocks, counts):
+        for index in range(count):
+            base = index * size
+            meta = ref[base + 4 * tokens : base + size].astype(jnp.float32)
+            gate = (meta[0:1] + meta[1:2]) + meta[2:3]
+            place = meta[3:4].astype(jnp.int32)
+            pair = (place[0, 0], place[0, seg])
+            if own_place is None:
+                own_place = pair
+            for half in range(2):
+                at = pl.multiple_of(pair[half] * seg, seg)
+                for slot, dest in enumerate((qs, ks, vs, gs)):
+                    first = base + slot * tokens + half * seg
+                    dest[pl.ds(at, seg), :] = ref[first : first + seg, :]
+                shifted = gate if half == 0 else pltpu.roll(gate, seg, 1)
+                cums[pl.ds(pair[half], 1), :] = jnp.where(left, shifted, 0.0)
+
+    inside = roll_sum_lanes(cums[...], seg, False)
+    whole = jnp.broadcast_to(inside[:, seg - 1 : seg], inside.shape)
+    before = roll_sum_rows(whole, False) - whole
+    cums[...] = (inside + before) * LOG2E
+    for tile in range(segments // 2):
+        even = cums[2 * tile : 2 * tile + 1, :]
+        odd = pltpu.roll(cums[2 * tile + 1 : 2 * tile + 2, :], seg, 1)
+        key_row[:, tile * tokens : (tile + 1) * tokens] = jnp.where(left, even, odd)
+
+    points[...] = jnp.zeros_like(points)
+    block_rows = ROWS
+    row_in = lax.broadcasted_iota(jnp.int32, (block_rows, block_rows), 0)
+    col_in = lax.broadcasted_iota(jnp.int32, (block_rows, block_rows), 1)
+    causal = col_in <= row_in
+    for block in range(total // block_rows):
+        r0 = block * block_rows
+        q = qs[r0 : r0 + block_rows, :]
+        g = gs[r0 : r0 + block_rows, :]
+        best = None
+        for tile in range(block + 1):
+            c0 = tile * block_rows
+            s = contract_last(q, ks[c0 : c0 + block_rows, :]) * (scale * LOG2E)
+            s = s - key_row[:, c0 : c0 + block_rows]
+            if tile == block:
+                s = jnp.where(causal, s, masked_value)
+            scores[:, c0 : c0 + block_rows] = s
+            part = jnp.maximum(s[:, :128], s[:, 128:])
+            best = part if best is None else jnp.maximum(best, part)
+        top = jnp.max(best, axis=1, keepdims=True)
+        mass = None
+        for tile in range(block + 1):
+            c0 = tile * block_rows
+            e = jnp.exp2(scores[:, c0 : c0 + block_rows] - top)
+            scores[:, c0 : c0 + block_rows] = e
+            part = e[:, :128] + e[:, 128:]
+            mass = part if mass is None else mass + part
+        inv = 1.0 / jnp.sum(mass, axis=1, keepdims=True)
+        acc = jnp.zeros((block_rows, width), jnp.float32)
+        for tile in range(block + 1):
+            c0 = tile * block_rows
+            p = (scores[:, c0 : c0 + block_rows] * inv).astype(jnp.bfloat16)
+            acc = acc + jnp.dot(p, vs[c0 : c0 + block_rows, :], preferred_element_type=jnp.float32)
+        delta = jnp.sum(g.astype(jnp.float32) * acc, axis=1, keepdims=True)
+        outs[r0 : r0 + block_rows, :] = acc
+        top_col[r0 : r0 + block_rows, :] = top
+        inv_col[r0 : r0 + block_rows, :] = inv
+        delta_col[r0 : r0 + block_rows, :] = delta
+        for tile in range(block + 1):
+            c0 = tile * block_rows
+            dp = contract_last(g, vs[c0 : c0 + block_rows, :])
+            ds = (scores[:, c0 : c0 + block_rows] * inv) * (dp - delta)
+            points[:, c0 : c0 + block_rows] += jnp.sum(
+                ds.reshape(block_rows // 8, 8, block_rows), axis=0
+            )
+
+    for tile in range(segments // 2):
+        c0 = tile * tokens
+        point_rows[tile : tile + 1, :] = -jnp.sum(
+            points[:, c0 : c0 + tokens], axis=0, keepdims=True
+        )
+    inside = roll_sum_lanes(point_rows[...], tokens, True)
+    whole = jnp.broadcast_to(inside[:, 0:1], inside.shape)
+    point_rows[...] = inside + (roll_sum_rows(whole, True) - whole)
+    halves = []
+    for half in range(2):
+        line = point_rows[pl.ds(own_place[half] // 2, 1), :]
+        turned = pltpu.roll(line, seg, 1)
+        halves.append(jnp.where(own_place[half] % 2 == half, line, turned))
+    gate_ref[...] = jnp.where(left, halves[0], halves[1])
+
+    own = blocks[0]
+    starts = [pl.multiple_of(p * seg, seg) for p in own_place]
+
+    def pick(ref):
+        return jnp.concatenate([ref[pl.ds(s, seg), :] for s in starts], axis=0)
+
+    top, inv, delta = pick(top_col), pick(inv_col), pick(delta_col)
+    out_ref[...] = pick(outs).astype(jnp.bfloat16)
+    inner = lax.broadcasted_iota(jnp.int32, (tokens, 1), 0)
+    row_pos = jnp.where(inner < seg, starts[0] + inner, starts[1] + inner - seg)
+    chunk = 512
+    q = own[0:tokens, :]
+    k = own[tokens : 2 * tokens, :]
+    v = own[2 * tokens : 3 * tokens, :]
+    g = own[3 * tokens : 4 * tokens, :]
+    acc = jnp.zeros((tokens, width), jnp.float32)
+    for c0 in range(0, total, chunk):
+        keys = ks[c0 : c0 + chunk, :]
+        s = contract_last(q, keys) * (scale * LOG2E) - key_row[:, c0 : c0 + chunk]
+        seen = lax.broadcasted_iota(jnp.int32, (tokens, chunk), 1) + c0 <= row_pos
+        p = jnp.where(seen, jnp.exp2(s - top), 0.0) * inv
+        ds = p * (contract_last(g, vs[c0 : c0 + chunk, :]) - delta)
+        acc = acc + jnp.dot(ds.astype(jnp.bfloat16), keys, preferred_element_type=jnp.float32)
+    dq_ref[...] = acc * scale
+
+    rows = [cums[pl.ds(p, 1), :] for p in own_place]
+    own_key = jnp.where(left, rows[0], pltpu.roll(rows[1], seg, 1))
+    col_pos = jnp.where(left, starts[0] + lane1, starts[1] + lane1 - seg)
+    acc_k = jnp.zeros((tokens, width), jnp.float32)
+    acc_v = jnp.zeros((tokens, width), jnp.float32)
+    for r0 in range(0, total, chunk):
+        queries = qs[r0 : r0 + chunk, :]
+        grads = gs[r0 : r0 + chunk, :]
+        s = contract_last(queries, k) * (scale * LOG2E) - own_key
+        seen = lax.broadcasted_iota(jnp.int32, (chunk, tokens), 0) + r0 >= col_pos
+        p = jnp.where(seen, jnp.exp2(s - top_col[r0 : r0 + chunk, :]), 0.0)
+        p = p * inv_col[r0 : r0 + chunk, :]
+        ds = p * (contract_last(grads, v) - delta_col[r0 : r0 + chunk, :])
+        acc_v = acc_v + contract_first(p.astype(jnp.bfloat16), grads)
+        acc_k = acc_k + contract_first(ds.astype(jnp.bfloat16), queries)
+    dk_ref[...] = acc_k * scale
+    dv_ref[...] = acc_v
+
+
+def core_call(blocks, tokens, width, devices):
+    size = 4 * tokens + META
+    counts = tuple(b.shape[0] // size for b in blocks)
+    total = tokens * devices
+    segments = 2 * devices
+    vmem = pl.BlockSpec(memory_space=pltpu.VMEM)
+    square = jax.ShapeDtypeStruct((tokens, width), jnp.float32)
+    import functools
+
+    return pl.pallas_call(
+        functools.partial(core_kernel, counts, tokens, width),
+        out_shape=(
+            jax.ShapeDtypeStruct((tokens, width), jnp.bfloat16),
+            square,
+            square,
+            square,
+            jax.ShapeDtypeStruct((1, tokens), jnp.float32),
+        ),
+        in_specs=[vmem] * len(blocks),
+        out_specs=[vmem] * 5,
+        scratch_shapes=[pltpu.VMEM((total, width), jnp.bfloat16)] * 4
+        + [
+            pltpu.VMEM((segments, tokens), jnp.float32),
+            pltpu.VMEM((1, total), jnp.float32),
+            pltpu.VMEM((ROWS, total), jnp.float32),
+            pltpu.VMEM((total, 1), jnp.float32),
+            pltpu.VMEM((total, 1), jnp.float32),
+            pltpu.VMEM((total, 1), jnp.float32),
+            pltpu.VMEM((total, width), jnp.float32),
+            pltpu.VMEM((8, total), jnp.float32),
+            pltpu.VMEM((segments // 2, tokens), jnp.float32),
+        ],
+        name="core",
+    )(*blocks)
+
+
+def shift(x, devices, ring=0, flip=0):
+    line = devices // 4
+    pairs = []
+    for i in range(devices):
+        place, low = i // 4, i % 4
+        pairs.append((i, ((place + ring) % line) * 4 + (low ^ flip)))
+    return lax.ppermute(x, "seq", pairs)
+
+
+def gather_blocks(x, devices):
+    a = shift(x, devices, flip=2)
+    b = shift(x, devices, ring=1)
+    c = shift(x, devices, ring=-1)
+    d = shift(c, devices, flip=2)
+    e = shift(a, devices, ring=1)
+    f = shift(c, devices, ring=-1)
+    g = shift(f, devices, flip=2)
+    near = [x, a, b, c, d, e, f, g]
+    return near + [shift(t, devices, flip=1) for t in near]
+
+
+def local_small(queries, keys, values, log_gate, out_grad, segment_order):
+    tokens, width = queries.shape
+    devices = lax.axis_size("seq")
+    vmem = pl.BlockSpec(memory_space=pltpu.VMEM)
+    packed = pl.pallas_call(
+        pack_kernel,
+        out_shape=jax.ShapeDtypeStruct((4 * tokens + META, width), jnp.bfloat16),
+        in_specs=[vmem] * 6,
+        out_specs=vmem,
+        name="pack",
+    )(queries, keys, values, out_grad, log_gate.reshape(1, tokens), segment_order.reshape(1, 2))
+    blocks = gather_blocks(packed, devices)
+    out, dq, dk, dv, gate = core_call(blocks, tokens, width, devices)
+    return (out, dq, dk, dv, gate.reshape(tokens))
+
+
+def local(queries, keys, values, log_gate, out_grad, segment_order):
+    tokens, width = queries.shape
+    small = tokens == 128 and width == 128 and lax.axis_size("seq") == 16
+    path = local_small if small else local_general
+    return path(queries, keys, values, log_gate, out_grad, segment_order)
+
+
 def solution(mesh):
     placed = (
         P(("grp", "seq"), None),

time: 212 us -> 41.1 us (0.19)
  blocking collectives: 197 us -> 0 us
  starting transfers between devices: 0 us -> 15.8 us
  Pallas kernels: 0 us -> 14.7 us
  waiting for transfers between devices: 0 us -> 8.55 us
  matrix products: 5.38 us -> 0 us
  local copies, waits for them, and re-layouts: 5.65 us -> 1.05 us
    all_gather x7 -> x0, blocking collectives: 138 us -> none  [the longest x1 24.6 us: local(): lax.all_gather(values, 'seq', axis=0, tiled=True)]
    unnamed x2 -> x0, blocking collectives: 59.6 us -> none
    ppermute x0 -> x15, starting transfers between devices: none -> 15.8 us  [shift(): return lax.ppermute(x, 'seq', pairs)]
    pallas_call x0 -> x2, Pallas kernels: none -> 14.7 us  [the longest x1 13.1 us: core_call(): pl.pallas_call(functools.partial(core_kernel, counts, tokens, width), out...]
    ppermute x0 -> x15, waiting for transfers between devices: none -> 8.55 us  [shift(): return lax.ppermute(x, 'seq', pairs)]
    dot_general x7 -> x0, matrix products: 5.38 us -> none  [the longest x2 1.95 us: contract_first(): lax.dot_general(left, right, (((0,), (0,)), ((), ())), preferred_element_...]
    unnamed x23 -> x30, local copies, waits for them, and re-layouts: 4.09 us -> 1.05 us
  transfers between devices with their start and end apart: 0 -> 15, of which waited for: 0 -> 6; matrix products, arithmetic and copies ran while one was open for 0% -> 0% of each run, Pallas kernels for 0% -> 0%
where the time goes in v1:
time: 41.1 us; the launch traced here: 40.9 us
  starting transfers between devices  15.8 us (38%)
  Pallas kernels  14.7 us (36%)
  waiting for transfers between devices  8.55 us (21%)
  local copies, waits for them, and re-layouts  1.05 us (3%)
  between operations  0.79 us (2%)
    ppermute x15, starting transfers between devices, shift(): return lax.ppermute(x, 'seq', pairs)  15.8 us
    pallas_call x1, Pallas kernels, core_call(): pl.pallas_call(functools.partial(core_kernel, counts, tokens, width), out...  13.1 us
    ppermute x15, waiting for transfers between devices, shift(): return lax.ppermute(x, 'seq', pairs)  8.55 us
    pallas_call x1, Pallas kernels, local_small(): pl.pallas_call(pack_kernel, out_shape=jax.ShapeDtypeStruct((4 * tokens +...  1.54 us
    unnamed x30, local copies, waits for them, and re-layouts  1.05 us
  transfers between devices with their start and end apart: 15, of which 6 were waited for; matrix products, arithmetic and copies ran while one was open for 0% of the time, Pallas kernels for 0%

profile of v1, /device:TPU:0, one launch (start us, length us, event | category | flops | bytes accessed | tf_op | source)
XLA Modules:
  0.0 40.9 jit_solution(7150699789651709668)
XLA Ops:
  0.6 1.5 %pack.1.refs_0_ = bf16[528,128]{1,0:T(8,128)(2,1)} custom-call(bf16[128,128]{1,0:T(8,128)(2,1)} %q_ref.1, bf16[128,128]{1,0:T(8,128)(2,1)} %k_ref.1, bf16[128,128]{1,0:T(8,128)(2,1)} %v_ref.1, bf16[128,128]{1,0:T(8,128)(2,1)} %g_ref.1, f32[1,128]{1,0:T(1,128)} %bitcast.3, s32[1,2]{1,0:T(1,128)} %bitcast.4), custom_call_target="tpu_custom_call" | custom-call | tf_op jit(solution)/shard_map/pack/pallas_call | solution.py:419
  2.2 5.1 %collective-permute-start.2 = (bf16[528,128]{1,0:T(8,128)(2,1)}, bf16[528,128]{1,0:T(8,128)(2,1)S(1)}, u32[]{:S(2)}, u32[]{:S(2)}) collective-permute-start(bf16[528,128]{1,0:T(8,128)(2,1)} %pack.1.refs_0_), channel_id=1, source_target_pairs={{0,12},{1,13},{2,14},{3,15},{4,0},{5,1},{6,2},{7,3},{8,4},{9,5},{1... | collective-permute-start | bytes 405512 | tf_op jit(solution)/shard_map/ppermute | solution.py:400
  7.3 0.0 collective-permute-start.7
  7.3 0.0 collective-permute-start.1
  7.3 1.5 %collective-permute-start = (bf16[528,128]{1,0:T(8,128)(2,1)}, bf16[528,128]{1,0:T(8,128)(2,1)S(1)}, u32[]{:S(2)}, u32[]{:S(2)}) collective-permute-start(bf16[528,128]{1,0:T(8,128)(2,1)} %pack.1.refs_0_), channel_id=1, source_target_pairs={{0,2},{1,3},{2,0},{3,1},{4,6},{5,7},{6,4},{7,5},{8,10},{9,11},{10,... | collective-permute-start | bytes 405512 | tf_op jit(solution)/shard_map/ppermute | solution.py:400
  8.7 2.8 %collective-permute-done.2.refs_3_ = bf16[528,128]{1,0:T(8,128)(2,1)S(1)} collective-permute-done((bf16[528,128]{1,0:T(8,128)(2,1)}, bf16[528,128]{1,0:T(8,128)(2,1)S(1)}, u32[]{:S(2)}, u32[]{:S(2)}) %collective-permute-start.2) | collective-permute-done | bytes 135200 | tf_op jit(solution)/shard_map/ppermute | solution.py:400
  11.5 4.2 %collective-permute-start.5 = (bf16[528,128]{1,0:T(8,128)(2,1)S(1)}, bf16[528,128]{1,0:T(8,128)(2,1)S(1)}, u32[]{:S(2)}, u32[]{:S(2)}) collective-permute-start(bf16[528,128]{1,0:T(8,128)(2,1)S(1)} %collective-permute-done.2.refs_3_), channel_id=1, source_target_pairs={{0,12},{1,13},{2,14},{3,15},{4,0},{5,1},{6,2},{7,3},{8,4},{9,5},{1... | collective-permute-start | bytes 405512 | tf_op jit(solution)/shard_map/ppermute | solution.py:400
  15.7 0.0 collective-permute-start.10
  15.7 0.0 collective-permute-done.7.refs_8_
  15.7 1.6 %collective-permute-start.3 = (bf16[528,128]{1,0:T(8,128)(2,1)S(1)}, bf16[528,128]{1,0:T(8,128)(2,1)S(1)}, u32[]{:S(2)}, u32[]{:S(2)}) collective-permute-start(bf16[528,128]{1,0:T(8,128)(2,1)S(1)} %collective-permute-done.2.refs_3_), channel_id=1, source_target_pairs={{0,2},{1,3},{2,0},{3,1},{4,6},{5,7},{6,4},{7,5},{8,10},{9,11},{10,... | collective-permute-start | bytes 405512 | tf_op jit(solution)/shard_map/ppermute | solution.py:400
  17.3 0.0 collective-permute-done.1.refs_2_
  17.3 0.2 collective-permute-start.9
  17.5 0.0 collective-permute-done.refs_1_
  17.5 0.0 collective-permute-start.4
  17.5 0.9 %collective-permute-done.5.refs_6_ = bf16[528,128]{1,0:T(8,128)(2,1)S(1)} collective-permute-done((bf16[528,128]{1,0:T(8,128)(2,1)S(1)}, bf16[528,128]{1,0:T(8,128)(2,1)S(1)}, u32[]{:S(2)}, u32[]{:S(2)}) %collective-permute-start.5) | collective-permute-done | bytes 135200 | tf_op jit(solution)/shard_map/ppermute | solution.py:400
  18.4 2.4 %collective-permute-start.6 = (bf16[528,128]{1,0:T(8,128)(2,1)S(1)}, bf16[528,128]{1,0:T(8,128)(2,1)S(1)}, u32[]{:S(2)}, u32[]{:S(2)}) collective-permute-start(bf16[528,128]{1,0:T(8,128)(2,1)S(1)} %collective-permute-done.5.refs_6_), channel_id=1, source_target_pairs={{0,2},{1,3},{2,0},{3,1},{4,6},{5,7},{6,4},{7,5},{8,10},{9,11},{10,... | collective-permute-start | bytes 405512 | tf_op jit(solution)/shard_map/ppermute | solution.py:400
  20.7 0.0 collective-permute-done.10.refs_11_
  20.8 0.0 collective-permute-start.8
  20.8 1.5 %collective-permute-done.3.refs_4_ = bf16[528,128]{1,0:T(8,128)(2,1)S(1)} collective-permute-done((bf16[528,128]{1,0:T(8,128)(2,1)S(1)}, bf16[528,128]{1,0:T(8,128)(2,1)S(1)}, u32[]{:S(2)}, u32[]{:S(2)}) %collective-permute-start.3) | collective-permute-done | bytes 135200 | tf_op jit(solution)/shard_map/ppermute | solution.py:400
  22.3 0.0 collective-permute-start.13
  22.3 0.0 collective-permute-done.9.refs_10_
  22.3 0.0 copy-start.7
  22.3 0.5 %collective-permute-start.11 = (bf16[528,128]{1,0:T(8,128)(2,1)S(1)}, bf16[528,128]{1,0:T(8,128)(2,1)S(1)}, u32[]{:S(2)}, u32[]{:S(2)}) collective-permute-start(bf16[528,128]{1,0:T(8,128)(2,1)S(1)} %collective-permute-done.3.refs_4_), channel_id=1, source_target_pairs={{0,1},{1,0},{2,3},{3,2},{4,5},{5,4},{6,7},{7,6},{8,9},{9,8},{10,11... | collective-permute-start | bytes 405512 | tf_op jit(solution)/shard_map/ppermute | solution.py:400
  22.8 2.3 %collective-permute-done.4.refs_5_ = bf16[528,128]{1,0:T(8,128)(2,1)S(1)} collective-permute-done((bf16[528,128]{1,0:T(8,128)(2,1)S(1)}, bf16[528,128]{1,0:T(8,128)(2,1)S(1)}, u32[]{:S(2)}, u32[]{:S(2)}) %collective-permute-start.4) | collective-permute-done | bytes 135200 | tf_op jit(solution)/shard_map/ppermute | solution.py:400
  25.1 0.0 collective-permute-start.12
  25.1 0.0 collective-permute-done.6.refs_7_
  25.1 0.0 copy-start.9
  25.1 0.5 %collective-permute-start.14 = (bf16[528,128]{1,0:T(8,128)(2,1)S(1)}, bf16[528,128]{1,0:T(8,128)(2,1)S(1)}, u32[]{:S(2)}, u32[]{:S(2)}) collective-permute-start(bf16[528,128]{1,0:T(8,128)(2,1)S(1)} %collective-permute-done.6.refs_7_), channel_id=1, source_target_pairs={{0,1},{1,0},{2,3},{3,2},{4,5},{5,4},{6,7},{7,6},{8,9},{9,8},{10,11... | collective-permute-start | bytes 405512 | tf_op jit(solution)/shard_map/ppermute | solution.py:400
  25.6 0.0 collective-permute-done.8.refs_9_
  25.6 0.0 collective-permute-done.13.refs_14_
  25.6 0.0 copy-start.11
  25.6 0.0 collective-permute-done.11.refs_12_
  25.7 0.0 copy-start.12
  25.7 0.8 %collective-permute-done.12.refs_13_ = bf16[528,128]{1,0:T(8,128)(2,1)S(1)} collective-permute-done((bf16[528,128]{1,0:T(8,128)(2,1)S(1)}, bf16[528,128]{1,0:T(8,128)(2,1)S(1)}, u32[]{:S(2)}, u32[]{:S(2)}) %collective-permute-start.12) | collective-permute-done | bytes 135200 | tf_op jit(solution)/shard_map/ppermute | solution.py:400
  26.5 0.2 collective-permute-done.14.refs_15_
  26.7 0.0 copy-done.3
  26.7 0.0 copy-done.4
  26.7 0.0 copy-done.5
  26.7 0.0 copy-done.6
  26.7 0.0 copy-done.7
  26.7 0.0 copy-done.8
  26.7 0.0 copy-done.9
  26.7 0.0 copy-done.10
  26.7 0.0 copy-done.11
  26.8 0.0 copy-done.12
  26.8 0.3 copy-done.13
  27.1 0.7 %copy-done.14 = bf16[528,128]{1,0:T(8,128)(2,1)} copy-done((bf16[528,128]{1,0:T(8,128)(2,1)}, bf16[528,128]{1,0:T(8,128)(2,1)S(1)}, u32[]{:S(2)}) %copy-start.14) | copy-done | bytes 135192
  27.8 13.1 %core.1 = (bf16[128,128]{1,0:T(8,128)(2,1)}, f32[128,128]{1,0:T(8,128)}, f32[128,128]{1,0:T(8,128)}, f32[128,128]{1,0:T(8,128)}, f32[1,128]{1,0:T(1,128)}) custom-call(bf16[528,128]{1,0:T(8,128)(2,1)} %pack.1.refs_0_, bf16[528,128]{1,0:T(8,128)(2,1)} %copy-done.3, bf16[528,128]{1,0:T(8,128)(2,1)} %copy-done.2, bf16[528,128]{1,0:T(8,128)(2,1)} %copy-done, ...), custom_call_target="tpu_custom_call" | custom-call | tf_op jit(solution)/shard_map/core/pallas_call | solution.py:367
  (14 shorter events, 0.0 us)
Async XLA Ops:
  2.2 9.4 %collective-permute-start.2 = (bf16[528,128]{1,0:T(8,128)(2,1)}, bf16[528,128]{1,0:T(8,128)(2,1)S(1)}, u32[]{:S(2)}, u32[]{:S(2)}) collective-permute-start(bf16[528,128]{1,0:T(8,128)(2,1)} %pack.1.refs_0_), channel_id=1, source_target_pairs={{0,12},{1,13},{2,14},{3,15},{4,0},{5,1},{6,2},{7,3},{8,4},{9,5},{1... | collective-permute-start | bytes 405512 | tf_op jit(solution)/shard_map/ppermute | solution.py:400
  7.3 8.5 %collective-permute-start.7 = (bf16[528,128]{1,0:T(8,128)(2,1)}, bf16[528,128]{1,0:T(8,128)(2,1)S(1)}, u32[]{:S(2)}, u32[]{:S(2)}) collective-permute-start(bf16[528,128]{1,0:T(8,128)(2,1)} %pack.1.refs_0_), channel_id=1, source_target_pairs={{0,1},{1,0},{2,3},{3,2},{4,5},{5,4},{6,7},{7,6},{8,9},{9,8},{10,11... | collective-permute-start | bytes 405512 | tf_op jit(solution)/shard_map/ppermute | solution.py:400
  7.3 10.0 %collective-permute-start.1 = (bf16[528,128]{1,0:T(8,128)(2,1)}, bf16[528,128]{1,0:T(8,128)(2,1)S(1)}, u32[]{:S(2)}, u32[]{:S(2)}) collective-permute-start(bf16[528,128]{1,0:T(8,128)(2,1)} %pack.1.refs_0_), channel_id=1, source_target_pairs={{0,4},{1,5},{2,6},{3,7},{4,8},{5,9},{6,10},{7,11},{8,12},{9,13},{1... | collective-permute-start | bytes 405512 | tf_op jit(solution)/shard_map/ppermute | solution.py:400
  7.3 10.2 %collective-permute-start = (bf16[528,128]{1,0:T(8,128)(2,1)}, bf16[528,128]{1,0:T(8,128)(2,1)S(1)}, u32[]{:S(2)}, u32[]{:S(2)}) collective-permute-start(bf16[528,128]{1,0:T(8,128)(2,1)} %pack.1.refs_0_), channel_id=1, source_target_pairs={{0,2},{1,3},{2,0},{3,1},{4,6},{5,7},{6,4},{7,5},{8,10},{9,11},{10,... | collective-permute-start | bytes 405512 | tf_op jit(solution)/shard_map/ppermute | solution.py:400
  11.5 15.1 %copy-start = (bf16[528,128]{1,0:T(8,128)(2,1)}, bf16[528,128]{1,0:T(8,128)(2,1)S(1)}, u32[]{:S(2)}) copy-start(bf16[528,128]{1,0:T(8,128)(2,1)S(1)} %collective-permute-done.2.refs_3_) | copy-start | bytes 405508
  11.5 6.8 %collective-permute-start.5 = (bf16[528,128]{1,0:T(8,128)(2,1)S(1)}, bf16[528,128]{1,0:T(8,128)(2,1)S(1)}, u32[]{:S(2)}, u32[]{:S(2)}) collective-permute-start(bf16[528,128]{1,0:T(8,128)(2,1)S(1)} %collective-permute-done.2.refs_3_), channel_id=1, source_target_pairs={{0,12},{1,13},{2,14},{3,15},{4,0},{5,1},{6,2},{7,3},{8,4},{9,5},{1... | collective-permute-start | bytes 405512 | tf_op jit(solution)/shard_map/ppermute | solution.py:400
  15.7 5.0 %collective-permute-start.10 = (bf16[528,128]{1,0:T(8,128)(2,1)S(1)}, bf16[528,128]{1,0:T(8,128)(2,1)S(1)}, u32[]{:S(2)}, u32[]{:S(2)}) collective-permute-start(bf16[528,128]{1,0:T(8,128)(2,1)S(1)} %collective-permute-done.2.refs_3_), channel_id=1, source_target_pairs={{0,1},{1,0},{2,3},{3,2},{4,5},{5,4},{6,7},{7,6},{8,9},{9,8},{10,11... | collective-permute-start | bytes 405512 | tf_op jit(solution)/shard_map/ppermute | solution.py:400
  15.7 10.9 %copy-start.1 = (bf16[528,128]{1,0:T(8,128)(2,1)}, bf16[528,128]{1,0:T(8,128)(2,1)S(1)}, u32[]{:S(2)}) copy-start(bf16[528,128]{1,0:T(8,128)(2,1)S(1)} %collective-permute-done.7.refs_8_) | copy-start | bytes 405508
  15.7 6.5 %collective-permute-start.3 = (bf16[528,128]{1,0:T(8,128)(2,1)S(1)}, bf16[528,128]{1,0:T(8,128)(2,1)S(1)}, u32[]{:S(2)}, u32[]{:S(2)}) collective-permute-start(bf16[528,128]{1,0:T(8,128)(2,1)S(1)} %collective-permute-done.2.refs_3_), channel_id=1, source_target_pairs={{0,2},{1,3},{2,0},{3,1},{4,6},{5,7},{6,4},{7,5},{8,10},{9,11},{10,... | collective-permute-start | bytes 405512 | tf_op jit(solution)/shard_map/ppermute | solution.py:400
  17.3 9.4 %copy-start.2 = (bf16[528,128]{1,0:T(8,128)(2,1)}, bf16[528,128]{1,0:T(8,128)(2,1)S(1)}, u32[]{:S(2)}) copy-start(bf16[528,128]{1,0:T(8,128)(2,1)S(1)} %collective-permute-done.1.refs_2_) | copy-start | bytes 405508
  17.3 5.0 %collective-permute-start.9 = (bf16[528,128]{1,0:T(8,128)(2,1)S(1)}, bf16[528,128]{1,0:T(8,128)(2,1)S(1)}, u32[]{:S(2)}, u32[]{:S(2)}) collective-permute-start(bf16[528,128]{1,0:T(8,128)(2,1)S(1)} %collective-permute-done.1.refs_2_), channel_id=1, source_target_pairs={{0,1},{1,0},{2,3},{3,2},{4,5},{5,4},{6,7},{7,6},{8,9},{9,8},{10,11... | collective-permute-start | bytes 405512 | tf_op jit(solution)/shard_map/ppermute | solution.py:400
  17.5 9.2 %copy-start.3 = (bf16[528,128]{1,0:T(8,128)(2,1)}, bf16[528,128]{1,0:T(8,128)(2,1)S(1)}, u32[]{:S(2)}) copy-start(bf16[528,128]{1,0:T(8,128)(2,1)S(1)} %collective-permute-done.refs_1_) | copy-start | bytes 405508
  17.5 7.6 %collective-permute-start.4 = (bf16[528,128]{1,0:T(8,128)(2,1)S(1)}, bf16[528,128]{1,0:T(8,128)(2,1)S(1)}, u32[]{:S(2)}, u32[]{:S(2)}) collective-permute-start(bf16[528,128]{1,0:T(8,128)(2,1)S(1)} %collective-permute-done.refs_1_), channel_id=1, source_target_pairs={{0,4},{1,5},{2,6},{3,7},{4,8},{5,9},{6,10},{7,11},{8,12},{9,13},{1... | collective-permute-start | bytes 405512 | tf_op jit(solution)/shard_map/ppermute | solution.py:400
  18.4 8.3 %copy-start.4 = (bf16[528,128]{1,0:T(8,128)(2,1)}, bf16[528,128]{1,0:T(8,128)(2,1)S(1)}, u32[]{:S(2)}) copy-start(bf16[528,128]{1,0:T(8,128)(2,1)S(1)} %collective-permute-done.5.refs_6_) | copy-start | bytes 405508
  18.4 6.7 %collective-permute-start.6 = (bf16[528,128]{1,0:T(8,128)(2,1)S(1)}, bf16[528,128]{1,0:T(8,128)(2,1)S(1)}, u32[]{:S(2)}, u32[]{:S(2)}) collective-permute-start(bf16[528,128]{1,0:T(8,128)(2,1)S(1)} %collective-permute-done.5.refs_6_), channel_id=1, source_target_pairs={{0,2},{1,3},{2,0},{3,1},{4,6},{5,7},{6,4},{7,5},{8,10},{9,11},{10,... | collective-permute-start | bytes 405512 | tf_op jit(solution)/shard_map/ppermute | solution.py:400
  20.8 5.9 %copy-start.5 = (bf16[528,128]{1,0:T(8,128)(2,1)}, bf16[528,128]{1,0:T(8,128)(2,1)S(1)}, u32[]{:S(2)}) copy-start(bf16[528,128]{1,0:T(8,128)(2,1)S(1)} %collective-permute-done.10.refs_11_) | copy-start | bytes 405508
  20.8 4.9 %collective-permute-start.8 = (bf16[528,128]{1,0:T(8,128)(2,1)S(1)}, bf16[528,128]{1,0:T(8,128)(2,1)S(1)}, u32[]{:S(2)}, u32[]{:S(2)}) collective-permute-start(bf16[528,128]{1,0:T(8,128)(2,1)S(1)} %collective-permute-done.refs_1_), channel_id=1, source_target_pairs={{0,1},{1,0},{2,3},{3,2},{4,5},{5,4},{6,7},{7,6},{8,9},{9,8},{10,11... | collective-permute-start | bytes 405512 | tf_op jit(solution)/shard_map/ppermute | solution.py:400
  22.3 4.4 %copy-start.6 = (bf16[528,128]{1,0:T(8,128)(2,1)}, bf16[528,128]{1,0:T(8,128)(2,1)S(1)}, u32[]{:S(2)}) copy-start(bf16[528,128]{1,0:T(8,128)(2,1)S(1)} %collective-permute-done.3.refs_4_) | copy-start | bytes 405508
  22.3 3.4 %collective-permute-start.13 = (bf16[528,128]{1,0:T(8,128)(2,1)S(1)}, bf16[528,128]{1,0:T(8,128)(2,1)S(1)}, u32[]{:S(2)}, u32[]{:S(2)}) collective-permute-start(bf16[528,128]{1,0:T(8,128)(2,1)S(1)} %collective-permute-done.5.refs_6_), channel_id=1, source_target_pairs={{0,1},{1,0},{2,3},{3,2},{4,5},{5,4},{6,7},{7,6},{8,9},{9,8},{10,11... | collective-permute-start | bytes 405512 | tf_op jit(solution)/shard_map/ppermute | solution.py:400
  22.3 4.4 %copy-start.7 = (bf16[528,128]{1,0:T(8,128)(2,1)}, bf16[528,128]{1,0:T(8,128)(2,1)S(1)}, u32[]{:S(2)}) copy-start(bf16[528,128]{1,0:T(8,128)(2,1)S(1)} %collective-permute-done.9.refs_10_) | copy-start | bytes 405508
  22.3 3.4 %collective-permute-start.11 = (bf16[528,128]{1,0:T(8,128)(2,1)S(1)}, bf16[528,128]{1,0:T(8,128)(2,1)S(1)}, u32[]{:S(2)}, u32[]{:S(2)}) collective-permute-start(bf16[528,128]{1,0:T(8,128)(2,1)S(1)} %collective-permute-done.3.refs_4_), channel_id=1, source_target_pairs={{0,1},{1,0},{2,3},{3,2},{4,5},{5,4},{6,7},{7,6},{8,9},{9,8},{10,11... | collective-permute-start | bytes 405512 | tf_op jit(solution)/shard_map/ppermute | solution.py:400
  25.1 1.6 %copy-start.8 = (bf16[528,128]{1,0:T(8,128)(2,1)}, bf16[528,128]{1,0:T(8,128)(2,1)S(1)}, u32[]{:S(2)}) copy-start(bf16[528,128]{1,0:T(8,128)(2,1)S(1)} %collective-permute-done.4.refs_5_) | copy-start | bytes 405508
  25.1 1.4 %collective-permute-start.12 = (bf16[528,128]{1,0:T(8,128)(2,1)S(1)}, bf16[528,128]{1,0:T(8,128)(2,1)S(1)}, u32[]{:S(2)}, u32[]{:S(2)}) collective-permute-start(bf16[528,128]{1,0:T(8,128)(2,1)S(1)} %collective-permute-done.4.refs_5_), channel_id=1, source_target_pairs={{0,1},{1,0},{2,3},{3,2},{4,5},{5,4},{6,7},{7,6},{8,9},{9,8},{10,11... | collective-permute-start | bytes 405512 | tf_op jit(solution)/shard_map/ppermute | solution.py:400
  25.1 1.6 %copy-start.9 = (bf16[528,128]{1,0:T(8,128)(2,1)}, bf16[528,128]{1,0:T(8,128)(2,1)S(1)}, u32[]{:S(2)}) copy-start(bf16[528,128]{1,0:T(8,128)(2,1)S(1)} %collective-permute-done.6.refs_7_) | copy-start | bytes 405508
  25.1 1.5 %collective-permute-start.14 = (bf16[528,128]{1,0:T(8,128)(2,1)S(1)}, bf16[528,128]{1,0:T(8,128)(2,1)S(1)}, u32[]{:S(2)}, u32[]{:S(2)}) collective-permute-start(bf16[528,128]{1,0:T(8,128)(2,1)S(1)} %collective-permute-done.6.refs_7_), channel_id=1, source_target_pairs={{0,1},{1,0},{2,3},{3,2},{4,5},{5,4},{6,7},{7,6},{8,9},{9,8},{10,11... | collective-permute-start | bytes 405512 | tf_op jit(solution)/shard_map/ppermute | solution.py:400
  25.6 1.1 %copy-start.10 = (bf16[528,128]{1,0:T(8,128)(2,1)}, bf16[528,128]{1,0:T(8,128)(2,1)S(1)}, u32[]{:S(2)}) copy-start(bf16[528,128]{1,0:T(8,128)(2,1)S(1)} %collective-permute-done.8.refs_9_) | copy-start | bytes 405508
  25.6 1.1 %copy-start.11 = (bf16[528,128]{1,0:T(8,128)(2,1)}, bf16[528,128]{1,0:T(8,128)(2,1)S(1)}, u32[]{:S(2)}) copy-start(bf16[528,128]{1,0:T(8,128)(2,1)S(1)} %collective-permute-done.13.refs_14_) | copy-start | bytes 405508
  25.7 1.1 %copy-start.12 = (bf16[528,128]{1,0:T(8,128)(2,1)}, bf16[528,128]{1,0:T(8,128)(2,1)S(1)}, u32[]{:S(2)}) copy-start(bf16[528,128]{1,0:T(8,128)(2,1)S(1)} %collective-permute-done.11.refs_12_) | copy-start | bytes 405508
  26.5 0.6 %copy-start.13 = (bf16[528,128]{1,0:T(8,128)(2,1)}, bf16[528,128]{1,0:T(8,128)(2,1)S(1)}, u32[]{:S(2)}) copy-start(bf16[528,128]{1,0:T(8,128)(2,1)S(1)} %collective-permute-done.12.refs_13_) | copy-start | bytes 405508
  27.1 0.7 %copy-start.14 = (bf16[528,128]{1,0:T(8,128)(2,1)}, bf16[528,128]{1,0:T(8,128)(2,1)S(1)}, u32[]{:S(2)}) copy-start(bf16[528,128]{1,0:T(8,128)(2,1)S(1)} %collective-permute-done.14.refs_15_) | copy-start | bytes 405508

commit v2 on v1

--- a/solution.py
+++ b/solution.py
@@ -213,8 +213,8 @@
 def core_kernel(counts, tokens, width, *refs):
     blocks = refs[: len(counts)]
     out_ref, dq_ref, dk_ref, dv_ref, gate_ref = refs[len(counts) : len(counts) + 5]
-    (qs, ks, vs, gs, cums, key_row, scores, top_col, inv_col, delta_col, outs, points,
-     point_rows) = refs[len(counts) + 5 :]
+    (qs, ks, vs, gs, cums, key_row, scores, dprobs, probs, own_scores, own_dprobs, top_col, inv_col,
+     delta_col, outs, points, point_rows) = refs[len(counts) + 5 :]
     seg = tokens // 2
     total = qs.shape[0]
     segments = total // seg
@@ -251,50 +251,110 @@
         key_row[:, tile * tokens : (tile + 1) * tokens] = jnp.where(left, even, odd)
 
     points[...] = jnp.zeros_like(points)
-    block_rows = ROWS
-    row_in = lax.broadcasted_iota(jnp.int32, (block_rows, block_rows), 0)
-    col_in = lax.broadcasted_iota(jnp.int32, (block_rows, block_rows), 1)
+    own = blocks[0]
+    starts = [pl.multiple_of(p * seg, seg) for p in own_place]
+    own_q = own[0:tokens, :]
+    own_k = own[tokens : 2 * tokens, :]
+    own_v = own[2 * tokens : 3 * tokens, :]
+    own_g = own[3 * tokens : 4 * tokens, :]
+    key_lines = [cums[pl.ds(p, 1), :] for p in own_place]
+    own_key = jnp.where(left, key_lines[0], pltpu.roll(key_lines[1], seg, 1))
+    col_pos = jnp.where(left, starts[0] + lane1, starts[1] + lane1 - seg)
+    inner = lax.broadcasted_iota(jnp.int32, (tokens, 1), 0)
+    row_pos = jnp.where(inner < seg, starts[0] + inner, starts[1] + inner - seg)
+    dk_ref[...] = jnp.zeros_like(dk_ref)
+    dv_ref[...] = jnp.zeros_like(dv_ref)
+
+    size_r = ROWS
+    blocks_r = total // size_r
+    row_in = lax.broadcasted_iota(jnp.int32, (size_r, size_r), 0)
+    col_in = lax.broadcasted_iota(jnp.int32, (size_r, size_r), 1)
     causal = col_in <= row_in
-    for block in range(total // block_rows):
-        r0 = block * block_rows
-        q = qs[r0 : r0 + block_rows, :]
-        g = gs[r0 : r0 + block_rows, :]
-        best = None
-        for tile in range(block + 1):
-            c0 = tile * block_rows
-            s = contract_last(q, ks[c0 : c0 + block_rows, :]) * (scale * LOG2E)
-            s = s - key_row[:, c0 : c0 + block_rows]
-            if tile == block:
-                s = jnp.where(causal, s, masked_value)
-            scores[:, c0 : c0 + block_rows] = s
-            part = jnp.maximum(s[:, :128], s[:, 128:])
-            best = part if best is None else jnp.maximum(best, part)
-        top = jnp.max(best, axis=1, keepdims=True)
+    factor = scale * LOG2E
+    best = {}
+
+    def rows_of(ref, block):
+        return ref[block * size_r : (block + 1) * size_r, :]
+
+    def score_tile(block, tile):
+        c0 = tile * size_r
+        s = contract_last(rows_of(qs, block), ks[c0 : c0 + size_r, :]) * factor
+        s = s - key_row[:, c0 : c0 + size_r]
+        if tile == block:
+            s = jnp.where(causal, s, masked_value)
+        scores[block % 2, :, c0 : c0 + size_r] = s
+        part = s[:, :width]
+        for at in range(width, size_r, width):
+            part = jnp.maximum(part, s[:, at : at + width])
+        best[block] = jnp.maximum(best[block], part) if block in best else part
+
+    def own_row_tile(tile):
+        c0 = tile * size_r
+        s = contract_last(own_q, ks[c0 : c0 + size_r, :]) * factor - key_row[:, c0 : c0 + size_r]
+        seen = lax.broadcasted_iota(jnp.int32, (tokens, size_r), 1) + c0 <= row_pos
+        own_scores[:, c0 : c0 + size_r] = jnp.where(seen, s, masked_value)
+        own_dprobs[:, c0 : c0 + size_r] = contract_last(own_g, vs[c0 : c0 + size_r, :])
+
+    def exp_block(block):
+        top = jnp.broadcast_to(jnp.max(best[block], axis=1, keepdims=True), (size_r, width))
+        rows_of_top = top
+        top_col[block * size_r : (block + 1) * size_r, :] = rows_of_top
         mass = None
         for tile in range(block + 1):
-            c0 = tile * block_rows
-            e = jnp.exp2(scores[:, c0 : c0 + block_rows] - top)
-            scores[:, c0 : c0 + block_rows] = e
-            part = e[:, :128] + e[:, 128:]
-            mass = part if mass is None else mass + part
-        inv = 1.0 / jnp.sum(mass, axis=1, keepdims=True)
-        acc = jnp.zeros((block_rows, width), jnp.float32)
+            c0 = tile * size_r
+            dprobs[block % 2, :, c0 : c0 + size_r] = contract_last(
+                rows_of(gs, block), vs[c0 : c0 + size_r, :]
+            )
+            for at in range(c0, c0 + size_r, width):
+                e = jnp.exp2(scores[block % 2, :, at : at + width] - top)
+                scores[block % 2, :, at : at + width] = e
+                mass = e if mass is None else mass + e
+        inv = jnp.broadcast_to(1.0 / jnp.sum(mass, axis=1, keepdims=True), (size_r, width))
+        inv_col[block * size_r : (block + 1) * size_r, :] = inv
+
+    for tile in range(1):
+        score_tile(0, tile)
+    exp_block(0)
+    for block in range(blocks_r):
+        r0 = block * size_r
+        wide = r0 + size_r
+        inv = rows_of(inv_col, block)
         for tile in range(block + 1):
-            c0 = tile * block_rows
-            p = (scores[:, c0 : c0 + block_rows] * inv).astype(jnp.bfloat16)
-            acc = acc + jnp.dot(p, vs[c0 : c0 + block_rows, :], preferred_element_type=jnp.float32)
-        delta = jnp.sum(g.astype(jnp.float32) * acc, axis=1, keepdims=True)
-        outs[r0 : r0 + block_rows, :] = acc
-        top_col[r0 : r0 + block_rows, :] = top
-        inv_col[r0 : r0 + block_rows, :] = inv
-        delta_col[r0 : r0 + block_rows, :] = delta
+            c0 = tile * size_r
+            for at in range(c0, c0 + size_r, width):
+                p = scores[block % 2, :, at : at + width] * inv
+                scores[block % 2, :, at : at + width] = p
+                probs[:, at : at + width] = p.astype(jnp.bfloat16)
+            if block + 1 < blocks_r:
+                score_tile(block + 1, tile)
+        if block + 1 < blocks_r:
+            score_tile(block + 1, block + 1)
+        acc = jnp.dot(probs[:, :wide], vs[:wide, :], preferred_element_type=jnp.float32)
+        outs[r0:wide, :] = acc
+        own_row_tile(block)
+        if block + 1 < blocks_r:
+            exp_block(block + 1)
+        g = rows_of(gs, block)
+        delta = jnp.broadcast_to(
+            jnp.sum(g.astype(jnp.float32) * acc, axis=1, keepdims=True), (size_r, width)
+        )
+        delta_col[r0:wide, :] = delta
+
+        s = contract_last(rows_of(qs, block), own_k) * factor - own_key
+        seen = lax.broadcasted_iota(jnp.int32, (size_r, tokens), 0) + r0 >= col_pos
+        p = jnp.where(seen, jnp.exp2(s - rows_of(top_col, block)), 0.0) * inv
+        ds = p * (contract_last(g, own_v) - delta)
+        dv_ref[...] += contract_first(p.astype(jnp.bfloat16), g)
+        dk_ref[...] += contract_first(ds.astype(jnp.bfloat16), rows_of(qs, block))
+
         for tile in range(block + 1):
-            c0 = tile * block_rows
-            dp = contract_last(g, vs[c0 : c0 + block_rows, :])
-            ds = (scores[:, c0 : c0 + block_rows] * inv) * (dp - delta)
-            points[:, c0 : c0 + block_rows] += jnp.sum(
-                ds.reshape(block_rows // 8, 8, block_rows), axis=0
-            )
+            c0 = tile * size_r
+            for at in range(c0, c0 + size_r, width):
+                ds = scores[block % 2, :, at : at + width] * (
+                    dprobs[block % 2, :, at : at + width] - delta
+                )
+                points[:, at : at + width] += jnp.sum(ds.reshape(size_r // 8, 8, width), axis=0)
+    dk_ref[...] = dk_ref[...] * scale
 
     for tile in range(segments // 2):
         c0 = tile * tokens
@@ -311,48 +371,16 @@
         halves.append(jnp.where(own_place[half] % 2 == half, line, turned))
     gate_ref[...] = jnp.where(left, halves[0], halves[1])
 
-    own = blocks[0]
-    starts = [pl.multiple_of(p * seg, seg) for p in own_place]
-
     def pick(ref):
         return jnp.concatenate([ref[pl.ds(s, seg), :] for s in starts], axis=0)
 
     top, inv, delta = pick(top_col), pick(inv_col), pick(delta_col)
     out_ref[...] = pick(outs).astype(jnp.bfloat16)
-    inner = lax.broadcasted_iota(jnp.int32, (tokens, 1), 0)
-    row_pos = jnp.where(inner < seg, starts[0] + inner, starts[1] + inner - seg)
-    chunk = 512
-    q = own[0:tokens, :]
-    k = own[tokens : 2 * tokens, :]
-    v = own[2 * tokens : 3 * tokens, :]
-    g = own[3 * tokens : 4 * tokens, :]
-    acc = jnp.zeros((tokens, width), jnp.float32)
-    for c0 in range(0, total, chunk):
-        keys = ks[c0 : c0 + chunk, :]
-        s = contract_last(q, keys) * (scale * LOG2E) - key_row[:, c0 : c0 + chunk]
-        seen = lax.broadcasted_iota(jnp.int32, (tokens, chunk), 1) + c0 <= row_pos
-        p = jnp.where(seen, jnp.exp2(s - top), 0.0) * inv
-        ds = p * (contract_last(g, vs[c0 : c0 + chunk, :]) - delta)
-        acc = acc + jnp.dot(ds.astype(jnp.bfloat16), keys, preferred_element_type=jnp.float32)
-    dq_ref[...] = acc * scale
-
-    rows = [cums[pl.ds(p, 1), :] for p in own_place]
-    own_key = jnp.where(left, rows[0], pltpu.roll(rows[1], seg, 1))
-    col_pos = jnp.where(left, starts[0] + lane1, starts[1] + lane1 - seg)
-    acc_k = jnp.zeros((tokens, width), jnp.float32)
-    acc_v = jnp.zeros((tokens, width), jnp.float32)
-    for r0 in range(0, total, chunk):
-        queries = qs[r0 : r0 + chunk, :]
-        grads = gs[r0 : r0 + chunk, :]
-        s = contract_last(queries, k) * (scale * LOG2E) - own_key
-        seen = lax.broadcasted_iota(jnp.int32, (chunk, tokens), 0) + r0 >= col_pos
-        p = jnp.where(seen, jnp.exp2(s - top_col[r0 : r0 + chunk, :]), 0.0)
-        p = p * inv_col[r0 : r0 + chunk, :]
-        ds = p * (contract_last(grads, v) - delta_col[r0 : r0 + chunk, :])
-        acc_v = acc_v + contract_first(p.astype(jnp.bfloat16), grads)
-        acc_k = acc_k + contract_first(ds.astype(jnp.bfloat16), queries)
-    dk_ref[...] = acc_k * scale
-    dv_ref[...] = acc_v
+    for at in range(0, total, width):
+        p = jnp.exp2(own_scores[:, at : at + width] - top) * inv
+        ds = p * (own_dprobs[:, at : at + width] - delta)
+        probs[0:tokens, at : at + width] = ds.astype(jnp.bfloat16)
+    dq_ref[...] = jnp.dot(probs[0:tokens, :], ks[...], preferred_element_type=jnp.float32) * scale
 
 
 def core_call(blocks, tokens, width, devices):
@@ -379,14 +407,19 @@
         + [
             pltpu.VMEM((segments, tokens), jnp.float32),
             pltpu.VMEM((1, total), jnp.float32),
-            pltpu.VMEM((ROWS, total), jnp.float32),
-            pltpu.VMEM((total, 1), jnp.float32),
-            pltpu.VMEM((total, 1), jnp.float32),
-            pltpu.VMEM((total, 1), jnp.float32),
+            pltpu.VMEM((2, ROWS, total), jnp.float32),
+            pltpu.VMEM((2, ROWS, total), jnp.float32),
+            pltpu.VMEM((ROWS, total), jnp.bfloat16),
+            pltpu.VMEM((tokens, total), jnp.float32),
+            pltpu.VMEM((tokens, total), jnp.float32),
+            pltpu.VMEM((total, width), jnp.float32),
+            pltpu.VMEM((total, width), jnp.float32),
+            pltpu.VMEM((total, width), jnp.float32),
             pltpu.VMEM((total, width), jnp.float32),
             pltpu.VMEM((8, total), jnp.float32),
             pltpu.VMEM((segments // 2, tokens), jnp.float32),
         ],
+        compiler_params=pltpu.CompilerParams(vmem_limit_bytes=32 * 2**20),
         name="core",
     )(*blocks)
 

time: 41.1 us -> 38.6 us (0.939)
  Pallas kernels: 14.7 us -> 12.5 us
    pallas_call x1, Pallas kernels: 13.1 us -> 10.9 us  [core_call(): pl.pallas_call(functools.partial(core_kernel, counts, tokens, width), out...]
    unnamed x30 -> x2, local copies, waits for them, and re-layouts: 1.05 us -> 0.91 us
where the time goes in v2:
time: 38.6 us; the launch traced here: 38.4 us
  starting transfers between devices  15.9 us (41%)
  Pallas kernels  12.5 us (32%)
  waiting for transfers between devices  8.53 us (22%)
  local copies, waits for them, and re-layouts  0.91 us (2%)
  between operations  0.65 us (2%)
    ppermute x15, starting transfers between devices, shift(): return lax.ppermute(x, 'seq', pairs)  15.9 us
    pallas_call x1, Pallas kernels, core_call(): pl.pallas_call(functools.partial(core_kernel, counts, tokens, width), out...  10.9 us
    ppermute x15, waiting for transfers between devices, shift(): return lax.ppermute(x, 'seq', pairs)  8.53 us
    pallas_call x1, Pallas kernels, local_small(): pl.pallas_call(pack_kernel, out_shape=jax.ShapeDtypeStruct((4 * tokens +...  1.55 us
    unnamed x2, local copies, waits for them, and re-layouts  0.91 us
  transfers between devices with their start and end apart: 15, of which 6 were waited for; matrix products, arithmetic and copies ran while one was open for 0% of the time, Pallas kernels for 0%

profile of v2, /device:TPU:0, one launch (start us, length us, event | category | flops | bytes accessed | tf_op | source)
XLA Modules:
  0.0 38.4 jit_solution(7079012163325155949)
XLA Ops:
  0.6 1.5 %pack.1.refs_0_ = bf16[528,128]{1,0:T(8,128)(2,1)} custom-call(bf16[128,128]{1,0:T(8,128)(2,1)} %q_ref.1, bf16[128,128]{1,0:T(8,128)(2,1)} %k_ref.1, bf16[128,128]{1,0:T(8,128)(2,1)} %v_ref.1, bf16[128,128]{1,0:T(8,128)(2,1)} %g_ref.1, f32[1,128]{1,0:T(1,128)} %bitcast.3, s32[1,2]{1,0:T(1,128)} %bitcast.4), custom_call_target="tpu_custom_call" | custom-call | tf_op jit(solution)/shard_map/pack/pallas_call | solution.py:452
  2.2 5.1 %collective-permute-start.2 = (bf16[528,128]{1,0:T(8,128)(2,1)}, bf16[528,128]{1,0:T(8,128)(2,1)S(1)}, u32[]{:S(2)}, u32[]{:S(2)}) collective-permute-start(bf16[528,128]{1,0:T(8,128)(2,1)} %pack.1.refs_0_), channel_id=1, source_target_pairs={{0,12},{1,13},{2,14},{3,15},{4,0},{5,1},{6,2},{7,3},{8,4},{9,5},{1... | collective-permute-start | bytes 405512 | tf_op jit(solution)/shard_map/ppermute | solution.py:433
  7.3 0.0 collective-permute-start.7
  7.3 0.0 collective-permute-start.1
  7.3 1.5 %collective-permute-start = (bf16[528,128]{1,0:T(8,128)(2,1)}, bf16[528,128]{1,0:T(8,128)(2,1)S(1)}, u32[]{:S(2)}, u32[]{:S(2)}) collective-permute-start(bf16[528,128]{1,0:T(8,128)(2,1)} %pack.1.refs_0_), channel_id=1, source_target_pairs={{0,2},{1,3},{2,0},{3,1},{4,6},{5,7},{6,4},{7,5},{8,10},{9,11},{10,... | collective-permute-start | bytes 405512 | tf_op jit(solution)/shard_map/ppermute | solution.py:433
  8.8 2.8 %collective-permute-done.2.refs_3_ = bf16[528,128]{1,0:T(8,128)(2,1)S(1)} collective-permute-done((bf16[528,128]{1,0:T(8,128)(2,1)}, bf16[528,128]{1,0:T(8,128)(2,1)S(1)}, u32[]{:S(2)}, u32[]{:S(2)}) %collective-permute-start.2) | collective-permute-done | bytes 135200 | tf_op jit(solution)/shard_map/ppermute | solution.py:433
  11.6 4.2 %collective-permute-start.5 = (bf16[528,128]{1,0:T(8,128)(2,1)S(1)}, bf16[528,128]{1,0:T(8,128)(2,1)S(1)}, u32[]{:S(2)}, u32[]{:S(2)}) collective-permute-start(bf16[528,128]{1,0:T(8,128)(2,1)S(1)} %collective-permute-done.2.refs_3_), channel_id=1, source_target_pairs={{0,12},{1,13},{2,14},{3,15},{4,0},{5,1},{6,2},{7,3},{8,4},{9,5},{1... | collective-permute-start | bytes 405512 | tf_op jit(solution)/shard_map/ppermute | solution.py:433
  15.7 0.0 collective-permute-start.10
  15.7 0.0 collective-permute-done.7.refs_8_
  15.7 1.5 %collective-permute-start.3 = (bf16[528,128]{1,0:T(8,128)(2,1)S(1)}, bf16[528,128]{1,0:T(8,128)(2,1)S(1)}, u32[]{:S(2)}, u32[]{:S(2)}) collective-permute-start(bf16[528,128]{1,0:T(8,128)(2,1)S(1)} %collective-permute-done.2.refs_3_), channel_id=1, source_target_pairs={{0,2},{1,3},{2,0},{3,1},{4,6},{5,7},{6,4},{7,5},{8,10},{9,11},{10,... | collective-permute-start | bytes 405512 | tf_op jit(solution)/shard_map/ppermute | solution.py:433
  17.2 0.0 collective-permute-done.1.refs_2_
  17.2 0.2 collective-permute-start.9
  17.5 0.0 collective-permute-done.refs_1_
  17.5 0.0 collective-permute-start.4
  17.5 1.0 %collective-permute-done.5.refs_6_ = bf16[528,128]{1,0:T(8,128)(2,1)S(1)} collective-permute-done((bf16[528,128]{1,0:T(8,128)(2,1)S(1)}, bf16[528,128]{1,0:T(8,128)(2,1)S(1)}, u32[]{:S(2)}, u32[]{:S(2)}) %collective-permute-start.5) | collective-permute-done | bytes 135200 | tf_op jit(solution)/shard_map/ppermute | solution.py:433
  18.5 2.4 %collective-permute-start.6 = (bf16[528,128]{1,0:T(8,128)(2,1)S(1)}, bf16[528,128]{1,0:T(8,128)(2,1)S(1)}, u32[]{:S(2)}, u32[]{:S(2)}) collective-permute-start(bf16[528,128]{1,0:T(8,128)(2,1)S(1)} %collective-permute-done.5.refs_6_), channel_id=1, source_target_pairs={{0,2},{1,3},{2,0},{3,1},{4,6},{5,7},{6,4},{7,5},{8,10},{9,11},{10,... | collective-permute-start | bytes 405512 | tf_op jit(solution)/shard_map/ppermute | solution.py:433
  20.8 0.0 collective-permute-done.10.refs_11_
  20.8 0.0 collective-permute-start.8
  20.8 1.4 %collective-permute-done.3.refs_4_ = bf16[528,128]{1,0:T(8,128)(2,1)S(1)} collective-permute-done((bf16[528,128]{1,0:T(8,128)(2,1)S(1)}, bf16[528,128]{1,0:T(8,128)(2,1)S(1)}, u32[]{:S(2)}, u32[]{:S(2)}) %collective-permute-start.3) | collective-permute-done | bytes 135200 | tf_op jit(solution)/shard_map/ppermute | solution.py:433
  22.2 0.0 collective-permute-start.13
  22.2 0.0 collective-permute-done.9.refs_10_
  22.2 0.5 %collective-permute-start.11 = (bf16[528,128]{1,0:T(8,128)(2,1)S(1)}, bf16[528,128]{1,0:T(8,128)(2,1)S(1)}, u32[]{:S(2)}, u32[]{:S(2)}) collective-permute-start(bf16[528,128]{1,0:T(8,128)(2,1)S(1)} %collective-permute-done.3.refs_4_), channel_id=1, source_target_pairs={{0,1},{1,0},{2,3},{3,2},{4,5},{5,4},{6,7},{7,6},{8,9},{9,8},{10,11... | collective-permute-start | bytes 405512 | tf_op jit(solution)/shard_map/ppermute | solution.py:433
  22.7 2.3 %collective-permute-done.4.refs_5_ = bf16[528,128]{1,0:T(8,128)(2,1)S(1)} collective-permute-done((bf16[528,128]{1,0:T(8,128)(2,1)S(1)}, bf16[528,128]{1,0:T(8,128)(2,1)S(1)}, u32[]{:S(2)}, u32[]{:S(2)}) %collective-permute-start.4) | collective-permute-done | bytes 135200 | tf_op jit(solution)/shard_map/ppermute | solution.py:433
  25.0 0.0 collective-permute-start.12
  25.0 0.0 collective-permute-done.6.refs_7_
  25.0 0.5 %collective-permute-start.14 = (bf16[528,128]{1,0:T(8,128)(2,1)S(1)}, bf16[528,128]{1,0:T(8,128)(2,1)S(1)}, u32[]{:S(2)}, u32[]{:S(2)}) collective-permute-start(bf16[528,128]{1,0:T(8,128)(2,1)S(1)} %collective-permute-done.6.refs_7_), channel_id=1, source_target_pairs={{0,1},{1,0},{2,3},{3,2},{4,5},{5,4},{6,7},{7,6},{8,9},{9,8},{10,11... | collective-permute-start | bytes 405512 | tf_op jit(solution)/shard_map/ppermute | solution.py:433
  25.5 0.0 collective-permute-done.8.refs_9_
  25.6 0.0 collective-permute-done.13.refs_14_
  25.6 0.0 collective-permute-done.11.refs_12_
  25.6 0.8 %collective-permute-done.12.refs_13_ = bf16[528,128]{1,0:T(8,128)(2,1)S(1)} collective-permute-done((bf16[528,128]{1,0:T(8,128)(2,1)S(1)}, bf16[528,128]{1,0:T(8,128)(2,1)S(1)}, u32[]{:S(2)}, u32[]{:S(2)}) %collective-permute-start.12) | collective-permute-done | bytes 135200 | tf_op jit(solution)/shard_map/ppermute | solution.py:433
  26.4 0.2 collective-permute-done.14.refs_15_
  26.6 0.0 copy-start
  26.6 0.9 %copy-done = bf16[528,128]{1,0:T(8,128)(2,1)S(1)} copy-done((bf16[528,128]{1,0:T(8,128)(2,1)S(1)}, bf16[528,128]{1,0:T(8,128)(2,1)}, u32[]{:S(2)}) %copy-start) | copy-done | bytes 135192
  27.5 10.9 %core.1 = (bf16[128,128]{1,0:T(8,128)(2,1)}, f32[128,128]{1,0:T(8,128)}, f32[128,128]{1,0:T(8,128)}, f32[128,128]{1,0:T(8,128)}, f32[1,128]{1,0:T(1,128)}) custom-call(bf16[528,128]{1,0:T(8,128)(2,1)S(1)} %copy-done, bf16[528,128]{1,0:T(8,128)(2,1)S(1)} %collective-permute-done.refs_1_, bf16[528,128]{1,0:T(8,128)(2,1)S(1)} %collective-permute-done.1.refs_2_, ...), custom_call_target="tpu_custom_call" | custom-call | tf_op jit(solution)/shard_map/core/pallas_call | solution.py:395
Async XLA Ops:
  2.2 9.4 %collective-permute-start.2 = (bf16[528,128]{1,0:T(8,128)(2,1)}, bf16[528,128]{1,0:T(8,128)(2,1)S(1)}, u32[]{:S(2)}, u32[]{:S(2)}) collective-permute-start(bf16[528,128]{1,0:T(8,128)(2,1)} %pack.1.refs_0_), channel_id=1, source_target_pairs={{0,12},{1,13},{2,14},{3,15},{4,0},{5,1},{6,2},{7,3},{8,4},{9,5},{1... | collective-permute-start | bytes 405512 | tf_op jit(solution)/shard_map/ppermute | solution.py:433
  7.3 8.5 %collective-permute-start.7 = (bf16[528,128]{1,0:T(8,128)(2,1)}, bf16[528,128]{1,0:T(8,128)(2,1)S(1)}, u32[]{:S(2)}, u32[]{:S(2)}) collective-permute-start(bf16[528,128]{1,0:T(8,128)(2,1)} %pack.1.refs_0_), channel_id=1, source_target_pairs={{0,1},{1,0},{2,3},{3,2},{4,5},{5,4},{6,7},{7,6},{8,9},{9,8},{10,11... | collective-permute-start | bytes 405512 | tf_op jit(solution)/shard_map/ppermute | solution.py:433
  7.3 10.0 %collective-permute-start.1 = (bf16[528,128]{1,0:T(8,128)(2,1)}, bf16[528,128]{1,0:T(8,128)(2,1)S(1)}, u32[]{:S(2)}, u32[]{:S(2)}) collective-permute-start(bf16[528,128]{1,0:T(8,128)(2,1)} %pack.1.refs_0_), channel_id=1, source_target_pairs={{0,4},{1,5},{2,6},{3,7},{4,8},{5,9},{6,10},{7,11},{8,12},{9,13},{1... | collective-permute-start | bytes 405512 | tf_op jit(solution)/shard_map/ppermute | solution.py:433
  7.3 10.2 %collective-permute-start = (bf16[528,128]{1,0:T(8,128)(2,1)}, bf16[528,128]{1,0:T(8,128)(2,1)S(1)}, u32[]{:S(2)}, u32[]{:S(2)}) collective-permute-start(bf16[528,128]{1,0:T(8,128)(2,1)} %pack.1.refs_0_), channel_id=1, source_target_pairs={{0,2},{1,3},{2,0},{3,1},{4,6},{5,7},{6,4},{7,5},{8,10},{9,11},{10,... | collective-permute-start | bytes 405512 | tf_op jit(solution)/shard_map/ppermute | solution.py:433
  11.6 6.9 %collective-permute-start.5 = (bf16[528,128]{1,0:T(8,128)(2,1)S(1)}, bf16[528,128]{1,0:T(8,128)(2,1)S(1)}, u32[]{:S(2)}, u32[]{:S(2)}) collective-permute-start(bf16[528,128]{1,0:T(8,128)(2,1)S(1)} %collective-permute-done.2.refs_3_), channel_id=1, source_target_pairs={{0,12},{1,13},{2,14},{3,15},{4,0},{5,1},{6,2},{7,3},{8,4},{9,5},{1... | collective-permute-start | bytes 405512 | tf_op jit(solution)/shard_map/ppermute | solution.py:433
  15.7 5.1 %collective-permute-start.10 = (bf16[528,128]{1,0:T(8,128)(2,1)S(1)}, bf16[528,128]{1,0:T(8,128)(2,1)S(1)}, u32[]{:S(2)}, u32[]{:S(2)}) collective-permute-start(bf16[528,128]{1,0:T(8,128)(2,1)S(1)} %collective-permute-done.2.refs_3_), channel_id=1, source_target_pairs={{0,1},{1,0},{2,3},{3,2},{4,5},{5,4},{6,7},{7,6},{8,9},{9,8},{10,11... | collective-permute-start | bytes 405512 | tf_op jit(solution)/shard_map/ppermute | solution.py:433
  15.7 6.5 %collective-permute-start.3 = (bf16[528,128]{1,0:T(8,128)(2,1)S(1)}, bf16[528,128]{1,0:T(8,128)(2,1)S(1)}, u32[]{:S(2)}, u32[]{:S(2)}) collective-permute-start(bf16[528,128]{1,0:T(8,128)(2,1)S(1)} %collective-permute-done.2.refs_3_), channel_id=1, source_target_pairs={{0,2},{1,3},{2,0},{3,1},{4,6},{5,7},{6,4},{7,5},{8,10},{9,11},{10,... | collective-permute-start | bytes 405512 | tf_op jit(solution)/shard_map/ppermute | solution.py:433
  17.2 5.0 %collective-permute-start.9 = (bf16[528,128]{1,0:T(8,128)(2,1)S(1)}, bf16[528,128]{1,0:T(8,128)(2,1)S(1)}, u32[]{:S(2)}, u32[]{:S(2)}) collective-permute-start(bf16[528,128]{1,0:T(8,128)(2,1)S(1)} %collective-permute-done.1.refs_2_), channel_id=1, source_target_pairs={{0,1},{1,0},{2,3},{3,2},{4,5},{5,4},{6,7},{7,6},{8,9},{9,8},{10,11... | collective-permute-start | bytes 405512 | tf_op jit(solution)/shard_map/ppermute | solution.py:433
  17.5 7.6 %collective-permute-start.4 = (bf16[528,128]{1,0:T(8,128)(2,1)S(1)}, bf16[528,128]{1,0:T(8,128)(2,1)S(1)}, u32[]{:S(2)}, u32[]{:S(2)}) collective-permute-start(bf16[528,128]{1,0:T(8,128)(2,1)S(1)} %collective-permute-done.refs_1_), channel_id=1, source_target_pairs={{0,4},{1,5},{2,6},{3,7},{4,8},{5,9},{6,10},{7,11},{8,12},{9,13},{1... | collective-permute-start | bytes 405512 | tf_op jit(solution)/shard_map/ppermute | solution.py:433
  18.5 6.6 %collective-permute-start.6 = (bf16[528,128]{1,0:T(8,128)(2,1)S(1)}, bf16[528,128]{1,0:T(8,128)(2,1)S(1)}, u32[]{:S(2)}, u32[]{:S(2)}) collective-permute-start(bf16[528,128]{1,0:T(8,128)(2,1)S(1)} %collective-permute-done.5.refs_6_), channel_id=1, source_target_pairs={{0,2},{1,3},{2,0},{3,1},{4,6},{5,7},{6,4},{7,5},{8,10},{9,11},{10,... | collective-permute-start | bytes 405512 | tf_op jit(solution)/shard_map/ppermute | solution.py:433
  20.8 4.7 %collective-permute-start.8 = (bf16[528,128]{1,0:T(8,128)(2,1)S(1)}, bf16[528,128]{1,0:T(8,128)(2,1)S(1)}, u32[]{:S(2)}, u32[]{:S(2)}) collective-permute-start(bf16[528,128]{1,0:T(8,128)(2,1)S(1)} %collective-permute-done.refs_1_), channel_id=1, source_target_pairs={{0,1},{1,0},{2,3},{3,2},{4,5},{5,4},{6,7},{7,6},{8,9},{9,8},{10,11... | collective-permute-start | bytes 405512 | tf_op jit(solution)/shard_map/ppermute | solution.py:433
  22.2 3.4 %collective-permute-start.13 = (bf16[528,128]{1,0:T(8,128)(2,1)S(1)}, bf16[528,128]{1,0:T(8,128)(2,1)S(1)}, u32[]{:S(2)}, u32[]{:S(2)}) collective-permute-start(bf16[528,128]{1,0:T(8,128)(2,1)S(1)} %collective-permute-done.5.refs_6_), channel_id=1, source_target_pairs={{0,1},{1,0},{2,3},{3,2},{4,5},{5,4},{6,7},{7,6},{8,9},{9,8},{10,11... | collective-permute-start | bytes 405512 | tf_op jit(solution)/shard_map/ppermute | solution.py:433
  22.2 3.4 %collective-permute-start.11 = (bf16[528,128]{1,0:T(8,128)(2,1)S(1)}, bf16[528,128]{1,0:T(8,128)(2,1)S(1)}, u32[]{:S(2)}, u32[]{:S(2)}) collective-permute-start(bf16[528,128]{1,0:T(8,128)(2,1)S(1)} %collective-permute-done.3.refs_4_), channel_id=1, source_target_pairs={{0,1},{1,0},{2,3},{3,2},{4,5},{5,4},{6,7},{7,6},{8,9},{9,8},{10,11... | collective-permute-start | bytes 405512 | tf_op jit(solution)/shard_map/ppermute | solution.py:433
  25.0 1.4 %collective-permute-start.12 = (bf16[528,128]{1,0:T(8,128)(2,1)S(1)}, bf16[528,128]{1,0:T(8,128)(2,1)S(1)}, u32[]{:S(2)}, u32[]{:S(2)}) collective-permute-start(bf16[528,128]{1,0:T(8,128)(2,1)S(1)} %collective-permute-done.4.refs_5_), channel_id=1, source_target_pairs={{0,1},{1,0},{2,3},{3,2},{4,5},{5,4},{6,7},{7,6},{8,9},{9,8},{10,11... | collective-permute-start | bytes 405512 | tf_op jit(solution)/shard_map/ppermute | solution.py:433
  25.0 1.5 %collective-permute-start.14 = (bf16[528,128]{1,0:T(8,128)(2,1)S(1)}, bf16[528,128]{1,0:T(8,128)(2,1)S(1)}, u32[]{:S(2)}, u32[]{:S(2)}) collective-permute-start(bf16[528,128]{1,0:T(8,128)(2,1)S(1)} %collective-permute-done.6.refs_7_), channel_id=1, source_target_pairs={{0,1},{1,0},{2,3},{3,2},{4,5},{5,4},{6,7},{7,6},{8,9},{9,8},{10,11... | collective-permute-start | bytes 405512 | tf_op jit(solution)/shard_map/ppermute | solution.py:433
  26.6 0.9 %copy-start = (bf16[528,128]{1,0:T(8,128)(2,1)S(1)}, bf16[528,128]{1,0:T(8,128)(2,1)}, u32[]{:S(2)}) copy-start(bf16[528,128]{1,0:T(8,128)(2,1)} %pack.1.refs_0_) | copy-start | bytes 405508

commit v3 on v2

--- a/solution.py
+++ b/solution.py
@@ -161,14 +161,25 @@
 LOG2E = 1.4426950408889634
 META = 16
 ROWS = 256
-
-
-def pack_kernel(q_ref, k_ref, v_ref, g_ref, gate_ref, order_ref, out_ref):
+COLS = 256
+
+
+def pack_kernel(q_ref, k_ref, v_ref, g_ref, gate_hbm, order_hbm, out_ref, gate_ref, order_ref, sems):
     tokens = q_ref.shape[0]
-    out_ref[0:tokens] = q_ref[...]
-    out_ref[tokens : 2 * tokens] = k_ref[...]
-    out_ref[2 * tokens : 3 * tokens] = v_ref[...]
-    out_ref[3 * tokens : 4 * tokens] = g_ref[...]
+    copies = [
+        pltpu.make_async_copy(gate_hbm, gate_ref, sems.at[0]),
+        pltpu.make_async_copy(order_hbm, order_ref, sems.at[1]),
+    ]
+    for index, ref in enumerate((q_ref, k_ref, v_ref, g_ref)):
+        copies.append(
+            pltpu.make_async_copy(
+                ref, out_ref.at[pl.ds(index * tokens, tokens), :], sems.at[index + 2]
+            )
+        )
+    for copy in copies:
+        copy.start()
+    copies[0].wait()
+    copies[1].wait()
     gate = gate_ref[...]
     high = gate.astype(jnp.bfloat16).astype(jnp.float32)
     rest = gate - high
@@ -182,6 +193,12 @@
         row == 0, high, jnp.where(row == 1, mid, jnp.where(row == 2, low, place))
     )
     out_ref[4 * tokens : 4 * tokens + META] = meta.astype(jnp.bfloat16)
+    for copy in copies[2:]:
+        copy.wait()
+
+
+def split(items, turn, turns):
+    return items[len(items) * turn // turns : len(items) * (turn + 1) // turns]
 
 
 def roll_sum_lanes(x, span, reverse):
@@ -213,8 +230,8 @@
 def core_kernel(counts, tokens, width, *refs):
     blocks = refs[: len(counts)]
     out_ref, dq_ref, dk_ref, dv_ref, gate_ref = refs[len(counts) : len(counts) + 5]
-    (qs, ks, vs, gs, cums, key_row, scores, dprobs, probs, own_scores, own_dprobs, top_col, inv_col,
-     delta_col, outs, points, point_rows) = refs[len(counts) + 5 :]
+    (qs, ks, vs, gs, cums, key_row, scores, probs, own_scores, own_dprobs, total_col, delta_col,
+     outs, points, point_rows) = refs[len(counts) + 5 :]
     seg = tokens // 2
     total = qs.shape[0]
     segments = total // seg
@@ -265,95 +282,122 @@
     dk_ref[...] = jnp.zeros_like(dk_ref)
     dv_ref[...] = jnp.zeros_like(dv_ref)
 
-    size_r = ROWS
+    size_r, size_c = ROWS, COLS
     blocks_r = total // size_r
-    row_in = lax.broadcasted_iota(jnp.int32, (size_r, size_r), 0)
-    col_in = lax.broadcasted_iota(jnp.int32, (size_r, size_r), 1)
-    causal = col_in <= row_in
+    row_in = lax.broadcasted_iota(jnp.int32, (size_r, size_c), 0)
+    col_in = lax.broadcasted_iota(jnp.int32, (size_r, size_c), 1)
+    causal = [col_in <= row_in + at for at in range(0, max(size_c, size_r), size_r)]
     factor = scale * LOG2E
     best = {}
+    slots = {}
 
     def rows_of(ref, block):
         return ref[block * size_r : (block + 1) * size_r, :]
 
+    def spread(column):
+        return jnp.broadcast_to(column, (column.shape[0], width))
+
+    def tiles_of(block):
+        return range(((block + 1) * size_r + size_c - 1) // size_c)
+
     def score_tile(block, tile):
-        c0 = tile * size_r
-        s = contract_last(rows_of(qs, block), ks[c0 : c0 + size_r, :]) * factor
-        s = s - key_row[:, c0 : c0 + size_r]
-        if tile == block:
-            s = jnp.where(causal, s, masked_value)
-        scores[block % 2, :, c0 : c0 + size_r] = s
+        c0 = tile * size_c
+        s = contract_last(rows_of(qs, block), ks[c0 : c0 + size_c, :]) * factor
+        s = s - key_row[:, c0 : c0 + size_c]
+        if c0 + size_c > block * size_r:
+            s = jnp.where(causal[block % len(causal)], s, masked_value)
+        scores[slots[block], :, c0 : c0 + size_c] = s
         part = s[:, :width]
-        for at in range(width, size_r, width):
+        for at in range(width, size_c, width):
             part = jnp.maximum(part, s[:, at : at + width])
         best[block] = jnp.maximum(best[block], part) if block in best else part
 
     def own_row_tile(tile):
-        c0 = tile * size_r
-        s = contract_last(own_q, ks[c0 : c0 + size_r, :]) * factor - key_row[:, c0 : c0 + size_r]
-        seen = lax.broadcasted_iota(jnp.int32, (tokens, size_r), 1) + c0 <= row_pos
-        own_scores[:, c0 : c0 + size_r] = jnp.where(seen, s, masked_value)
-        own_dprobs[:, c0 : c0 + size_r] = contract_last(own_g, vs[c0 : c0 + size_r, :])
-
-    def exp_block(block):
-        top = jnp.broadcast_to(jnp.max(best[block], axis=1, keepdims=True), (size_r, width))
-        rows_of_top = top
-        top_col[block * size_r : (block + 1) * size_r, :] = rows_of_top
+        c0 = tile * size_c
+        s = contract_last(own_q, ks[c0 : c0 + size_c, :]) * factor - key_row[:, c0 : c0 + size_c]
+        seen = lax.broadcasted_iota(jnp.int32, (tokens, size_c), 1) + c0 <= row_pos
+        own_scores[:, c0 : c0 + size_c] = jnp.where(seen, s, masked_value)
+        own_dprobs[:, c0 : c0 + size_c] = contract_last(own_g, vs[c0 : c0 + size_c, :])
+
+    def totals(block):
+        top = spread(jnp.max(best[block], axis=1, keepdims=True))
         mass = None
-        for tile in range(block + 1):
-            c0 = tile * size_r
-            dprobs[block % 2, :, c0 : c0 + size_r] = contract_last(
-                rows_of(gs, block), vs[c0 : c0 + size_r, :]
-            )
-            for at in range(c0, c0 + size_r, width):
-                e = jnp.exp2(scores[block % 2, :, at : at + width] - top)
-                scores[block % 2, :, at : at + width] = e
-                mass = e if mass is None else mass + e
-        inv = jnp.broadcast_to(1.0 / jnp.sum(mass, axis=1, keepdims=True), (size_r, width))
-        inv_col[block * size_r : (block + 1) * size_r, :] = inv
-
-    for tile in range(1):
-        score_tile(0, tile)
-    exp_block(0)
-    for block in range(blocks_r):
+        for at in range(0, len(tiles_of(block)) * size_c, width):
+            e = jnp.exp2(scores[slots[block], :, at : at + width] - top)
+            mass = e if mass is None else mass + e
+        total_col[block * size_r : (block + 1) * size_r, :] = top + spread(
+            jnp.log2(jnp.sum(mass, axis=1, keepdims=True))
+        )
+
+    def prob_tile(block, tile, low):
+        log_total = rows_of(total_col, block)
+        for at in range(tile * size_c, (tile + 1) * size_c, width):
+            p = jnp.exp2(scores[slots[block], :, at : at + width] - log_total)
+            probs[slots[block], :, at : at + width] = p
+            low.append(p.astype(jnp.bfloat16))
+
+    def outputs(block, low):
+        wide = len(tiles_of(block)) * size_c
+        acc = jnp.dot(
+            jnp.concatenate(low, axis=1), vs[:wide, :], preferred_element_type=jnp.float32
+        )
+        outs[block * size_r : (block + 1) * size_r, :] = acc
+        g = rows_of(gs, block).astype(jnp.float32)
+        delta_col[block * size_r : (block + 1) * size_r, :] = spread(
+            jnp.sum(g * acc, axis=1, keepdims=True)
+        )
+
+    def own_cols(block):
         r0 = block * size_r
-        wide = r0 + size_r
-        inv = rows_of(inv_col, block)
-        for tile in range(block + 1):
-            c0 = tile * size_r
-            for at in range(c0, c0 + size_r, width):
-                p = scores[block % 2, :, at : at + width] * inv
-                scores[block % 2, :, at : at + width] = p
-                probs[:, at : at + width] = p.astype(jnp.bfloat16)
-            if block + 1 < blocks_r:
-                score_tile(block + 1, tile)
-        if block + 1 < blocks_r:
-            score_tile(block + 1, block + 1)
-        acc = jnp.dot(probs[:, :wide], vs[:wide, :], preferred_element_type=jnp.float32)
-        outs[r0:wide, :] = acc
-        own_row_tile(block)
-        if block + 1 < blocks_r:
-            exp_block(block + 1)
         g = rows_of(gs, block)
-        delta = jnp.broadcast_to(
-            jnp.sum(g.astype(jnp.float32) * acc, axis=1, keepdims=True), (size_r, width)
-        )
-        delta_col[r0:wide, :] = delta
-
         s = contract_last(rows_of(qs, block), own_k) * factor - own_key
         seen = lax.broadcasted_iota(jnp.int32, (size_r, tokens), 0) + r0 >= col_pos
-        p = jnp.where(seen, jnp.exp2(s - rows_of(top_col, block)), 0.0) * inv
-        ds = p * (contract_last(g, own_v) - delta)
+        p = jnp.where(seen, jnp.exp2(s - rows_of(total_col, block)), 0.0)
+        ds = p * (contract_last(g, own_v) - rows_of(delta_col, block))
         dv_ref[...] += contract_first(p.astype(jnp.bfloat16), g)
         dk_ref[...] += contract_first(ds.astype(jnp.bfloat16), rows_of(qs, block))
 
-        for tile in range(block + 1):
-            c0 = tile * size_r
-            for at in range(c0, c0 + size_r, width):
-                ds = scores[block % 2, :, at : at + width] * (
-                    dprobs[block % 2, :, at : at + width] - delta
-                )
-                points[:, at : at + width] += jnp.sum(ds.reshape(size_r // 8, 8, width), axis=0)
+    def point_tile(block, tile):
+        c0 = tile * size_c
+        delta = rows_of(delta_col, block)
+        dp = contract_last(rows_of(gs, block), vs[c0 : c0 + size_c, :])
+        for at in range(0, size_c, width):
+            ds = probs[slots[block], :, c0 + at : c0 + at + width] * (dp[:, at : at + width] - delta)
+            points[:, c0 + at : c0 + at + width] += jnp.sum(
+                ds.reshape(size_r // 8, 8, width), axis=0
+            )
+
+    rest = list(range(1, blocks_r))
+    sequence = []
+    while rest:
+        sequence.append(rest.pop(0))
+        if rest:
+            sequence.append(rest.pop())
+    sequence.append(0)
+    slots.update({block: step % 2 for step, block in enumerate(sequence)})
+    first = sequence[0]
+    for tile in tiles_of(first):
+        score_tile(first, tile)
+    totals(first)
+    row_tiles = list(range(total // size_c))
+    for step, block in enumerate(sequence):
+        after = sequence[step + 1] if step + 1 < blocks_r else None
+        ahead = list(tiles_of(after)) if after is not None else []
+        here = list(tiles_of(block))
+        low = []
+        for turn in range(max(len(here), len(ahead))):
+            for tile in split(ahead, turn, max(len(here), len(ahead))):
+                score_tile(after, tile)
+            for tile in split(here, turn, max(len(here), len(ahead))):
+                prob_tile(block, tile, low)
+        outputs(block, low)
+        if after is not None:
+            totals(after)
+        if row_tiles and step % max(1, blocks_r // (total // size_c)) == 0:
+            own_row_tile(row_tiles.pop(0))
+        own_cols(block)
+        for tile in here:
+            point_tile(block, tile)
     dk_ref[...] = dk_ref[...] * scale
 
     for tile in range(segments // 2):
@@ -374,13 +418,16 @@
     def pick(ref):
         return jnp.concatenate([ref[pl.ds(s, seg), :] for s in starts], axis=0)
 
-    top, inv, delta = pick(top_col), pick(inv_col), pick(delta_col)
+    log_total, delta = pick(total_col), pick(delta_col)
     out_ref[...] = pick(outs).astype(jnp.bfloat16)
+    low = []
     for at in range(0, total, width):
-        p = jnp.exp2(own_scores[:, at : at + width] - top) * inv
+        p = jnp.exp2(own_scores[:, at : at + width] - log_total)
         ds = p * (own_dprobs[:, at : at + width] - delta)
-        probs[0:tokens, at : at + width] = ds.astype(jnp.bfloat16)
-    dq_ref[...] = jnp.dot(probs[0:tokens, :], ks[...], preferred_element_type=jnp.float32) * scale
+        low.append(ds.astype(jnp.bfloat16))
+    dq_ref[...] = scale * jnp.dot(
+        jnp.concatenate(low, axis=1), ks[...], preferred_element_type=jnp.float32
+    )
 
 
 def core_call(blocks, tokens, width, devices):
@@ -409,17 +456,15 @@
             pltpu.VMEM((1, total), jnp.float32),
             pltpu.VMEM((2, ROWS, total), jnp.float32),
             pltpu.VMEM((2, ROWS, total), jnp.float32),
-            pltpu.VMEM((ROWS, total), jnp.bfloat16),
             pltpu.VMEM((tokens, total), jnp.float32),
             pltpu.VMEM((tokens, total), jnp.float32),
-            pltpu.VMEM((total, width), jnp.float32),
             pltpu.VMEM((total, width), jnp.float32),
             pltpu.VMEM((total, width), jnp.float32),
             pltpu.VMEM((total, width), jnp.float32),
             pltpu.VMEM((8, total), jnp.float32),
             pltpu.VMEM((segments // 2, tokens), jnp.float32),
         ],
-        compiler_params=pltpu.CompilerParams(vmem_limit_bytes=32 * 2**20),
+        compiler_params=pltpu.CompilerParams(vmem_limit_bytes=40 * 2**20),
         name="core",
     )(*blocks)
 
@@ -452,10 +497,16 @@
     packed = pl.pallas_call(
         pack_kernel,
         out_shape=jax.ShapeDtypeStruct((4 * tokens + META, width), jnp.bfloat16),
-        in_specs=[vmem] * 6,
+        in_specs=[pl.BlockSpec(memory_space=pltpu.HBM)] * 6,
         out_specs=vmem,
+        scratch_shapes=[
+            pltpu.VMEM((1, tokens), jnp.float32),
+            pltpu.VMEM((1, 2), jnp.int32),
+            pltpu.SemaphoreType.DMA((6,)),
+        ],
+        compiler_params=pltpu.CompilerParams(vmem_limit_bytes=2 * 2**20),
         name="pack",
-    )(queries, keys, values, out_grad, log_gate.reshape(1, tokens), segment_order.reshape(1, 2))
+    )(*[pltpu.with_memory_space_constraint(t, pltpu.HBM) for t in (queries, keys, values, out_grad, log_gate.reshape(1, tokens), segment_order.reshape(1, 2))])
     blocks = gather_blocks(packed, devices)
     out, dq, dk, dv, gate = core_call(blocks, tokens, width, devices)
     return (out, dq, dk, dv, gate.reshape(tokens))

time: 38.6 us -> 35.3 us (0.915)
  Pallas kernels: 12.5 us -> 10.2 us
  local copies, waits for them, and re-layouts: 0.91 us -> 0 us
    pallas_call x1, Pallas kernels: 10.9 us -> 9.36 us  [core_call(): pl.pallas_call(functools.partial(core_kernel, counts, tokens, width), out...]
    unnamed x2 -> x0, local copies, waits for them, and re-layouts: 0.91 us -> none
    pallas_call x1, Pallas kernels: 1.55 us -> 0.89 us  [local_small(): pl.pallas_call(pack_kernel, out_shape=jax.ShapeDtypeStruct((4 * tokens +...]
where the time goes in v3:
time: 35.3 us; the launch traced here: 35.1 us
  starting transfers between devices  16 us (45%)
  Pallas kernels  10.2 us (29%)
  waiting for transfers between devices  8.21 us (23%)
  between operations  0.66 us (2%)
    ppermute x15, starting transfers between devices, shift(): return lax.ppermute(x, 'seq', pairs)  16 us
    pallas_call x1, Pallas kernels, core_call(): pl.pallas_call(functools.partial(core_kernel, counts, tokens, width), out...  9.36 us
    ppermute x15, waiting for transfers between devices, shift(): return lax.ppermute(x, 'seq', pairs)  8.21 us
    pallas_call x1, Pallas kernels, local_small(): pl.pallas_call(pack_kernel, out_shape=jax.ShapeDtypeStruct((4 * tokens +...  0.89 us
  transfers between devices with their start and end apart: 15, of which 6 were waited for; matrix products, arithmetic and copies ran while one was open for 0% of the time, Pallas kernels for 0%

profile of v3, /device:TPU:0, one launch (start us, length us, event | category | flops | bytes accessed | tf_op | source)
XLA Modules:
  0.0 35.1 jit_solution(200959938999842378)
XLA Ops:
  0.6 0.9 %pack.1.refs_0_ = bf16[528,128]{1,0:T(8,128)(2,1)S(1)} custom-call(bf16[128,128]{1,0:T(8,128)(2,1)} %q_ref.1, bf16[128,128]{1,0:T(8,128)(2,1)} %k_ref.1, bf16[128,128]{1,0:T(8,128)(2,1)} %v_ref.1, bf16[128,128]{1,0:T(8,128)(2,1)} %g_ref.1, f32[1,128]{1,0:T(1,128)} %bitcast.3, s32[1,2]{1,0:T(1,128)} %bitcast.4), custom_call_target="tpu_custom_call" | custom-call | tf_op jit(solution)/shard_map/pack/pallas_call | solution.py:497
  1.5 5.1 %collective-permute-start.2 = (bf16[528,128]{1,0:T(8,128)(2,1)S(1)}, bf16[528,128]{1,0:T(8,128)(2,1)S(1)}, u32[]{:S(2)}, u32[]{:S(2)}) collective-permute-start(bf16[528,128]{1,0:T(8,128)(2,1)S(1)} %pack.1.refs_0_), channel_id=1, source_target_pairs={{0,12},{1,13},{2,14},{3,15},{4,0},{5,1},{6,2},{7,3},{8,4},{9,5},{1... | collective-permute-start | bytes 405512 | tf_op jit(solution)/shard_map/ppermute | solution.py:478
  6.7 0.0 collective-permute-start.7
  6.7 0.0 collective-permute-start.1
  6.7 1.5 %collective-permute-start = (bf16[528,128]{1,0:T(8,128)(2,1)S(1)}, bf16[528,128]{1,0:T(8,128)(2,1)S(1)}, u32[]{:S(2)}, u32[]{:S(2)}) collective-permute-start(bf16[528,128]{1,0:T(8,128)(2,1)S(1)} %pack.1.refs_0_), channel_id=1, source_target_pairs={{0,2},{1,3},{2,0},{3,1},{4,6},{5,7},{6,4},{7,5},{8,10},{9,11},{10,... | collective-permute-start | bytes 405512 | tf_op jit(solution)/shard_map/ppermute | solution.py:478
  8.2 2.5 %collective-permute-done.2.refs_3_ = bf16[528,128]{1,0:T(8,128)(2,1)S(1)} collective-permute-done((bf16[528,128]{1,0:T(8,128)(2,1)S(1)}, bf16[528,128]{1,0:T(8,128)(2,1)S(1)}, u32[]{:S(2)}, u32[]{:S(2)}) %collective-permute-start.2) | collective-permute-done | bytes 135200 | tf_op jit(solution)/shard_map/ppermute | solution.py:478
  10.6 4.3 %collective-permute-start.5 = (bf16[528,128]{1,0:T(8,128)(2,1)S(1)}, bf16[528,128]{1,0:T(8,128)(2,1)S(1)}, u32[]{:S(2)}, u32[]{:S(2)}) collective-permute-start(bf16[528,128]{1,0:T(8,128)(2,1)S(1)} %collective-permute-done.2.refs_3_), channel_id=1, source_target_pairs={{0,12},{1,13},{2,14},{3,15},{4,0},{5,1},{6,2},{7,3},{8,4},{9,5},{1... | collective-permute-start | bytes 405512 | tf_op jit(solution)/shard_map/ppermute | solution.py:478
  14.9 0.0 collective-permute-start.10
  14.9 0.0 collective-permute-done.7.refs_8_
  14.9 1.5 %collective-permute-start.3 = (bf16[528,128]{1,0:T(8,128)(2,1)S(1)}, bf16[528,128]{1,0:T(8,128)(2,1)S(1)}, u32[]{:S(2)}, u32[]{:S(2)}) collective-permute-start(bf16[528,128]{1,0:T(8,128)(2,1)S(1)} %collective-permute-done.2.refs_3_), channel_id=1, source_target_pairs={{0,2},{1,3},{2,0},{3,1},{4,6},{5,7},{6,4},{7,5},{8,10},{9,11},{10,... | collective-permute-start | bytes 405512 | tf_op jit(solution)/shard_map/ppermute | solution.py:478
  16.4 0.0 collective-permute-done.1.refs_2_
  16.4 0.2 collective-permute-start.9
  16.7 0.0 collective-permute-done.refs_1_
  16.7 0.0 collective-permute-start.4
  16.7 1.0 %collective-permute-done.5.refs_6_ = bf16[528,128]{1,0:T(8,128)(2,1)S(1)} collective-permute-done((bf16[528,128]{1,0:T(8,128)(2,1)S(1)}, bf16[528,128]{1,0:T(8,128)(2,1)S(1)}, u32[]{:S(2)}, u32[]{:S(2)}) %collective-permute-start.5) | collective-permute-done | bytes 135200 | tf_op jit(solution)/shard_map/ppermute | solution.py:478
  17.7 2.4 %collective-permute-start.6 = (bf16[528,128]{1,0:T(8,128)(2,1)S(1)}, bf16[528,128]{1,0:T(8,128)(2,1)S(1)}, u32[]{:S(2)}, u32[]{:S(2)}) collective-permute-start(bf16[528,128]{1,0:T(8,128)(2,1)S(1)} %collective-permute-done.5.refs_6_), channel_id=1, source_target_pairs={{0,2},{1,3},{2,0},{3,1},{4,6},{5,7},{6,4},{7,5},{8,10},{9,11},{10,... | collective-permute-start | bytes 405512 | tf_op jit(solution)/shard_map/ppermute | solution.py:478
  20.0 0.0 collective-permute-done.10.refs_11_
  20.0 0.0 collective-permute-start.8
  20.0 1.4 %collective-permute-done.3.refs_4_ = bf16[528,128]{1,0:T(8,128)(2,1)S(1)} collective-permute-done((bf16[528,128]{1,0:T(8,128)(2,1)S(1)}, bf16[528,128]{1,0:T(8,128)(2,1)S(1)}, u32[]{:S(2)}, u32[]{:S(2)}) %collective-permute-start.3) | collective-permute-done | bytes 135200 | tf_op jit(solution)/shard_map/ppermute | solution.py:478
  21.4 0.0 collective-permute-start.13
  21.4 0.0 collective-permute-done.9.refs_10_
  21.4 0.5 %collective-permute-start.11 = (bf16[528,128]{1,0:T(8,128)(2,1)S(1)}, bf16[528,128]{1,0:T(8,128)(2,1)S(1)}, u32[]{:S(2)}, u32[]{:S(2)}) collective-permute-start(bf16[528,128]{1,0:T(8,128)(2,1)S(1)} %collective-permute-done.3.refs_4_), channel_id=1, source_target_pairs={{0,1},{1,0},{2,3},{3,2},{4,5},{5,4},{6,7},{7,6},{8,9},{9,8},{10,11... | collective-permute-start | bytes 405512 | tf_op jit(solution)/shard_map/ppermute | solution.py:478
  21.9 2.3 %collective-permute-done.4.refs_5_ = bf16[528,128]{1,0:T(8,128)(2,1)S(1)} collective-permute-done((bf16[528,128]{1,0:T(8,128)(2,1)S(1)}, bf16[528,128]{1,0:T(8,128)(2,1)S(1)}, u32[]{:S(2)}, u32[]{:S(2)}) %collective-permute-start.4) | collective-permute-done | bytes 135200 | tf_op jit(solution)/shard_map/ppermute | solution.py:478
  24.2 0.0 collective-permute-start.12
  24.2 0.0 collective-permute-done.6.refs_7_
  24.2 0.5 %collective-permute-start.14 = (bf16[528,128]{1,0:T(8,128)(2,1)S(1)}, bf16[528,128]{1,0:T(8,128)(2,1)S(1)}, u32[]{:S(2)}, u32[]{:S(2)}) collective-permute-start(bf16[528,128]{1,0:T(8,128)(2,1)S(1)} %collective-permute-done.6.refs_7_), channel_id=1, source_target_pairs={{0,1},{1,0},{2,3},{3,2},{4,5},{5,4},{6,7},{7,6},{8,9},{9,8},{10,11... | collective-permute-start | bytes 405512 | tf_op jit(solution)/shard_map/ppermute | solution.py:478
  24.7 0.0 collective-permute-done.8.refs_9_
  24.7 0.0 collective-permute-done.13.refs_14_
  24.8 0.0 collective-permute-done.11.refs_12_
  24.8 0.8 %collective-permute-done.12.refs_13_ = bf16[528,128]{1,0:T(8,128)(2,1)S(1)} collective-permute-done((bf16[528,128]{1,0:T(8,128)(2,1)S(1)}, bf16[528,128]{1,0:T(8,128)(2,1)S(1)}, u32[]{:S(2)}, u32[]{:S(2)}) %collective-permute-start.12) | collective-permute-done | bytes 135200 | tf_op jit(solution)/shard_map/ppermute | solution.py:478
  25.6 0.2 collective-permute-done.14.refs_15_
  25.8 9.4 %core.1 = (bf16[128,128]{1,0:T(8,128)(2,1)}, f32[128,128]{1,0:T(8,128)}, f32[128,128]{1,0:T(8,128)}, f32[128,128]{1,0:T(8,128)}, f32[1,128]{1,0:T(1,128)}) custom-call(bf16[528,128]{1,0:T(8,128)(2,1)S(1)} %pack.1.refs_0_, bf16[528,128]{1,0:T(8,128)(2,1)S(1)} %collective-permute-done.refs_1_, bf16[528,128]{1,0:T(8,128)(2,1)S(1)} %collective-permute-done.1.refs_2_, ...), custom_call_target="tpu_custom_call" | custom-call | tf_op jit(solution)/shard_map/core/pallas_call | solution.py:442
Async XLA Ops:
  1.5 9.1 %collective-permute-start.2 = (bf16[528,128]{1,0:T(8,128)(2,1)S(1)}, bf16[528,128]{1,0:T(8,128)(2,1)S(1)}, u32[]{:S(2)}, u32[]{:S(2)}) collective-permute-start(bf16[528,128]{1,0:T(8,128)(2,1)S(1)} %pack.1.refs_0_), channel_id=1, source_target_pairs={{0,12},{1,13},{2,14},{3,15},{4,0},{5,1},{6,2},{7,3},{8,4},{9,5},{1... | collective-permute-start | bytes 405512 | tf_op jit(solution)/shard_map/ppermute | solution.py:478
  6.7 8.3 %collective-permute-start.7 = (bf16[528,128]{1,0:T(8,128)(2,1)S(1)}, bf16[528,128]{1,0:T(8,128)(2,1)S(1)}, u32[]{:S(2)}, u32[]{:S(2)}) collective-permute-start(bf16[528,128]{1,0:T(8,128)(2,1)S(1)} %pack.1.refs_0_), channel_id=1, source_target_pairs={{0,1},{1,0},{2,3},{3,2},{4,5},{5,4},{6,7},{7,6},{8,9},{9,8},{10,11... | collective-permute-start | bytes 405512 | tf_op jit(solution)/shard_map/ppermute | solution.py:478
  6.7 9.8 %collective-permute-start.1 = (bf16[528,128]{1,0:T(8,128)(2,1)S(1)}, bf16[528,128]{1,0:T(8,128)(2,1)S(1)}, u32[]{:S(2)}, u32[]{:S(2)}) collective-permute-start(bf16[528,128]{1,0:T(8,128)(2,1)S(1)} %pack.1.refs_0_), channel_id=1, source_target_pairs={{0,4},{1,5},{2,6},{3,7},{4,8},{5,9},{6,10},{7,11},{8,12},{9,13},{1... | collective-permute-start | bytes 405512 | tf_op jit(solution)/shard_map/ppermute | solution.py:478
  6.7 10.0 %collective-permute-start = (bf16[528,128]{1,0:T(8,128)(2,1)S(1)}, bf16[528,128]{1,0:T(8,128)(2,1)S(1)}, u32[]{:S(2)}, u32[]{:S(2)}) collective-permute-start(bf16[528,128]{1,0:T(8,128)(2,1)S(1)} %pack.1.refs_0_), channel_id=1, source_target_pairs={{0,2},{1,3},{2,0},{3,1},{4,6},{5,7},{6,4},{7,5},{8,10},{9,11},{10,... | collective-permute-start | bytes 405512 | tf_op jit(solution)/shard_map/ppermute | solution.py:478
  10.6 7.0 %collective-permute-start.5 = (bf16[528,128]{1,0:T(8,128)(2,1)S(1)}, bf16[528,128]{1,0:T(8,128)(2,1)S(1)}, u32[]{:S(2)}, u32[]{:S(2)}) collective-permute-start(bf16[528,128]{1,0:T(8,128)(2,1)S(1)} %collective-permute-done.2.refs_3_), channel_id=1, source_target_pairs={{0,12},{1,13},{2,14},{3,15},{4,0},{5,1},{6,2},{7,3},{8,4},{9,5},{1... | collective-permute-start | bytes 405512 | tf_op jit(solution)/shard_map/ppermute | solution.py:478
  14.9 5.1 %collective-permute-start.10 = (bf16[528,128]{1,0:T(8,128)(2,1)S(1)}, bf16[528,128]{1,0:T(8,128)(2,1)S(1)}, u32[]{:S(2)}, u32[]{:S(2)}) collective-permute-start(bf16[528,128]{1,0:T(8,128)(2,1)S(1)} %collective-permute-done.2.refs_3_), channel_id=1, source_target_pairs={{0,1},{1,0},{2,3},{3,2},{4,5},{5,4},{6,7},{7,6},{8,9},{9,8},{10,11... | collective-permute-start | bytes 405512 | tf_op jit(solution)/shard_map/ppermute | solution.py:478
  14.9 6.5 %collective-permute-start.3 = (bf16[528,128]{1,0:T(8,128)(2,1)S(1)}, bf16[528,128]{1,0:T(8,128)(2,1)S(1)}, u32[]{:S(2)}, u32[]{:S(2)}) collective-permute-start(bf16[528,128]{1,0:T(8,128)(2,1)S(1)} %collective-permute-done.2.refs_3_), channel_id=1, source_target_pairs={{0,2},{1,3},{2,0},{3,1},{4,6},{5,7},{6,4},{7,5},{8,10},{9,11},{10,... | collective-permute-start | bytes 405512 | tf_op jit(solution)/shard_map/ppermute | solution.py:478
  16.4 5.0 %collective-permute-start.9 = (bf16[528,128]{1,0:T(8,128)(2,1)S(1)}, bf16[528,128]{1,0:T(8,128)(2,1)S(1)}, u32[]{:S(2)}, u32[]{:S(2)}) collective-permute-start(bf16[528,128]{1,0:T(8,128)(2,1)S(1)} %collective-permute-done.1.refs_2_), channel_id=1, source_target_pairs={{0,1},{1,0},{2,3},{3,2},{4,5},{5,4},{6,7},{7,6},{8,9},{9,8},{10,11... | collective-permute-start | bytes 405512 | tf_op jit(solution)/shard_map/ppermute | solution.py:478
  16.7 7.6 %collective-permute-start.4 = (bf16[528,128]{1,0:T(8,128)(2,1)S(1)}, bf16[528,128]{1,0:T(8,128)(2,1)S(1)}, u32[]{:S(2)}, u32[]{:S(2)}) collective-permute-start(bf16[528,128]{1,0:T(8,128)(2,1)S(1)} %collective-permute-done.refs_1_), channel_id=1, source_target_pairs={{0,4},{1,5},{2,6},{3,7},{4,8},{5,9},{6,10},{7,11},{8,12},{9,13},{1... | collective-permute-start | bytes 405512 | tf_op jit(solution)/shard_map/ppermute | solution.py:478
  17.7 6.6 %collective-permute-start.6 = (bf16[528,128]{1,0:T(8,128)(2,1)S(1)}, bf16[528,128]{1,0:T(8,128)(2,1)S(1)}, u32[]{:S(2)}, u32[]{:S(2)}) collective-permute-start(bf16[528,128]{1,0:T(8,128)(2,1)S(1)} %collective-permute-done.5.refs_6_), channel_id=1, source_target_pairs={{0,2},{1,3},{2,0},{3,1},{4,6},{5,7},{6,4},{7,5},{8,10},{9,11},{10,... | collective-permute-start | bytes 405512 | tf_op jit(solution)/shard_map/ppermute | solution.py:478
  20.0 4.7 %collective-permute-start.8 = (bf16[528,128]{1,0:T(8,128)(2,1)S(1)}, bf16[528,128]{1,0:T(8,128)(2,1)S(1)}, u32[]{:S(2)}, u32[]{:S(2)}) collective-permute-start(bf16[528,128]{1,0:T(8,128)(2,1)S(1)} %collective-permute-done.refs_1_), channel_id=1, source_target_pairs={{0,1},{1,0},{2,3},{3,2},{4,5},{5,4},{6,7},{7,6},{8,9},{9,8},{10,11... | collective-permute-start | bytes 405512 | tf_op jit(solution)/shard_map/ppermute | solution.py:478
  21.4 3.4 %collective-permute-start.13 = (bf16[528,128]{1,0:T(8,128)(2,1)S(1)}, bf16[528,128]{1,0:T(8,128)(2,1)S(1)}, u32[]{:S(2)}, u32[]{:S(2)}) collective-permute-start(bf16[528,128]{1,0:T(8,128)(2,1)S(1)} %collective-permute-done.5.refs_6_), channel_id=1, source_target_pairs={{0,1},{1,0},{2,3},{3,2},{4,5},{5,4},{6,7},{7,6},{8,9},{9,8},{10,11... | collective-permute-start | bytes 405512 | tf_op jit(solution)/shard_map/ppermute | solution.py:478
  21.4 3.4 %collective-permute-start.11 = (bf16[528,128]{1,0:T(8,128)(2,1)S(1)}, bf16[528,128]{1,0:T(8,128)(2,1)S(1)}, u32[]{:S(2)}, u32[]{:S(2)}) collective-permute-start(bf16[528,128]{1,0:T(8,128)(2,1)S(1)} %collective-permute-done.3.refs_4_), channel_id=1, source_target_pairs={{0,1},{1,0},{2,3},{3,2},{4,5},{5,4},{6,7},{7,6},{8,9},{9,8},{10,11... | collective-permute-start | bytes 405512 | tf_op jit(solution)/shard_map/ppermute | solution.py:478
  24.2 1.4 %collective-permute-start.12 = (bf16[528,128]{1,0:T(8,128)(2,1)S(1)}, bf16[528,128]{1,0:T(8,128)(2,1)S(1)}, u32[]{:S(2)}, u32[]{:S(2)}) collective-permute-start(bf16[528,128]{1,0:T(8,128)(2,1)S(1)} %collective-permute-done.4.refs_5_), channel_id=1, source_target_pairs={{0,1},{1,0},{2,3},{3,2},{4,5},{5,4},{6,7},{7,6},{8,9},{9,8},{10,11... | collective-permute-start | bytes 405512 | tf_op jit(solution)/shard_map/ppermute | solution.py:478
  24.2 1.5 %collective-permute-start.14 = (bf16[528,128]{1,0:T(8,128)(2,1)S(1)}, bf16[528,128]{1,0:T(8,128)(2,1)S(1)}, u32[]{:S(2)}, u32[]{:S(2)}) collective-permute-start(bf16[528,128]{1,0:T(8,128)(2,1)S(1)} %collective-permute-done.6.refs_7_), channel_id=1, source_target_pairs={{0,1},{1,0},{2,3},{3,2},{4,5},{5,4},{6,7},{7,6},{8,9},{9,8},{10,11... | collective-permute-start | bytes 405512 | tf_op jit(solution)/shard_map/ppermute | solution.py:478

commit v4 on v3

--- a/solution.py
+++ b/solution.py
@@ -1,9 +1,12 @@
+import functools
+
 import jax
 import jax.numpy as jnp
 from jax import lax
 from jax.experimental import pallas as pl
 from jax.experimental.pallas import tpu as pltpu
 from jax.sharding import PartitionSpec as P
+
 
 masked_value = -1e30
 
@@ -70,7 +73,7 @@
 
     def stats_step(block_index, carry):
         run_max, run_sum = carry
-        key_rows, value_rows, key_gate, key_pos = key_tile(block_index)
+        key_rows, _, key_gate, key_pos = key_tile(block_index)
         scores, visible = tile_scores(
             queries, own_gate, own_pos, key_rows, key_gate, key_pos, score_scale
         )
@@ -107,7 +110,7 @@
         return (key_rows, probs, probs * (dprob - row_delta[:, None]))
 
     def query_step(block_index, total):
-        key_rows, probs, dscore = row_terms(block_index)
+        key_rows, _, dscore = row_terms(block_index)
         return total + jnp.dot(
             dscore.astype(jnp.bfloat16), key_rows, preferred_element_type=jnp.float32
         )
@@ -240,7 +243,7 @@
     lane1 = lax.broadcasted_iota(jnp.int32, (1, tokens), 1)
     left = lane1 < seg
 
-    own_place = None
+    places = []
     for ref, count in zip(blocks, counts):
         for index in range(count):
             base = index * size
@@ -248,15 +251,15 @@
             gate = (meta[0:1] + meta[1:2]) + meta[2:3]
             place = meta[3:4].astype(jnp.int32)
             pair = (place[0, 0], place[0, seg])
-            if own_place is None:
-                own_place = pair
+            places.append((ref, base, pair))
             for half in range(2):
                 at = pl.multiple_of(pair[half] * seg, seg)
-                for slot, dest in enumerate((qs, ks, vs, gs)):
+                for slot, dest in enumerate((qs, ks)):
                     first = base + slot * tokens + half * seg
                     dest[pl.ds(at, seg), :] = ref[first : first + seg, :]
                 shifted = gate if half == 0 else pltpu.roll(gate, seg, 1)
                 cums[pl.ds(pair[half], 1), :] = jnp.where(left, shifted, 0.0)
+    own_place = places[0][2]
 
     inside = roll_sum_lanes(cums[...], seg, False)
     whole = jnp.broadcast_to(inside[:, seg - 1 : seg], inside.shape)
@@ -266,6 +269,13 @@
         even = cums[2 * tile : 2 * tile + 1, :]
         odd = pltpu.roll(cums[2 * tile + 1 : 2 * tile + 2, :], seg, 1)
         key_row[:, tile * tokens : (tile + 1) * tokens] = jnp.where(left, even, odd)
+
+    for ref, base, pair in places:
+        for half in range(2):
+            at = pl.multiple_of(pair[half] * seg, seg)
+            for slot, dest in ((2, vs), (3, gs)):
+                first = base + slot * tokens + half * seg
+                dest[pl.ds(at, seg), :] = ref[first : first + seg, :]
 
     points[...] = jnp.zeros_like(points)
     own = blocks[0]
@@ -395,10 +405,24 @@
             totals(after)
         if row_tiles and step % max(1, blocks_r // (total // size_c)) == 0:
             own_row_tile(row_tiles.pop(0))
-        own_cols(block)
         for tile in here:
             point_tile(block, tile)
+        own_cols(block)
     dk_ref[...] = dk_ref[...] * scale
+
+    def pick(ref):
+        return jnp.concatenate([ref[pl.ds(s, seg), :] for s in starts], axis=0)
+
+    log_total, delta = pick(total_col), pick(delta_col)
+    out_ref[...] = pick(outs).astype(jnp.bfloat16)
+    low = []
+    for at in range(0, total, width):
+        p = jnp.exp2(own_scores[:, at : at + width] - log_total)
+        ds = p * (own_dprobs[:, at : at + width] - delta)
+        low.append(ds.astype(jnp.bfloat16))
+    dq_ref[...] = scale * jnp.dot(
+        jnp.concatenate(low, axis=1), ks[...], preferred_element_type=jnp.float32
+    )
 
     for tile in range(segments // 2):
         c0 = tile * tokens
@@ -415,20 +439,6 @@
         halves.append(jnp.where(own_place[half] % 2 == half, line, turned))
     gate_ref[...] = jnp.where(left, halves[0], halves[1])
 
-    def pick(ref):
-        return jnp.concatenate([ref[pl.ds(s, seg), :] for s in starts], axis=0)
-
-    log_total, delta = pick(total_col), pick(delta_col)
-    out_ref[...] = pick(outs).astype(jnp.bfloat16)
-    low = []
-    for at in range(0, total, width):
-        p = jnp.exp2(own_scores[:, at : at + width] - log_total)
-        ds = p * (own_dprobs[:, at : at + width] - delta)
-        low.append(ds.astype(jnp.bfloat16))
-    dq_ref[...] = scale * jnp.dot(
-        jnp.concatenate(low, axis=1), ks[...], preferred_element_type=jnp.float32
-    )
-
 
 def core_call(blocks, tokens, width, devices):
     size = 4 * tokens + META
@@ -437,8 +447,6 @@
     segments = 2 * devices
     vmem = pl.BlockSpec(memory_space=pltpu.VMEM)
     square = jax.ShapeDtypeStruct((tokens, width), jnp.float32)
-    import functools
-
     return pl.pallas_call(
         functools.partial(core_kernel, counts, tokens, width),
         out_shape=(
@@ -471,23 +479,39 @@
 
 def shift(x, devices, ring=0, flip=0):
     line = devices // 4
+    walk = [0] + list(range(1, line, 2)) + list(range(2, line, 2))[::-1]
     pairs = []
-    for i in range(devices):
-        place, low = i // 4, i % 4
-        pairs.append((i, ((place + ring) % line) * 4 + (low ^ flip)))
+    for step, place in enumerate(walk):
+        target = walk[(step + ring) % line]
+        pairs += [(place * 4 + low, target * 4 + (low ^ flip)) for low in range(4)]
     return lax.ppermute(x, "seq", pairs)
 
 
+MOVES = (
+    ("down", "down", "own"),
+    ("up", "up", "own"),
+    ("side", "side", "own"),
+    ("own_core", "core", "own"),
+    ("down_down", "down", "down"),
+    ("down_side", "side", "down"),
+    ("side_up", "up", "side"),
+    ("up_core", "core", "up"),
+    ("last", "side", "down_down"),
+    ("down_core", "core", "down"),
+    ("down_side_core", "core", "down_side"),
+    ("side_core", "core", "side"),
+    ("side_up_core", "core", "side_up"),
+    ("down_down_core", "core", "down_down"),
+    ("last_core", "core", "last"),
+)
+KINDS = {"up": {"ring": 1}, "down": {"ring": -1}, "side": {"flip": 2}, "core": {"flip": 1}}
+
+
 def gather_blocks(x, devices):
-    a = shift(x, devices, flip=2)
-    b = shift(x, devices, ring=1)
-    c = shift(x, devices, ring=-1)
-    d = shift(c, devices, flip=2)
-    e = shift(a, devices, ring=1)
-    f = shift(c, devices, ring=-1)
-    g = shift(f, devices, flip=2)
-    near = [x, a, b, c, d, e, f, g]
-    return near + [shift(t, devices, flip=1) for t in near]
+    blocks = {"own": x}
+    for name, kind, sent in MOVES:
+        blocks[name] = shift(blocks[sent], devices, **KINDS[kind])
+    return list(blocks.values())
 
 
 def local_small(queries, keys, values, log_gate, out_grad, segment_order):

time: 35.3 us -> 33.3 us (0.943)
  starting transfers between devices: 16 us -> 12.6 us
  waiting for transfers between devices: 8.21 us -> 9.78 us
    ppermute x15, starting transfers between devices: 16 us -> 12.6 us  [shift(): return lax.ppermute(x, 'seq', pairs)]
    ppermute x15, waiting for transfers between devices: 8.21 us -> 9.78 us  [shift(): return lax.ppermute(x, 'seq', pairs)]
where the time goes in v4:
time: 33.3 us; the launch traced here: 33.1 us
  starting transfers between devices  12.6 us (38%)
  Pallas kernels  10.1 us (30%)
  waiting for transfers between devices  9.78 us (29%)
  between operations  0.68 us (2%)
    ppermute x15, starting transfers between devices, shift(): return lax.ppermute(x, 'seq', pairs)  12.6 us
    ppermute x15, waiting for transfers between devices, shift(): return lax.ppermute(x, 'seq', pairs)  9.78 us
    pallas_call x1, Pallas kernels, core_call(): pl.pallas_call(functools.partial(core_kernel, counts, tokens, width), out...  9.21 us
    pallas_call x1, Pallas kernels, local_small(): pl.pallas_call(pack_kernel, out_shape=jax.ShapeDtypeStruct((4 * tokens +...  0.89 us
  transfers between devices with their start and end apart: 15, of which 6 were waited for; matrix products, arithmetic and copies ran while one was open for 0% of the time, Pallas kernels for 0%

profile of v4, /device:TPU:0, one launch (start us, length us, event | category | flops | bytes accessed | tf_op | source)
XLA Modules:
  0.0 33.1 jit_solution(4115588320347679573)
XLA Ops:
  0.6 0.9 %pack.1.refs_0_ = bf16[528,128]{1,0:T(8,128)(2,1)S(1)} custom-call(bf16[128,128]{1,0:T(8,128)(2,1)} %q_ref.1, bf16[128,128]{1,0:T(8,128)(2,1)} %k_ref.1, bf16[128,128]{1,0:T(8,128)(2,1)} %v_ref.1, bf16[128,128]{1,0:T(8,128)(2,1)} %g_ref.1, f32[1,128]{1,0:T(1,128)} %bitcast.3, s32[1,2]{1,0:T(1,128)} %bitcast.4), custom_call_target="tpu_custom_call" | custom-call | tf_op jit(solution)/shard_map/pack/pallas_call | solution.py:521
  1.5 4.1 %collective-permute-start = (bf16[528,128]{1,0:T(8,128)(2,1)S(1)}, bf16[528,128]{1,0:T(8,128)(2,1)S(1)}, u32[]{:S(2)}, u32[]{:S(2)}) collective-permute-start(bf16[528,128]{1,0:T(8,128)(2,1)S(1)} %pack.1.refs_0_), channel_id=1, source_target_pairs={{0,8},{1,9},{2,10},{3,11},{4,0},{5,1},{6,2},{7,3},{12,4},{13,5},{1... | collective-permute-start | bytes 405512 | tf_op jit(solution)/shard_map/ppermute | solution.py:487
  5.6 1.5 %collective-permute-start.2 = (bf16[528,128]{1,0:T(8,128)(2,1)S(1)}, bf16[528,128]{1,0:T(8,128)(2,1)S(1)}, u32[]{:S(2)}, u32[]{:S(2)}) collective-permute-start(bf16[528,128]{1,0:T(8,128)(2,1)S(1)} %pack.1.refs_0_), channel_id=1, source_target_pairs={{0,2},{1,3},{2,0},{3,1},{4,6},{5,7},{6,4},{7,5},{12,14},{13,15},{1... | collective-permute-start | bytes 405512 | tf_op jit(solution)/shard_map/ppermute | solution.py:487
  7.1 0.0 collective-permute-start.1
  7.1 0.0 collective-permute-start.3
  7.1 2.5 %collective-permute-done.refs_1_ = bf16[528,128]{1,0:T(8,128)(2,1)S(1)} collective-permute-done((bf16[528,128]{1,0:T(8,128)(2,1)S(1)}, bf16[528,128]{1,0:T(8,128)(2,1)S(1)}, u32[]{:S(2)}, u32[]{:S(2)}) %collective-permute-start) | collective-permute-done | bytes 135200 | tf_op jit(solution)/shard_map/ppermute | solution.py:487
  9.6 3.4 %collective-permute-start.4 = (bf16[528,128]{1,0:T(8,128)(2,1)S(1)}, bf16[528,128]{1,0:T(8,128)(2,1)S(1)}, u32[]{:S(2)}, u32[]{:S(2)}) collective-permute-start(bf16[528,128]{1,0:T(8,128)(2,1)S(1)} %collective-permute-done.refs_1_), channel_id=1, source_target_pairs={{0,8},{1,9},{2,10},{3,11},{4,0},{5,1},{6,2},{7,3},{12,4},{13,5},{1... | collective-permute-start | bytes 405512 | tf_op jit(solution)/shard_map/ppermute | solution.py:487
  13.0 0.0 collective-permute-done.2.refs_3_
  13.0 0.0 collective-permute-start.11
  13.0 0.0 collective-permute-start.6
  13.0 0.7 %collective-permute-done.1.refs_2_ = bf16[528,128]{1,0:T(8,128)(2,1)S(1)} collective-permute-done((bf16[528,128]{1,0:T(8,128)(2,1)S(1)}, bf16[528,128]{1,0:T(8,128)(2,1)S(1)}, u32[]{:S(2)}, u32[]{:S(2)}) %collective-permute-start.1) | collective-permute-done | bytes 135200 | tf_op jit(solution)/shard_map/ppermute | solution.py:487
  13.7 0.0 collective-permute-start.7
  13.7 0.0 collective-permute-done.3.refs_4_
  13.7 1.5 %collective-permute-start.5 = (bf16[528,128]{1,0:T(8,128)(2,1)S(1)}, bf16[528,128]{1,0:T(8,128)(2,1)S(1)}, u32[]{:S(2)}, u32[]{:S(2)}) collective-permute-start(bf16[528,128]{1,0:T(8,128)(2,1)S(1)} %collective-permute-done.refs_1_), channel_id=1, source_target_pairs={{0,2},{1,3},{2,0},{3,1},{4,6},{5,7},{6,4},{7,5},{12,14},{13,15},{1... | collective-permute-start | bytes 405512 | tf_op jit(solution)/shard_map/ppermute | solution.py:487
  15.2 1.6 %collective-permute-done.4.refs_5_ = bf16[528,128]{1,0:T(8,128)(2,1)S(1)} collective-permute-done((bf16[528,128]{1,0:T(8,128)(2,1)S(1)}, bf16[528,128]{1,0:T(8,128)(2,1)S(1)}, u32[]{:S(2)}, u32[]{:S(2)}) %collective-permute-start.4) | collective-permute-done | bytes 135200 | tf_op jit(solution)/shard_map/ppermute | solution.py:487
  16.8 1.5 %collective-permute-start.8 = (bf16[528,128]{1,0:T(8,128)(2,1)S(1)}, bf16[528,128]{1,0:T(8,128)(2,1)S(1)}, u32[]{:S(2)}, u32[]{:S(2)}) collective-permute-start(bf16[528,128]{1,0:T(8,128)(2,1)S(1)} %collective-permute-done.4.refs_5_), channel_id=1, source_target_pairs={{0,2},{1,3},{2,0},{3,1},{4,6},{5,7},{6,4},{7,5},{12,14},{13,15},{1... | collective-permute-start | bytes 405512 | tf_op jit(solution)/shard_map/ppermute | solution.py:487
  18.3 0.0 collective-permute-done.11.refs_12_
  18.3 0.0 collective-permute-start.9
  18.3 1.8 %collective-permute-done.6.refs_7_ = bf16[528,128]{1,0:T(8,128)(2,1)S(1)} collective-permute-done((bf16[528,128]{1,0:T(8,128)(2,1)S(1)}, bf16[528,128]{1,0:T(8,128)(2,1)S(1)}, u32[]{:S(2)}, u32[]{:S(2)}) %collective-permute-start.6) | collective-permute-done | bytes 135200 | tf_op jit(solution)/shard_map/ppermute | solution.py:487
  20.1 0.0 collective-permute-start.13
  20.1 0.0 collective-permute-done.7.refs_8_
  20.1 0.5 %collective-permute-start.12 = (bf16[528,128]{1,0:T(8,128)(2,1)S(1)}, bf16[528,128]{1,0:T(8,128)(2,1)S(1)}, u32[]{:S(2)}, u32[]{:S(2)}) collective-permute-start(bf16[528,128]{1,0:T(8,128)(2,1)S(1)} %collective-permute-done.6.refs_7_), channel_id=1, source_target_pairs={{0,1},{1,0},{2,3},{3,2},{4,5},{5,4},{6,7},{7,6},{12,13},{13,12},{1... | collective-permute-start | bytes 405512 | tf_op jit(solution)/shard_map/ppermute | solution.py:487
  20.6 0.0 collective-permute-done.5.refs_6_
  20.6 0.1 collective-permute-start.10
  20.7 1.9 %collective-permute-done.8.refs_9_ = bf16[528,128]{1,0:T(8,128)(2,1)S(1)} collective-permute-done((bf16[528,128]{1,0:T(8,128)(2,1)S(1)}, bf16[528,128]{1,0:T(8,128)(2,1)S(1)}, u32[]{:S(2)}, u32[]{:S(2)}) %collective-permute-start.8) | collective-permute-done | bytes 135200 | tf_op jit(solution)/shard_map/ppermute | solution.py:487
  22.6 0.0 collective-permute-start.14
  22.6 0.0 collective-permute-done.9.refs_10_
  22.6 0.0 collective-permute-done.12.refs_13_
  22.6 0.0 collective-permute-done.10.refs_11_
  22.6 0.0 collective-permute-done.13.refs_14_
  22.6 1.3 %collective-permute-done.14.refs_15_ = bf16[528,128]{1,0:T(8,128)(2,1)S(1)} collective-permute-done((bf16[528,128]{1,0:T(8,128)(2,1)S(1)}, bf16[528,128]{1,0:T(8,128)(2,1)S(1)}, u32[]{:S(2)}, u32[]{:S(2)}) %collective-permute-start.14) | collective-permute-done | bytes 135200 | tf_op jit(solution)/shard_map/ppermute | solution.py:487
  23.9 9.2 %core.1 = (bf16[128,128]{1,0:T(8,128)(2,1)}, f32[128,128]{1,0:T(8,128)}, f32[128,128]{1,0:T(8,128)}, f32[128,128]{1,0:T(8,128)}, f32[1,128]{1,0:T(1,128)}) custom-call(bf16[528,128]{1,0:T(8,128)(2,1)S(1)} %pack.1.refs_0_, bf16[528,128]{1,0:T(8,128)(2,1)S(1)} %collective-permute-done.refs_1_, bf16[528,128]{1,0:T(8,128)(2,1)S(1)} %collective-permute-done.1.refs_2_, ...), custom_call_target="tpu_custom_call" | custom-call | tf_op jit(solution)/shard_map/core/pallas_call | solution.py:450
Async XLA Ops:
  1.5 8.1 %collective-permute-start = (bf16[528,128]{1,0:T(8,128)(2,1)S(1)}, bf16[528,128]{1,0:T(8,128)(2,1)S(1)}, u32[]{:S(2)}, u32[]{:S(2)}) collective-permute-start(bf16[528,128]{1,0:T(8,128)(2,1)S(1)} %pack.1.refs_0_), channel_id=1, source_target_pairs={{0,8},{1,9},{2,10},{3,11},{4,0},{5,1},{6,2},{7,3},{12,4},{13,5},{1... | collective-permute-start | bytes 405512 | tf_op jit(solution)/shard_map/ppermute | solution.py:487
  5.6 7.4 %collective-permute-start.2 = (bf16[528,128]{1,0:T(8,128)(2,1)S(1)}, bf16[528,128]{1,0:T(8,128)(2,1)S(1)}, u32[]{:S(2)}, u32[]{:S(2)}) collective-permute-start(bf16[528,128]{1,0:T(8,128)(2,1)S(1)} %pack.1.refs_0_), channel_id=1, source_target_pairs={{0,2},{1,3},{2,0},{3,1},{4,6},{5,7},{6,4},{7,5},{12,14},{13,15},{1... | collective-permute-start | bytes 405512 | tf_op jit(solution)/shard_map/ppermute | solution.py:487
  7.1 6.5 %collective-permute-start.1 = (bf16[528,128]{1,0:T(8,128)(2,1)S(1)}, bf16[528,128]{1,0:T(8,128)(2,1)S(1)}, u32[]{:S(2)}, u32[]{:S(2)}) collective-permute-start(bf16[528,128]{1,0:T(8,128)(2,1)S(1)} %pack.1.refs_0_), channel_id=1, source_target_pairs={{0,4},{1,5},{2,6},{3,7},{4,12},{5,13},{6,14},{7,15},{12,8},{13,9},... | collective-permute-start | bytes 405512 | tf_op jit(solution)/shard_map/ppermute | solution.py:487
  7.1 6.5 %collective-permute-start.3 = (bf16[528,128]{1,0:T(8,128)(2,1)S(1)}, bf16[528,128]{1,0:T(8,128)(2,1)S(1)}, u32[]{:S(2)}, u32[]{:S(2)}) collective-permute-start(bf16[528,128]{1,0:T(8,128)(2,1)S(1)} %pack.1.refs_0_), channel_id=1, source_target_pairs={{0,1},{1,0},{2,3},{3,2},{4,5},{5,4},{6,7},{7,6},{12,13},{13,12},{1... | collective-permute-start | bytes 405512 | tf_op jit(solution)/shard_map/ppermute | solution.py:487
  9.6 7.2 %collective-permute-start.4 = (bf16[528,128]{1,0:T(8,128)(2,1)S(1)}, bf16[528,128]{1,0:T(8,128)(2,1)S(1)}, u32[]{:S(2)}, u32[]{:S(2)}) collective-permute-start(bf16[528,128]{1,0:T(8,128)(2,1)S(1)} %collective-permute-done.refs_1_), channel_id=1, source_target_pairs={{0,8},{1,9},{2,10},{3,11},{4,0},{5,1},{6,2},{7,3},{12,4},{13,5},{1... | collective-permute-start | bytes 405512 | tf_op jit(solution)/shard_map/ppermute | solution.py:487
  13.0 5.3 %collective-permute-start.11 = (bf16[528,128]{1,0:T(8,128)(2,1)S(1)}, bf16[528,128]{1,0:T(8,128)(2,1)S(1)}, u32[]{:S(2)}, u32[]{:S(2)}) collective-permute-start(bf16[528,128]{1,0:T(8,128)(2,1)S(1)} %collective-permute-done.2.refs_3_), channel_id=1, source_target_pairs={{0,1},{1,0},{2,3},{3,2},{4,5},{5,4},{6,7},{7,6},{12,13},{13,12},{1... | collective-permute-start | bytes 405512 | tf_op jit(solution)/shard_map/ppermute | solution.py:487
  13.0 7.1 %collective-permute-start.6 = (bf16[528,128]{1,0:T(8,128)(2,1)S(1)}, bf16[528,128]{1,0:T(8,128)(2,1)S(1)}, u32[]{:S(2)}, u32[]{:S(2)}) collective-permute-start(bf16[528,128]{1,0:T(8,128)(2,1)S(1)} %collective-permute-done.2.refs_3_), channel_id=1, source_target_pairs={{0,4},{1,5},{2,6},{3,7},{4,12},{5,13},{6,14},{7,15},{12,8},{13,9},... | collective-permute-start | bytes 405512 | tf_op jit(solution)/shard_map/ppermute | solution.py:487
  13.7 6.4 %collective-permute-start.7 = (bf16[528,128]{1,0:T(8,128)(2,1)S(1)}, bf16[528,128]{1,0:T(8,128)(2,1)S(1)}, u32[]{:S(2)}, u32[]{:S(2)}) collective-permute-start(bf16[528,128]{1,0:T(8,128)(2,1)S(1)} %collective-permute-done.1.refs_2_), channel_id=1, source_target_pairs={{0,1},{1,0},{2,3},{3,2},{4,5},{5,4},{6,7},{7,6},{12,13},{13,12},{1... | collective-permute-start | bytes 405512 | tf_op jit(solution)/shard_map/ppermute | solution.py:487
  13.7 6.9 %collective-permute-start.5 = (bf16[528,128]{1,0:T(8,128)(2,1)S(1)}, bf16[528,128]{1,0:T(8,128)(2,1)S(1)}, u32[]{:S(2)}, u32[]{:S(2)}) collective-permute-start(bf16[528,128]{1,0:T(8,128)(2,1)S(1)} %collective-permute-done.refs_1_), channel_id=1, source_target_pairs={{0,2},{1,3},{2,0},{3,1},{4,6},{5,7},{6,4},{7,5},{12,14},{13,15},{1... | collective-permute-start | bytes 405512 | tf_op jit(solution)/shard_map/ppermute | solution.py:487
  16.8 5.8 %collective-permute-start.8 = (bf16[528,128]{1,0:T(8,128)(2,1)S(1)}, bf16[528,128]{1,0:T(8,128)(2,1)S(1)}, u32[]{:S(2)}, u32[]{:S(2)}) collective-permute-start(bf16[528,128]{1,0:T(8,128)(2,1)S(1)} %collective-permute-done.4.refs_5_), channel_id=1, source_target_pairs={{0,2},{1,3},{2,0},{3,1},{4,6},{5,7},{6,4},{7,5},{12,14},{13,15},{1... | collective-permute-start | bytes 405512 | tf_op jit(solution)/shard_map/ppermute | solution.py:487
  18.3 4.3 %collective-permute-start.9 = (bf16[528,128]{1,0:T(8,128)(2,1)S(1)}, bf16[528,128]{1,0:T(8,128)(2,1)S(1)}, u32[]{:S(2)}, u32[]{:S(2)}) collective-permute-start(bf16[528,128]{1,0:T(8,128)(2,1)S(1)} %collective-permute-done.refs_1_), channel_id=1, source_target_pairs={{0,1},{1,0},{2,3},{3,2},{4,5},{5,4},{6,7},{7,6},{12,13},{13,12},{1... | collective-permute-start | bytes 405512 | tf_op jit(solution)/shard_map/ppermute | solution.py:487
  20.1 2.5 %collective-permute-start.13 = (bf16[528,128]{1,0:T(8,128)(2,1)S(1)}, bf16[528,128]{1,0:T(8,128)(2,1)S(1)}, u32[]{:S(2)}, u32[]{:S(2)}) collective-permute-start(bf16[528,128]{1,0:T(8,128)(2,1)S(1)} %collective-permute-done.4.refs_5_), channel_id=1, source_target_pairs={{0,1},{1,0},{2,3},{3,2},{4,5},{5,4},{6,7},{7,6},{12,13},{13,12},{1... | collective-permute-start | bytes 405512 | tf_op jit(solution)/shard_map/ppermute | solution.py:487
  20.1 2.5 %collective-permute-start.12 = (bf16[528,128]{1,0:T(8,128)(2,1)S(1)}, bf16[528,128]{1,0:T(8,128)(2,1)S(1)}, u32[]{:S(2)}, u32[]{:S(2)}) collective-permute-start(bf16[528,128]{1,0:T(8,128)(2,1)S(1)} %collective-permute-done.6.refs_7_), channel_id=1, source_target_pairs={{0,1},{1,0},{2,3},{3,2},{4,5},{5,4},{6,7},{7,6},{12,13},{13,12},{1... | collective-permute-start | bytes 405512 | tf_op jit(solution)/shard_map/ppermute | solution.py:487
  20.6 2.0 %collective-permute-start.10 = (bf16[528,128]{1,0:T(8,128)(2,1)S(1)}, bf16[528,128]{1,0:T(8,128)(2,1)S(1)}, u32[]{:S(2)}, u32[]{:S(2)}) collective-permute-start(bf16[528,128]{1,0:T(8,128)(2,1)S(1)} %collective-permute-done.5.refs_6_), channel_id=1, source_target_pairs={{0,1},{1,0},{2,3},{3,2},{4,5},{5,4},{6,7},{7,6},{12,13},{13,12},{1... | collective-permute-start | bytes 405512 | tf_op jit(solution)/shard_map/ppermute | solution.py:487
  22.6 1.4 %collective-permute-start.14 = (bf16[528,128]{1,0:T(8,128)(2,1)S(1)}, bf16[528,128]{1,0:T(8,128)(2,1)S(1)}, u32[]{:S(2)}, u32[]{:S(2)}) collective-permute-start(bf16[528,128]{1,0:T(8,128)(2,1)S(1)} %collective-permute-done.8.refs_9_), channel_id=1, source_target_pairs={{0,1},{1,0},{2,3},{3,2},{4,5},{5,4},{6,7},{7,6},{12,13},{13,12},{1... | collective-permute-start | bytes 405512 | tf_op jit(solution)/shard_map/ppermute | solution.py:487

commit v5 on v4

--- a/solution.py
+++ b/solution.py
@@ -163,8 +163,6 @@
 
 LOG2E = 1.4426950408889634
 META = 16
-ROWS = 256
-COLS = 256
 
 
 def pack_kernel(q_ref, k_ref, v_ref, g_ref, gate_hbm, order_hbm, out_ref, gate_ref, order_ref, sems):
@@ -204,6 +202,10 @@
     return items[len(items) * turn // turns : len(items) * (turn + 1) // turns]
 
 
+def block_order(steps):
+    return [1] + list(range(steps - 1, 1, -1)) + [0]
+
+
 def roll_sum_lanes(x, span, reverse):
     lanes = x.shape[1]
     lane = lax.broadcasted_iota(jnp.int32, x.shape, 1)
@@ -230,16 +232,80 @@
     return x
 
 
-def core_kernel(counts, tokens, width, *refs):
+def spread(column, width):
+    return jnp.broadcast_to(column, (column.shape[0], width))
+
+
+def halves(x, width):
+    return [x[:, at : at + width] for at in range(0, x.shape[1], width)]
+
+
+def log_total_of(pieces, width):
+    best = pieces[0]
+    for s in pieces[1:]:
+        best = jnp.maximum(best, s)
+    top = spread(jnp.max(best, axis=1, keepdims=True), width)
+    mass = jnp.exp2(pieces[0] - top)
+    for s in pieces[1:]:
+        mass = mass + jnp.exp2(s - top)
+    return top + spread(jnp.log2(jnp.sum(mass, axis=1, keepdims=True)), width)
+
+
+def score_of(q, ks, key_row, tile, cols, factor):
+    c0 = tile * cols
+    return contract_last(q, ks[c0 : c0 + cols, :]) * factor - key_row[:, c0 : c0 + cols]
+
+
+def start_rows(own, place, ks, key_row, own_s, own_total):
+    total, width = ks.shape
+    tokens = own_s.shape[0]
+    seg = tokens // 2
+    cols = 2 * tokens
+    inner = lax.broadcasted_iota(jnp.int32, (tokens, 1), 0)
+    row_pos = jnp.where(inner < seg, place[0] * seg + inner, place[1] * seg + inner - seg)
+    q = own[0:tokens, :]
+    pieces = []
+    for tile in range(total // cols):
+        c0 = tile * cols
+        seen = lax.broadcasted_iota(jnp.int32, (tokens, cols), 1) + c0 <= row_pos
+        s = score_of(q, ks, key_row, tile, cols, width ** (-0.5) * LOG2E)
+        s = jnp.where(seen, s, masked_value)
+        own_s[:, c0 : c0 + cols] = s
+        pieces += halves(s, width)
+    own_total[...] = log_total_of(pieces, width)
+
+
+def row_kernel(own, ks, vs, own_s, own_total, out_ref, dq_ref):
+    total, width = ks.shape
+    tokens = out_ref.shape[0]
+    cols = 2 * tokens
+    g = own[3 * tokens : 4 * tokens, :]
+    log_total = own_total[...]
+    p, dps = [], []
+    for tile in range(total // cols):
+        c0 = tile * cols
+        p += [jnp.exp2(s - log_total) for s in halves(own_s[:, c0 : c0 + cols], width)]
+        dps += halves(contract_last(g, vs[c0 : c0 + cols, :]), width)
+    low = jnp.concatenate([t.astype(jnp.bfloat16) for t in p], axis=1)
+    out = jnp.dot(low, vs[...], preferred_element_type=jnp.float32)
+    out_ref[...] = out.astype(jnp.bfloat16)
+    delta = spread(jnp.sum(g.astype(jnp.float32) * out, axis=1, keepdims=True), width)
+    low = jnp.concatenate(
+        [(t * (dp - delta)).astype(jnp.bfloat16) for t, dp in zip(p, dps)], axis=1
+    )
+    dq_ref[...] = width ** (-0.5) * jnp.dot(low, ks[...], preferred_element_type=jnp.float32)
+
+
+def core_kernel(counts, partner, tokens, width, core_ref, *refs):
     blocks = refs[: len(counts)]
-    out_ref, dq_ref, dk_ref, dv_ref, gate_ref = refs[len(counts) : len(counts) + 5]
-    (qs, ks, vs, gs, cums, key_row, scores, probs, own_scores, own_dprobs, total_col, delta_col,
-     outs, points, point_rows) = refs[len(counts) + 5 :]
+    keep_ref, send_ref, ks, vs, own_s, own_total = refs[len(counts) : len(counts) + 6]
+    qs, gs, cums, key_row, points, lines = refs[len(counts) + 6 :]
     seg = tokens // 2
     total = qs.shape[0]
     segments = total // seg
     size = 4 * tokens + META
     scale = width ** (-0.5)
+    factor = scale * LOG2E
     lane1 = lax.broadcasted_iota(jnp.int32, (1, tokens), 1)
     left = lane1 < seg
 
@@ -278,203 +344,204 @@
                 dest[pl.ds(at, seg), :] = ref[first : first + seg, :]
 
     points[...] = jnp.zeros_like(points)
+    inner = lax.broadcasted_iota(jnp.int32, (tokens, 1), 0)
     own = blocks[0]
-    starts = [pl.multiple_of(p * seg, seg) for p in own_place]
-    own_q = own[0:tokens, :]
-    own_k = own[tokens : 2 * tokens, :]
-    own_v = own[2 * tokens : 3 * tokens, :]
-    own_g = own[3 * tokens : 4 * tokens, :]
-    key_lines = [cums[pl.ds(p, 1), :] for p in own_place]
-    own_key = jnp.where(left, key_lines[0], pltpu.roll(key_lines[1], seg, 1))
-    col_pos = jnp.where(left, starts[0] + lane1, starts[1] + lane1 - seg)
-    inner = lax.broadcasted_iota(jnp.int32, (tokens, 1), 0)
-    row_pos = jnp.where(inner < seg, starts[0] + inner, starts[1] + inner - seg)
-    dk_ref[...] = jnp.zeros_like(dk_ref)
-    dv_ref[...] = jnp.zeros_like(dv_ref)
-
-    size_r, size_c = ROWS, COLS
-    blocks_r = total // size_r
-    row_in = lax.broadcasted_iota(jnp.int32, (size_r, size_c), 0)
-    col_in = lax.broadcasted_iota(jnp.int32, (size_r, size_c), 1)
-    causal = [col_in <= row_in + at for at in range(0, max(size_c, size_r), size_r)]
-    factor = scale * LOG2E
-    best = {}
-    slots = {}
-
-    def rows_of(ref, block):
-        return ref[block * size_r : (block + 1) * size_r, :]
-
-    def spread(column):
-        return jnp.broadcast_to(column, (column.shape[0], width))
-
-    def tiles_of(block):
-        return range(((block + 1) * size_r + size_c - 1) // size_c)
-
-    def score_tile(block, tile):
-        c0 = tile * size_c
-        s = contract_last(rows_of(qs, block), ks[c0 : c0 + size_c, :]) * factor
-        s = s - key_row[:, c0 : c0 + size_c]
-        if c0 + size_c > block * size_r:
-            s = jnp.where(causal[block % len(causal)], s, masked_value)
-        scores[slots[block], :, c0 : c0 + size_c] = s
-        part = s[:, :width]
-        for at in range(width, size_c, width):
-            part = jnp.maximum(part, s[:, at : at + width])
-        best[block] = jnp.maximum(best[block], part) if block in best else part
-
-    def own_row_tile(tile):
-        c0 = tile * size_c
-        s = contract_last(own_q, ks[c0 : c0 + size_c, :]) * factor - key_row[:, c0 : c0 + size_c]
-        seen = lax.broadcasted_iota(jnp.int32, (tokens, size_c), 1) + c0 <= row_pos
-        own_scores[:, c0 : c0 + size_c] = jnp.where(seen, s, masked_value)
-        own_dprobs[:, c0 : c0 + size_c] = contract_last(own_g, vs[c0 : c0 + size_c, :])
-
-    def totals(block):
-        top = spread(jnp.max(best[block], axis=1, keepdims=True))
-        mass = None
-        for at in range(0, len(tiles_of(block)) * size_c, width):
-            e = jnp.exp2(scores[slots[block], :, at : at + width] - top)
-            mass = e if mass is None else mass + e
-        total_col[block * size_r : (block + 1) * size_r, :] = top + spread(
-            jnp.log2(jnp.sum(mass, axis=1, keepdims=True))
-        )
-
-    def prob_tile(block, tile, low):
-        log_total = rows_of(total_col, block)
-        for at in range(tile * size_c, (tile + 1) * size_c, width):
-            p = jnp.exp2(scores[slots[block], :, at : at + width] - log_total)
-            probs[slots[block], :, at : at + width] = p
-            low.append(p.astype(jnp.bfloat16))
-
-    def outputs(block, low):
-        wide = len(tiles_of(block)) * size_c
-        acc = jnp.dot(
-            jnp.concatenate(low, axis=1), vs[:wide, :], preferred_element_type=jnp.float32
-        )
-        outs[block * size_r : (block + 1) * size_r, :] = acc
-        g = rows_of(gs, block).astype(jnp.float32)
-        delta_col[block * size_r : (block + 1) * size_r, :] = spread(
-            jnp.sum(g * acc, axis=1, keepdims=True)
-        )
-
-    def own_cols(block):
-        r0 = block * size_r
-        g = rows_of(gs, block)
-        s = contract_last(rows_of(qs, block), own_k) * factor - own_key
-        seen = lax.broadcasted_iota(jnp.int32, (size_r, tokens), 0) + r0 >= col_pos
-        p = jnp.where(seen, jnp.exp2(s - rows_of(total_col, block)), 0.0)
-        ds = p * (contract_last(g, own_v) - rows_of(delta_col, block))
-        dv_ref[...] += contract_first(p.astype(jnp.bfloat16), g)
-        dk_ref[...] += contract_first(ds.astype(jnp.bfloat16), rows_of(qs, block))
-
-    def point_tile(block, tile):
-        c0 = tile * size_c
-        delta = rows_of(delta_col, block)
-        dp = contract_last(rows_of(gs, block), vs[c0 : c0 + size_c, :])
-        for at in range(0, size_c, width):
-            ds = probs[slots[block], :, c0 + at : c0 + at + width] * (dp[:, at : at + width] - delta)
-            points[:, c0 + at : c0 + at + width] += jnp.sum(
-                ds.reshape(size_r // 8, 8, width), axis=0
-            )
-
-    rest = list(range(1, blocks_r))
-    sequence = []
-    while rest:
-        sequence.append(rest.pop(0))
-        if rest:
-            sequence.append(rest.pop())
-    sequence.append(0)
-    slots.update({block: step % 2 for step, block in enumerate(sequence)})
-    first = sequence[0]
-    for tile in tiles_of(first):
-        score_tile(first, tile)
-    totals(first)
-    row_tiles = list(range(total // size_c))
-    for step, block in enumerate(sequence):
-        after = sequence[step + 1] if step + 1 < blocks_r else None
-        ahead = list(tiles_of(after)) if after is not None else []
-        here = list(tiles_of(block))
-        low = []
-        for turn in range(max(len(here), len(ahead))):
-            for tile in split(ahead, turn, max(len(here), len(ahead))):
+
+    other = blocks[partner]
+    pair_k = jnp.concatenate([own[tokens : 2 * tokens, :], other[tokens : 2 * tokens, :]], axis=0)
+    pair_v = jnp.concatenate(
+        [own[2 * tokens : 3 * tokens, :], other[2 * tokens : 3 * tokens, :]], axis=0
+    )
+    firsts = [0, sum(counts[:partner])]
+    pair_key, pair_pos = [], []
+    for first in firsts:
+        place = places[first][2]
+        key = [cums[pl.ds(p, 1), :] for p in place]
+        pair_key.append(jnp.where(left, key[0], pltpu.roll(key[1], seg, 1)))
+        pair_pos.append(
+            jnp.where(left, place[0] * seg + lane1, place[1] * seg + lane1 - seg)
+        )
+    pair_key = jnp.concatenate(pair_key, axis=1)
+    pair_pos = jnp.concatenate(pair_pos, axis=1)
+
+    rows, cols = tokens, 2 * tokens
+    steps = total // cols
+    core = core_ref[0, 0]
+    row_in = lax.broadcasted_iota(jnp.int32, (rows, cols), 0) + core * rows
+    col_in = lax.broadcasted_iota(jnp.int32, (rows, cols), 1)
+    causal = col_in <= row_in
+    state = {}
+
+    def open_item(item):
+        r0 = pl.multiple_of((2 * item + core) * rows, rows)
+        state[item] = dict(
+            q=qs[pl.ds(r0, rows), :], g=gs[pl.ds(r0, rows), :], r0=r0, tiles=item + 1,
+            s=[], p=[], low=[],
+        )
+
+    def score_tile(item, tile):
+        it = state[item]
+        s = score_of(it["q"], ks, key_row, tile, cols, factor)
+        if tile == item:
+            s = jnp.where(causal, s, masked_value)
+        it["s"] += halves(s, width)
+
+    def prob_tile(item, tile):
+        it = state[item]
+        for s in it["s"][2 * tile : 2 * tile + 2]:
+            p = jnp.exp2(s - it["total"])
+            it["p"].append(p)
+            it["low"].append(p.astype(jnp.bfloat16))
+
+    def outputs(item):
+        it = state[item]
+        out = jnp.dot(
+            jnp.concatenate(it["low"], axis=1),
+            vs[: it["tiles"] * cols, :],
+            preferred_element_type=jnp.float32,
+        )
+        g = it["g"].astype(jnp.float32)
+        it["delta"] = spread(jnp.sum(g * out, axis=1, keepdims=True), width)
+
+    sums = dict(k=jnp.zeros((cols, width), jnp.float32), v=jnp.zeros((cols, width), jnp.float32))
+
+    def pair_columns(item):
+        it = state[item]
+        s = contract_last(it["q"], pair_k) * factor - pair_key
+        seen = pair_pos <= it["r0"] + inner
+        p = jnp.where(seen, jnp.exp2(s - jnp.concatenate([it["total"]] * 2, axis=1)), 0.0)
+        ds = p * (contract_last(it["g"], pair_v) - jnp.concatenate([it["delta"]] * 2, axis=1))
+        sums["v"] = sums["v"] + contract_first(p.astype(jnp.bfloat16), it["g"])
+        sums["k"] = sums["k"] + contract_first(ds.astype(jnp.bfloat16), it["q"])
+
+    def last_stage(item):
+        it = state[item]
+        for tile in range(it["tiles"]):
+            c0 = tile * cols
+            dp = halves(contract_last(it["g"], vs[c0 : c0 + cols, :]), width)
+            for at in range(2):
+                ds = it["p"][2 * tile + at] * (dp[at] - it["delta"])
+                first = c0 + at * width
+                points[:, first : first + width] += jnp.sum(
+                    ds.reshape(rows // 8, 8, width), axis=0
+                )
+        pair_columns(item)
+
+    order = block_order(steps)
+    open_item(order[0])
+    for tile in range(state[order[0]]["tiles"]):
+        score_tile(order[0], tile)
+    state[order[0]]["total"] = log_total_of(state[order[0]]["s"], width)
+    for turn, item in enumerate(order):
+        after = order[turn + 1] if turn + 1 < len(order) else None
+        here = list(range(state[item]["tiles"]))
+        ahead = []
+        if after is not None:
+            open_item(after)
+            ahead = list(range(state[after]["tiles"]))
+        count = max(len(here), len(ahead))
+        for at in range(count):
+            for tile in split(ahead, at, count):
                 score_tile(after, tile)
-            for tile in split(here, turn, max(len(here), len(ahead))):
-                prob_tile(block, tile, low)
-        outputs(block, low)
+            for tile in split(here, at, count):
+                prob_tile(item, tile)
+        outputs(item)
         if after is not None:
-            totals(after)
-        if row_tiles and step % max(1, blocks_r // (total // size_c)) == 0:
-            own_row_tile(row_tiles.pop(0))
-        for tile in here:
-            point_tile(block, tile)
-        own_cols(block)
-    dk_ref[...] = dk_ref[...] * scale
-
-    def pick(ref):
-        return jnp.concatenate([ref[pl.ds(s, seg), :] for s in starts], axis=0)
-
-    log_total, delta = pick(total_col), pick(delta_col)
-    out_ref[...] = pick(outs).astype(jnp.bfloat16)
-    low = []
-    for at in range(0, total, width):
-        p = jnp.exp2(own_scores[:, at : at + width] - log_total)
-        ds = p * (own_dprobs[:, at : at + width] - delta)
-        low.append(ds.astype(jnp.bfloat16))
-    dq_ref[...] = scale * jnp.dot(
-        jnp.concatenate(low, axis=1), ks[...], preferred_element_type=jnp.float32
-    )
-
-    for tile in range(segments // 2):
-        c0 = tile * tokens
-        point_rows[tile : tile + 1, :] = -jnp.sum(
-            points[:, c0 : c0 + tokens], axis=0, keepdims=True
-        )
-    inside = roll_sum_lanes(point_rows[...], tokens, True)
+            state[after]["total"] = log_total_of(state[after]["s"], width)
+        last_stage(item)
+
+    for tile in range(total // width):
+        lines[tile : tile + 1, :] = -jnp.sum(
+            points[:, tile * width : (tile + 1) * width], axis=0, keepdims=True
+        )
+    inside = roll_sum_lanes(lines[...], tokens, True)
     whole = jnp.broadcast_to(inside[:, 0:1], inside.shape)
-    point_rows[...] = inside + (roll_sum_rows(whole, True) - whole)
-    halves = []
-    for half in range(2):
-        line = point_rows[pl.ds(own_place[half] // 2, 1), :]
-        turned = pltpu.roll(line, seg, 1)
-        halves.append(jnp.where(own_place[half] % 2 == half, line, turned))
-    gate_ref[...] = jnp.where(left, halves[0], halves[1])
-
-
-def core_call(blocks, tokens, width, devices):
+    lines[...] = inside + (roll_sum_rows(whole, True) - whole)
+    for index, ref in enumerate((keep_ref, send_ref)):
+        ref[0:tokens, :] = sums["k"][index * tokens : (index + 1) * tokens, :] * scale
+        ref[tokens : 2 * tokens, :] = sums["v"][index * tokens : (index + 1) * tokens, :]
+        parts = []
+        for half, place in enumerate(places[firsts[index]][2]):
+            line = lines[pl.ds(place // 2, 1), :]
+            parts.append(jnp.where(place % 2 == half, line, pltpu.roll(line, seg, 1)))
+        ref[2 * tokens : 2 * tokens + 8, :] = jnp.broadcast_to(
+            jnp.where(left, parts[0], parts[1]), (8, width)
+        )
+    start_rows(own, own_place, ks, key_row, own_s, own_total)
+
+
+def join_kernel(keep_ref, got_ref, dk_ref, dv_ref, gate_ref):
+    tokens = dk_ref.shape[0]
+    dk_ref[...] = keep_ref[0:tokens, :] + got_ref[0:tokens, :]
+    dv_ref[...] = keep_ref[tokens : 2 * tokens, :] + got_ref[tokens : 2 * tokens, :]
+    gate_ref[...] = keep_ref[2 * tokens : 2 * tokens + 1, :] + got_ref[2 * tokens : 2 * tokens + 1, :]
+
+
+def core_call(blocks, tokens, width, devices, core, partner):
     size = 4 * tokens + META
     counts = tuple(b.shape[0] // size for b in blocks)
     total = tokens * devices
     segments = 2 * devices
     vmem = pl.BlockSpec(memory_space=pltpu.VMEM)
-    square = jax.ShapeDtypeStruct((tokens, width), jnp.float32)
+    smem = pl.BlockSpec(memory_space=pltpu.SMEM)
+    part = jax.ShapeDtypeStruct((2 * tokens + 8, width), jnp.float32)
+    sorted_rows = jax.ShapeDtypeStruct((total, width), jnp.bfloat16)
     return pl.pallas_call(
-        functools.partial(core_kernel, counts, tokens, width),
+        functools.partial(core_kernel, counts, partner, tokens, width),
         out_shape=(
-            jax.ShapeDtypeStruct((tokens, width), jnp.bfloat16),
-            square,
-            square,
-            square,
-            jax.ShapeDtypeStruct((1, tokens), jnp.float32),
+            part,
+            part,
+            sorted_rows,
+            sorted_rows,
+            jax.ShapeDtypeStruct((tokens, total), jnp.float32),
+            jax.ShapeDtypeStruct((tokens, width), jnp.float32),
         ),
-        in_specs=[vmem] * len(blocks),
-        out_specs=[vmem] * 5,
-        scratch_shapes=[pltpu.VMEM((total, width), jnp.bfloat16)] * 4
-        + [
+        in_specs=[smem] + [vmem] * len(blocks),
+        out_specs=[vmem] * 6,
+        scratch_shapes=[
+            pltpu.VMEM((total, width), jnp.bfloat16),
+            pltpu.VMEM((total, width), jnp.bfloat16),
             pltpu.VMEM((segments, tokens), jnp.float32),
             pltpu.VMEM((1, total), jnp.float32),
-            pltpu.VMEM((2, ROWS, total), jnp.float32),
-            pltpu.VMEM((2, ROWS, total), jnp.float32),
-            pltpu.VMEM((tokens, total), jnp.float32),
-            pltpu.VMEM((tokens, total), jnp.float32),
-            pltpu.VMEM((total, width), jnp.float32),
-            pltpu.VMEM((total, width), jnp.float32),
-            pltpu.VMEM((total, width), jnp.float32),
             pltpu.VMEM((8, total), jnp.float32),
-            pltpu.VMEM((segments // 2, tokens), jnp.float32),
+            pltpu.VMEM((total // width, width), jnp.float32),
         ],
         compiler_params=pltpu.CompilerParams(vmem_limit_bytes=40 * 2**20),
         name="core",
-    )(*blocks)
+    )(core, *blocks)
+
+
+def row_call(own, ks, vs, own_s, own_total, tokens, width):
+    vmem = pl.BlockSpec(memory_space=pltpu.VMEM)
+    return pl.pallas_call(
+        row_kernel,
+        out_shape=(
+            jax.ShapeDtypeStruct((tokens, width), jnp.bfloat16),
+            jax.ShapeDtypeStruct((tokens, width), jnp.float32),
+        ),
+        in_specs=[vmem] * 5,
+        out_specs=[vmem] * 2,
+        compiler_params=pltpu.CompilerParams(vmem_limit_bytes=24 * 2**20),
+        cost_estimate=pl.CostEstimate(
+            flops=6 * tokens * ks.shape[0] * width,
+            bytes_accessed=4 * ks.shape[0] * width,
+            transcendentals=tokens * ks.shape[0],
+        ),
+        name="rows",
+    )(own, ks, vs, own_s, own_total)
+
+
+def join_call(keep, got, tokens, width):
+    vmem = pl.BlockSpec(memory_space=pltpu.VMEM)
+    square = jax.ShapeDtypeStruct((tokens, width), jnp.float32)
+    return pl.pallas_call(
+        join_kernel,
+        out_shape=(square, square, jax.ShapeDtypeStruct((1, width), jnp.float32)),
+        in_specs=[vmem, vmem],
+        out_specs=[vmem] * 3,
+        compiler_params=pltpu.CompilerParams(vmem_limit_bytes=2 * 2**20),
+        name="join",
+    )(keep, got)
 
 
 def shift(x, devices, ring=0, flip=0):
@@ -532,7 +599,12 @@
         name="pack",
     )(*[pltpu.with_memory_space_constraint(t, pltpu.HBM) for t in (queries, keys, values, out_grad, log_gate.reshape(1, tokens), segment_order.reshape(1, 2))])
     blocks = gather_blocks(packed, devices)
-    out, dq, dk, dv, gate = core_call(blocks, tokens, width, devices)
+    core = (lax.axis_index("seq") % 2).astype(jnp.int32).reshape(1, 1)
+    partner = 1 + [m[0] for m in MOVES].index("own_core")
+    keep, send, ks, vs, own_s, own_total = core_call(blocks, tokens, width, devices, core, partner)
+    got = shift(send, devices, flip=1)
+    out, dq = row_call(packed, ks, vs, own_s, own_total, tokens, width)
+    dk, dv, gate = join_call(keep, got, tokens, width)
     return (out, dq, dk, dv, gate.reshape(tokens))
 
 

time: 33.3 us -> 32.7 us (0.982)
  Pallas kernels: 10.1 us -> 9.2 us
    pallas_call x1 -> x3, Pallas kernels: 9.21 us -> 8.31 us  [the longest x1 6.19 us: core_call(): pl.pallas_call(functools.partial(core_kernel, counts, partner, tokens, wi...]
    ppermute x15 -> x16, starting transfers between devices: 12.6 us -> 12.8 us  [shift(): return lax.ppermute(x, 'seq', pairs)]
    ppermute x15 -> x16, waiting for transfers between devices: 9.78 us -> 9.78 us  [shift(): return lax.ppermute(x, 'seq', pairs)]
  transfers between devices with their start and end apart: 15 -> 16, of which waited for: 6 -> 6; matrix products, arithmetic and copies ran while one was open for 0% -> 0% of each run, Pallas kernels for 0% -> 4%
where the time goes in v5:
time: 32.7 us; the launch traced here: 32.5 us
  starting transfers between devices  12.8 us (39%)
  waiting for transfers between devices  9.78 us (30%)
  Pallas kernels  9.2 us (28%)
  between operations  0.69 us (2%)
    ppermute x16, starting transfers between devices, shift(): return lax.ppermute(x, 'seq', pairs)  12.8 us
    ppermute x16, waiting for transfers between devices, shift(): return lax.ppermute(x, 'seq', pairs)  9.78 us
    pallas_call x1, Pallas kernels, core_call(): pl.pallas_call(functools.partial(core_kernel, counts, partner, tokens, wi...  6.19 us
    pallas_call x1, Pallas kernels, row_call(): pl.pallas_call(row_kernel, out_shape=(jax.ShapeDtypeStruct((tokens, width...  1.45 us
    pallas_call x1, Pallas kernels, local_small(): pl.pallas_call(pack_kernel, out_shape=jax.ShapeDtypeStruct((4 * tokens +...  0.89 us
    pallas_call x1, Pallas kernels, join_call(): pl.pallas_call(join_kernel, out_shape=(square, square, jax.ShapeDtypeStru...  0.67 us
  transfers between devices with their start and end apart: 16, of which 6 were waited for; matrix products, arithmetic and copies ran while one was open for 0% of the time, Pallas kernels for 4%

profile of v5, /device:TPU:0, one launch (start us, length us, event | category | flops | bytes accessed | tf_op | source)
XLA Modules:
  0.0 32.5 jit_solution(8966795475346698257)
XLA Ops:
  0.6 0.9 %pack.1.refs_0_.own = bf16[528,128]{1,0:T(8,128)(2,1)S(1)} custom-call(bf16[128,128]{1,0:T(8,128)(2,1)} %q_ref.1, bf16[128,128]{1,0:T(8,128)(2,1)} %k_ref.1, bf16[128,128]{1,0:T(8,128)(2,1)} %v_ref.1, bf16[128,128]{1,0:T(8,128)(2,1)} %g_ref.1, f32[1,128]{1,0:T(1,128)} %bitcast.4, s32[1,2]{1,0:T(1,128)} %bitcast.5), custom_call_target="tpu_custom_call" | custom-call | tf_op jit(solution)/shard_map/pack/pallas_call | solution.py:588
  1.5 4.1 %collective-permute-start = (bf16[528,128]{1,0:T(8,128)(2,1)S(1)}, bf16[528,128]{1,0:T(8,128)(2,1)S(1)}, u32[]{:S(2)}, u32[]{:S(2)}) collective-permute-start(bf16[528,128]{1,0:T(8,128)(2,1)S(1)} %pack.1.refs_0_.own), channel_id=1, source_target_pairs={{0,8},{1,9},{2,10},{3,11},{4,0},{5,1},{6,2},{7,3},{12,4},{13,5},{1... | collective-permute-start | bytes 405512 | tf_op jit(solution)/shard_map/ppermute | solution.py:554
  5.6 1.5 %collective-permute-start.2 = (bf16[528,128]{1,0:T(8,128)(2,1)S(1)}, bf16[528,128]{1,0:T(8,128)(2,1)S(1)}, u32[]{:S(2)}, u32[]{:S(2)}) collective-permute-start(bf16[528,128]{1,0:T(8,128)(2,1)S(1)} %pack.1.refs_0_.own), channel_id=1, source_target_pairs={{0,2},{1,3},{2,0},{3,1},{4,6},{5,7},{6,4},{7,5},{12,14},{13,15},{1... | collective-permute-start | bytes 405512 | tf_op jit(solution)/shard_map/ppermute | solution.py:554
  7.1 0.0 collective-permute-start.1
  7.1 0.0 collective-permute-start.3
  7.1 2.5 %collective-permute-done.refs_1_ = bf16[528,128]{1,0:T(8,128)(2,1)S(1)} collective-permute-done((bf16[528,128]{1,0:T(8,128)(2,1)S(1)}, bf16[528,128]{1,0:T(8,128)(2,1)S(1)}, u32[]{:S(2)}, u32[]{:S(2)}) %collective-permute-start) | collective-permute-done | bytes 135200 | tf_op jit(solution)/shard_map/ppermute | solution.py:554
  9.6 3.4 %collective-permute-start.4 = (bf16[528,128]{1,0:T(8,128)(2,1)S(1)}, bf16[528,128]{1,0:T(8,128)(2,1)S(1)}, u32[]{:S(2)}, u32[]{:S(2)}) collective-permute-start(bf16[528,128]{1,0:T(8,128)(2,1)S(1)} %collective-permute-done.refs_1_), channel_id=1, source_target_pairs={{0,8},{1,9},{2,10},{3,11},{4,0},{5,1},{6,2},{7,3},{12,4},{13,5},{1... | collective-permute-start | bytes 405512 | tf_op jit(solution)/shard_map/ppermute | solution.py:554
  13.0 0.0 collective-permute-done.2.refs_3_
  13.0 0.0 collective-permute-start.11
  13.0 0.0 collective-permute-start.6
  13.0 0.7 %collective-permute-done.1.refs_2_ = bf16[528,128]{1,0:T(8,128)(2,1)S(1)} collective-permute-done((bf16[528,128]{1,0:T(8,128)(2,1)S(1)}, bf16[528,128]{1,0:T(8,128)(2,1)S(1)}, u32[]{:S(2)}, u32[]{:S(2)}) %collective-permute-start.1) | collective-permute-done | bytes 135200 | tf_op jit(solution)/shard_map/ppermute | solution.py:554
  13.7 0.0 collective-permute-start.7
  13.7 0.0 collective-permute-done.3.refs_4_
  13.7 1.5 %collective-permute-start.5 = (bf16[528,128]{1,0:T(8,128)(2,1)S(1)}, bf16[528,128]{1,0:T(8,128)(2,1)S(1)}, u32[]{:S(2)}, u32[]{:S(2)}) collective-permute-start(bf16[528,128]{1,0:T(8,128)(2,1)S(1)} %collective-permute-done.refs_1_), channel_id=1, source_target_pairs={{0,2},{1,3},{2,0},{3,1},{4,6},{5,7},{6,4},{7,5},{12,14},{13,15},{1... | collective-permute-start | bytes 405512 | tf_op jit(solution)/shard_map/ppermute | solution.py:554
  15.2 1.6 %collective-permute-done.4.refs_5_ = bf16[528,128]{1,0:T(8,128)(2,1)S(1)} collective-permute-done((bf16[528,128]{1,0:T(8,128)(2,1)S(1)}, bf16[528,128]{1,0:T(8,128)(2,1)S(1)}, u32[]{:S(2)}, u32[]{:S(2)}) %collective-permute-start.4) | collective-permute-done | bytes 135200 | tf_op jit(solution)/shard_map/ppermute | solution.py:554
  16.8 1.5 %collective-permute-start.8 = (bf16[528,128]{1,0:T(8,128)(2,1)S(1)}, bf16[528,128]{1,0:T(8,128)(2,1)S(1)}, u32[]{:S(2)}, u32[]{:S(2)}) collective-permute-start(bf16[528,128]{1,0:T(8,128)(2,1)S(1)} %collective-permute-done.4.refs_5_), channel_id=1, source_target_pairs={{0,2},{1,3},{2,0},{3,1},{4,6},{5,7},{6,4},{7,5},{12,14},{13,15},{1... | collective-permute-start | bytes 405512 | tf_op jit(solution)/shard_map/ppermute | solution.py:554
  18.3 0.0 collective-permute-done.11.refs_12_
  18.3 0.0 collective-permute-start.9
  18.3 1.8 %collective-permute-done.6.refs_7_ = bf16[528,128]{1,0:T(8,128)(2,1)S(1)} collective-permute-done((bf16[528,128]{1,0:T(8,128)(2,1)S(1)}, bf16[528,128]{1,0:T(8,128)(2,1)S(1)}, u32[]{:S(2)}, u32[]{:S(2)}) %collective-permute-start.6) | collective-permute-done | bytes 135200 | tf_op jit(solution)/shard_map/ppermute | solution.py:554
  20.1 0.0 collective-permute-start.13
  20.1 0.0 collective-permute-done.7.refs_8_
  20.1 0.5 %collective-permute-start.12 = (bf16[528,128]{1,0:T(8,128)(2,1)S(1)}, bf16[528,128]{1,0:T(8,128)(2,1)S(1)}, u32[]{:S(2)}, u32[]{:S(2)}) collective-permute-start(bf16[528,128]{1,0:T(8,128)(2,1)S(1)} %collective-permute-done.6.refs_7_), channel_id=1, source_target_pairs={{0,1},{1,0},{2,3},{3,2},{4,5},{5,4},{6,7},{7,6},{12,13},{13,12},{1... | collective-permute-start | bytes 405512 | tf_op jit(solution)/shard_map/ppermute | solution.py:554
  20.6 0.0 collective-permute-done.5.refs_6_
  20.6 0.1 collective-permute-start.10
  20.7 1.9 %collective-permute-done.8.refs_9_ = bf16[528,128]{1,0:T(8,128)(2,1)S(1)} collective-permute-done((bf16[528,128]{1,0:T(8,128)(2,1)S(1)}, bf16[528,128]{1,0:T(8,128)(2,1)S(1)}, u32[]{:S(2)}, u32[]{:S(2)}) %collective-permute-start.8) | collective-permute-done | bytes 135200 | tf_op jit(solution)/shard_map/ppermute | solution.py:554
  22.6 0.0 collective-permute-start.14
  22.6 0.0 collective-permute-done.9.refs_10_
  22.6 0.0 collective-permute-done.12.refs_13_
  22.6 0.0 collective-permute-done.10.refs_11_
  22.6 0.0 collective-permute-done.13.refs_14_
  22.6 1.3 %collective-permute-done.14.refs_15_ = bf16[528,128]{1,0:T(8,128)(2,1)S(1)} collective-permute-done((bf16[528,128]{1,0:T(8,128)(2,1)S(1)}, bf16[528,128]{1,0:T(8,128)(2,1)S(1)}, u32[]{:S(2)}, u32[]{:S(2)}) %collective-permute-start.14) | collective-permute-done | bytes 135200 | tf_op jit(solution)/shard_map/ppermute | solution.py:554
  23.9 6.2 %core.1 = (f32[264,128]{1,0:T(8,128)S(1)}, f32[264,128]{1,0:T(8,128)S(1)}, bf16[2048,128]{1,0:T(8,128)(2,1)S(1)}, bf16[2048,128]{1,0:T(8,128)(2,1)S(1)}, f32[128...) custom-call(s32[1,1]{1,0:T(1,128)} %bitcast.2.core_ref, bf16[528,128]{1,0:T(8,128)(2,1)S(1)} %pack.1.refs_0_.own, ...), custom_call_target="tpu_custom_call" | custom-call | tf_op jit(solution)/shard_map/core/pallas_call | solution.py:489
  30.1 0.2 collective-permute-start.15
  30.3 1.5 %rows.1 = (bf16[128,128]{1,0:T(8,128)(2,1)}, f32[128,128]{1,0:T(8,128)}) custom-call(bf16[528,128]{1,0:T(8,128)(2,1)S(1)} %pack.1.refs_0_.own, bf16[2048,128]{1,0:T(8,128)(2,1)S(1)} %get-tuple-element.16.ks, bf16[2048,128]{1,0:T(8,128)(2,1)S(1)} %get-tuple-element.17.vs, f32[128,2048]{1,0:T(8,128)S(1)} %get-tuple-element.18.own_s, ...), custom_call_target="tpu_custom_call" | custom-call | flops 201326592 | bytes 1048576 | tf_op jit(solution)/shard_map/rows/pallas_call | solution.py:516
  31.8 0.0 collective-permute-done.15.got_ref
  31.8 0.7 %join.1 = (f32[128,128]{1,0:T(8,128)}, f32[128,128]{1,0:T(8,128)}, f32[1,128]{1,0:T(1,128)}) custom-call(f32[264,128]{1,0:T(8,128)S(1)} %get-tuple-element.22.keep_ref, f32[264,128]{1,0:T(8,128)S(1)} %collective-permute-done.15.got_ref), custom_call_target="tpu_custom_call" | custom-call | tf_op jit(solution)/shard_map/join/pallas_call | solution.py:537
Async XLA Ops:
  1.5 8.1 %collective-permute-start = (bf16[528,128]{1,0:T(8,128)(2,1)S(1)}, bf16[528,128]{1,0:T(8,128)(2,1)S(1)}, u32[]{:S(2)}, u32[]{:S(2)}) collective-permute-start(bf16[528,128]{1,0:T(8,128)(2,1)S(1)} %pack.1.refs_0_.own), channel_id=1, source_target_pairs={{0,8},{1,9},{2,10},{3,11},{4,0},{5,1},{6,2},{7,3},{12,4},{13,5},{1... | collective-permute-start | bytes 405512 | tf_op jit(solution)/shard_map/ppermute | solution.py:554
  5.6 7.4 %collective-permute-start.2 = (bf16[528,128]{1,0:T(8,128)(2,1)S(1)}, bf16[528,128]{1,0:T(8,128)(2,1)S(1)}, u32[]{:S(2)}, u32[]{:S(2)}) collective-permute-start(bf16[528,128]{1,0:T(8,128)(2,1)S(1)} %pack.1.refs_0_.own), channel_id=1, source_target_pairs={{0,2},{1,3},{2,0},{3,1},{4,6},{5,7},{6,4},{7,5},{12,14},{13,15},{1... | collective-permute-start | bytes 405512 | tf_op jit(solution)/shard_map/ppermute | solution.py:554
  7.1 6.5 %collective-permute-start.1 = (bf16[528,128]{1,0:T(8,128)(2,1)S(1)}, bf16[528,128]{1,0:T(8,128)(2,1)S(1)}, u32[]{:S(2)}, u32[]{:S(2)}) collective-permute-start(bf16[528,128]{1,0:T(8,128)(2,1)S(1)} %pack.1.refs_0_.own), channel_id=1, source_target_pairs={{0,4},{1,5},{2,6},{3,7},{4,12},{5,13},{6,14},{7,15},{12,8},{13,9},... | collective-permute-start | bytes 405512 | tf_op jit(solution)/shard_map/ppermute | solution.py:554
  7.1 6.5 %collective-permute-start.3 = (bf16[528,128]{1,0:T(8,128)(2,1)S(1)}, bf16[528,128]{1,0:T(8,128)(2,1)S(1)}, u32[]{:S(2)}, u32[]{:S(2)}) collective-permute-start(bf16[528,128]{1,0:T(8,128)(2,1)S(1)} %pack.1.refs_0_.own), channel_id=1, source_target_pairs={{0,1},{1,0},{2,3},{3,2},{4,5},{5,4},{6,7},{7,6},{12,13},{13,12},{1... | collective-permute-start | bytes 405512 | tf_op jit(solution)/shard_map/ppermute | solution.py:554
  9.6 7.2 %collective-permute-start.4 = (bf16[528,128]{1,0:T(8,128)(2,1)S(1)}, bf16[528,128]{1,0:T(8,128)(2,1)S(1)}, u32[]{:S(2)}, u32[]{:S(2)}) collective-permute-start(bf16[528,128]{1,0:T(8,128)(2,1)S(1)} %collective-permute-done.refs_1_), channel_id=1, source_target_pairs={{0,8},{1,9},{2,10},{3,11},{4,0},{5,1},{6,2},{7,3},{12,4},{13,5},{1... | collective-permute-start | bytes 405512 | tf_op jit(solution)/shard_map/ppermute | solution.py:554
  13.0 5.3 %collective-permute-start.11 = (bf16[528,128]{1,0:T(8,128)(2,1)S(1)}, bf16[528,128]{1,0:T(8,128)(2,1)S(1)}, u32[]{:S(2)}, u32[]{:S(2)}) collective-permute-start(bf16[528,128]{1,0:T(8,128)(2,1)S(1)} %collective-permute-done.2.refs_3_), channel_id=1, source_target_pairs={{0,1},{1,0},{2,3},{3,2},{4,5},{5,4},{6,7},{7,6},{12,13},{13,12},{1... | collective-permute-start | bytes 405512 | tf_op jit(solution)/shard_map/ppermute | solution.py:554
  13.0 7.1 %collective-permute-start.6 = (bf16[528,128]{1,0:T(8,128)(2,1)S(1)}, bf16[528,128]{1,0:T(8,128)(2,1)S(1)}, u32[]{:S(2)}, u32[]{:S(2)}) collective-permute-start(bf16[528,128]{1,0:T(8,128)(2,1)S(1)} %collective-permute-done.2.refs_3_), channel_id=1, source_target_pairs={{0,4},{1,5},{2,6},{3,7},{4,12},{5,13},{6,14},{7,15},{12,8},{13,9},... | collective-permute-start | bytes 405512 | tf_op jit(solution)/shard_map/ppermute | solution.py:554
  13.7 6.4 %collective-permute-start.7 = (bf16[528,128]{1,0:T(8,128)(2,1)S(1)}, bf16[528,128]{1,0:T(8,128)(2,1)S(1)}, u32[]{:S(2)}, u32[]{:S(2)}) collective-permute-start(bf16[528,128]{1,0:T(8,128)(2,1)S(1)} %collective-permute-done.1.refs_2_), channel_id=1, source_target_pairs={{0,1},{1,0},{2,3},{3,2},{4,5},{5,4},{6,7},{7,6},{12,13},{13,12},{1... | collective-permute-start | bytes 405512 | tf_op jit(solution)/shard_map/ppermute | solution.py:554
  13.7 6.9 %collective-permute-start.5 = (bf16[528,128]{1,0:T(8,128)(2,1)S(1)}, bf16[528,128]{1,0:T(8,128)(2,1)S(1)}, u32[]{:S(2)}, u32[]{:S(2)}) collective-permute-start(bf16[528,128]{1,0:T(8,128)(2,1)S(1)} %collective-permute-done.refs_1_), channel_id=1, source_target_pairs={{0,2},{1,3},{2,0},{3,1},{4,6},{5,7},{6,4},{7,5},{12,14},{13,15},{1... | collective-permute-start | bytes 405512 | tf_op jit(solution)/shard_map/ppermute | solution.py:554
  16.8 5.8 %collective-permute-start.8 = (bf16[528,128]{1,0:T(8,128)(2,1)S(1)}, bf16[528,128]{1,0:T(8,128)(2,1)S(1)}, u32[]{:S(2)}, u32[]{:S(2)}) collective-permute-start(bf16[528,128]{1,0:T(8,128)(2,1)S(1)} %collective-permute-done.4.refs_5_), channel_id=1, source_target_pairs={{0,2},{1,3},{2,0},{3,1},{4,6},{5,7},{6,4},{7,5},{12,14},{13,15},{1... | collective-permute-start | bytes 405512 | tf_op jit(solution)/shard_map/ppermute | solution.py:554
  18.3 4.3 %collective-permute-start.9 = (bf16[528,128]{1,0:T(8,128)(2,1)S(1)}, bf16[528,128]{1,0:T(8,128)(2,1)S(1)}, u32[]{:S(2)}, u32[]{:S(2)}) collective-permute-start(bf16[528,128]{1,0:T(8,128)(2,1)S(1)} %collective-permute-done.refs_1_), channel_id=1, source_target_pairs={{0,1},{1,0},{2,3},{3,2},{4,5},{5,4},{6,7},{7,6},{12,13},{13,12},{1... | collective-permute-start | bytes 405512 | tf_op jit(solution)/shard_map/ppermute | solution.py:554
  20.1 2.5 %collective-permute-start.13 = (bf16[528,128]{1,0:T(8,128)(2,1)S(1)}, bf16[528,128]{1,0:T(8,128)(2,1)S(1)}, u32[]{:S(2)}, u32[]{:S(2)}) collective-permute-start(bf16[528,128]{1,0:T(8,128)(2,1)S(1)} %collective-permute-done.4.refs_5_), channel_id=1, source_target_pairs={{0,1},{1,0},{2,3},{3,2},{4,5},{5,4},{6,7},{7,6},{12,13},{13,12},{1... | collective-permute-start | bytes 405512 | tf_op jit(solution)/shard_map/ppermute | solution.py:554
  20.1 2.5 %collective-permute-start.12 = (bf16[528,128]{1,0:T(8,128)(2,1)S(1)}, bf16[528,128]{1,0:T(8,128)(2,1)S(1)}, u32[]{:S(2)}, u32[]{:S(2)}) collective-permute-start(bf16[528,128]{1,0:T(8,128)(2,1)S(1)} %collective-permute-done.6.refs_7_), channel_id=1, source_target_pairs={{0,1},{1,0},{2,3},{3,2},{4,5},{5,4},{6,7},{7,6},{12,13},{13,12},{1... | collective-permute-start | bytes 405512 | tf_op jit(solution)/shard_map/ppermute | solution.py:554
  20.6 2.0 %collective-permute-start.10 = (bf16[528,128]{1,0:T(8,128)(2,1)S(1)}, bf16[528,128]{1,0:T(8,128)(2,1)S(1)}, u32[]{:S(2)}, u32[]{:S(2)}) collective-permute-start(bf16[528,128]{1,0:T(8,128)(2,1)S(1)} %collective-permute-done.5.refs_6_), channel_id=1, source_target_pairs={{0,1},{1,0},{2,3},{3,2},{4,5},{5,4},{6,7},{7,6},{12,13},{13,12},{1... | collective-permute-start | bytes 405512 | tf_op jit(solution)/shard_map/ppermute | solution.py:554
  22.6 1.4 %collective-permute-start.14 = (bf16[528,128]{1,0:T(8,128)(2,1)S(1)}, bf16[528,128]{1,0:T(8,128)(2,1)S(1)}, u32[]{:S(2)}, u32[]{:S(2)}) collective-permute-start(bf16[528,128]{1,0:T(8,128)(2,1)S(1)} %collective-permute-done.8.refs_9_), channel_id=1, source_target_pairs={{0,1},{1,0},{2,3},{3,2},{4,5},{5,4},{6,7},{7,6},{12,13},{13,12},{1... | collective-permute-start | bytes 405512 | tf_op jit(solution)/shard_map/ppermute | solution.py:554
  30.1 1.7 %collective-permute-start.15 = (f32[264,128]{1,0:T(8,128)S(1)}, f32[264,128]{1,0:T(8,128)S(1)}, u32[]{:S(2)}, u32[]{:S(2)}) collective-permute-start(f32[264,128]{1,0:T(8,128)S(1)} %get-tuple-element.23), channel_id=1, source_target_pairs={{0,1},{1,0},{2,3},{3,2},{4,5},{5,4},{6,7},{7,6},{12,13},{13,12},{1... | collective-permute-start | bytes 405512 | tf_op jit(solution)/shard_map/ppermute | solution.py:554
